TPU v7x, 256 devices: a whole 4x4x8 slice. The times are simulated.
256 devices in a mesh: flow: 32 (over y, x, core), span: 8 (over z).
Axes of the slice: x: 4, y: 4, z: 8, core: 2. Of those that a mesh axis runs over, the one named last changes fastest.
Arguments:
- solid_start: float32 [32, 2048, 1024], P(None, 'flow', 'span'), may hold values from -6 to 6
- heat_gen: float32 [32, 2048, 1024], P(None, 'flow', 'span'), may hold values from 0 to 0.05
- conductance: float32 [128, 65536], P('span', 'flow'), may hold values from 0 to 1, as said below
- heat_capacity: float32 [128], P('span'), may hold values from 0.2 to 1
- inlet_temp: float32 [128], P('span'), may hold values from -4 to 4
- wall_owner: int32 [65536, 1], P(('flow', 'span')), may hold values from 0 to 31; in each aligned block of 256 rows (0 to 255, 256 to 511, ...) at most 16 rows name the same one
- wall_row: int32 [65536, 1], P(('flow', 'span')), may hold values from 0 to 63
Outputs:
- solid_final: float32 [32, 2048, 1024], P(None, 'flow', 'span')
- coolant_final: float32 [128, 65536], P('span', 'flow')
Inputs may be any that keep to these rules, and one draw needn't show every extreme that they name: `conductance`: Positive. `wall_owner`: within the segments of one device (aligned blocks of 256 rows) no flow index is named more than 16 times, and some flow index is named exactly 16 times.
All inputs are finite; a program needn't handle non-finite values.
Results may differ from a plain program's by a relative error of at most 0.0003.
Values sent between devices are 32-bit elements; how exact they have to be, the bound alone decides.
No kernel may reach another device: no remote copies, remote signals or barrier semaphores. Data moves between devices by JAX's collectives and lax.ppermute only.
A program may use at most 128 MiB of HBM per device.

v0:
```python
import jax
import jax.numpy as jnp
from jax import lax
from jax.sharding import PartitionSpec as P

STEPS = 10


KAPPA = 0.16


def extended(cells, sides, width):
    for axis, dim in sides:
        count = lax.axis_size(axis)
        ends = count - 1
        head = lax.slice_in_dim(cells, 0, width, axis=dim)
        tail = lax.slice_in_dim(cells, cells.shape[dim] - width, cells.shape[dim], axis=dim)
        cells = jnp.concatenate(
            [
                lax.ppermute(tail, axis, [(i, (i + 1) % count) for i in range(ends)]),
                cells,
                lax.ppermute(head, axis, [((i + 1) % count, i) for i in range(ends)]),
            ],
            axis=dim,
        )
    return cells


def copy_for_each(x, axis):
    size = lax.axis_size(axis)
    return lax.all_to_all(jnp.broadcast_to(x[None], (size, *x.shape)), axis, 0, 0, tiled=True)


def gathered_once(x, axis):
    leaves = jax.tree.leaves(x)
    sequence = sorted(range(len(leaves)), key=lambda k: -leaves[k].size)
    width = (1, *leaves[sequence[0]].shape)[-1]
    lines = [
        jnp.pad(leaves[k].reshape(-1), (0, -leaves[k].size % width)).reshape(-1, width)
        for k in sequence
    ]
    both, at, found = (copy_for_each(jnp.concatenate(lines), axis), 0, {})
    for k, line in zip(sequence, lines):
        piece = both[:, at : at + len(line)].reshape(len(both), -1)
        found[k] = piece[:, : leaves[k].size].reshape(-1, *leaves[k].shape)
        at += len(line)
    numbers = iter(range(len(leaves)))
    return jax.tree.map(lambda _: found[next(numbers)], x)


def folded_in_pairs(pieces, combine):
    while len(jax.tree.leaves(pieces)[0]) > 1:
        pieces = jax.vmap(combine)(
            *(jax.tree.map(lambda part: part[side::2], pieces) for side in (0, 1))
        )
    return jax.tree.map(lambda part: part[0], pieces)


def prefix(x, axis, combine, identity):
    size, index = (lax.axis_size(axis), lax.axis_index(axis))
    passed = jnp.arange(size) < index

    def kept(part, zero, own):
        part = jnp.where(
            passed.reshape(-1, *(1 for _ in own.shape)), part, jnp.asarray(zero, own.dtype)
        )
        return part

    pieces = gathered_once(x, axis)
    return folded_in_pairs(jax.tree.map(kept, pieces, identity, x), combine)


def compose(earlier, later):
    return (earlier[0] * later[0], later[0] * earlier[1] + later[1])


def shift_matrix(width, offset):
    rows_iota = jnp.arange(width, dtype=jnp.int32)
    return (rows_iota[:, None] + offset == rows_iota[None, :]).astype(jnp.float32)


def move_cols(values, matrix):
    return jnp.dot(
        values, matrix, precision=lax.Precision.HIGHEST, preferred_element_type=jnp.float32
    )


def conduct(solid_field, heat_gen, band_matrix, first_col, last_col):
    padded = extended(solid_field, (("flow", 1),), 1)
    edges = jnp.stack([solid_field[:, :, 0], solid_field[:, :, -1]], axis=2)
    side = extended(edges, (("span", 2),), 1)
    layered = jnp.pad(solid_field, ((1, 1), (0, 0), (0, 0)))
    beside = padded[:, 2:, :] + padded[:, :-2, :]
    beside = beside + move_cols(solid_field, band_matrix)
    beside = beside + side[:, :, 0:1] * first_col + side[:, :, 3:4] * last_col
    beside = beside + layered[2:] + layered[:-2]
    return solid_field + KAPPA * (beside - 6.0 * solid_field) + heat_gen


def body(solid_start, heat_gen, conductance, heat_capacity, inlet_temp, wall_owner, wall_row):
    flow_size = lax.axis_size("flow")
    block_rows = solid_start.shape[1]
    seg_cells = solid_start.shape[2]
    channels, stations = conductance.shape
    seg_total = wall_owner.shape[0]
    seg_count = stations // seg_cells
    capacity = max(2, 2 * seg_total // flow_size)
    owners = wall_owner[:, 0]
    rows_local = wall_row[:, 0]
    decays = jnp.exp(-conductance).reshape(seg_total, seg_cells)
    owner_hits = (owners[:, None] == jnp.arange(flow_size, dtype=jnp.int32)[None, :]).astype(
        jnp.int32
    )
    slot_rank = jnp.sum(jnp.cumsum(owner_hits, axis=0) * owner_hits, axis=1) - 1
    slot_index = owners * capacity + slot_rank
    col_iota = jnp.arange(seg_cells, dtype=jnp.int32)
    band_matrix = shift_matrix(seg_cells, 1) + shift_matrix(seg_cells, -1)
    first_col = (col_iota == 0).astype(jnp.float32)
    last_col = (col_iota == seg_cells - 1).astype(jnp.float32)
    levels = seg_cells.bit_length() - 1
    level_mats = [shift_matrix(seg_cells, 1 << level) for level in range(levels)]
    level_fill = [(col_iota < 1 << level).astype(jnp.float32) for level in range(levels)]
    slot_rows = jnp.zeros((flow_size * capacity,), jnp.int32).at[slot_index].set(rows_local)
    owner_rows = lax.all_to_all(slot_rows, "flow", split_axis=0, concat_axis=0, tiled=True)
    row_select = (jnp.arange(block_rows, dtype=jnp.int32)[:, None] == owner_rows[None, :]).astype(
        jnp.float32
    )
    solid_field = solid_start
    coolant = jnp.zeros((channels, stations), jnp.float32)
    for turn in range(STEPS):
        bottom_layer = solid_field[0]
        asked = jnp.take(bottom_layer, owner_rows, axis=0)
        returned = lax.all_to_all(asked, "flow", split_axis=0, concat_axis=0, tiled=True)
        seg_temp = jnp.take(returned, slot_index, axis=0)
        gain_rows = decays
        shift_rows = (1.0 - decays) * seg_temp
        for level in range(levels):
            earlier_gain = move_cols(gain_rows, level_mats[level]) + level_fill[level]
            earlier_shift = move_cols(shift_rows, level_mats[level])
            shift_rows = gain_rows * earlier_shift + shift_rows
            gain_rows = earlier_gain * gain_rows
        seg_gain = gain_rows[:, -1].reshape(channels, seg_count)
        seg_shift = shift_rows[:, -1].reshape(channels, seg_count)
        run_gain, run_shift = lax.associative_scan(compose, (seg_gain, seg_shift), axis=1)
        device_map = (run_gain[:, -1], run_shift[:, -1])
        identity = (jnp.ones_like(inlet_temp), jnp.zeros_like(inlet_temp))
        upper_gain, upper_shift = prefix(device_map, "flow", compose, identity)
        carry_in = upper_gain * inlet_temp + upper_shift
        seg_out = run_gain * carry_in[:, None] + run_shift
        seg_enter = jnp.concatenate([carry_in[:, None], seg_out[:, :-1]], axis=1).reshape(
            seg_total, 1
        )
        coolant_rows = gain_rows * seg_enter + shift_rows
        upstream_rows = move_cols(coolant_rows, level_mats[0]) + seg_enter * first_col
        coolant = coolant_rows.reshape(channels, stations)
        heat_flow = (
            heat_capacity[:, None] * (coolant - upstream_rows.reshape(channels, stations))
        ).reshape(seg_total, seg_cells)
        flux_slots = (
            jnp.zeros((flow_size * capacity, seg_cells), jnp.float32).at[slot_index].set(heat_flow)
        )
        flux_in = lax.all_to_all(flux_slots, "flow", split_axis=0, concat_axis=0, tiled=True)
        wall_sink = jnp.dot(row_select, flux_in, precision=lax.Precision.HIGHEST)
        solid_field = conduct(solid_field, heat_gen, band_matrix, first_col, last_col)
        solid_field = solid_field.at[0].add(-wall_sink)
    return (solid_field, coolant)


def solution(mesh):
    placed = (
        P(None, "flow", "span"),
        P(None, "flow", "span"),
        P("span", "flow"),
        P("span"),
        P("span"),
        P(("flow", "span"), None),
        P(("flow", "span"), None),
    )
    return jax.shard_map(
        body,
        mesh=mesh,
        in_specs=placed,
        out_specs=(P(None, "flow", "span"), P("span", "flow")),
        check_vma=False,
    )
```

profile of v0, /device:TPU:97, one launch (start us, length us, event | category | flops | bytes accessed | tf_op | source)
XLA Modules:
  0.0 635.5 jit_solution(8928215360615425949)
XLA Ops:
  13.0 4.8 collective-permute-start.2
  21.0 8.1 %all-to-all-start = ((s32[32,16,1]{1,2,0:T(1,128)}), s32[32,16,1]{1,2,0:T(1,128)S(1)}, u32[]{:S(2)}, u32[]{:S(2)}) async-start(s32[32,16,1]{1,2,0:T(1,128)} %bitcast.10), calls=%async_computation | async-start | bytes 32768 | tf_op jit(solution)/shard_map/all_to_all | solution.py:124
  39.2 4.2 all-to-all-start.1
  43.7 8.7 %all-to-all-done.1 = f32[32,16,128]{2,1,0:T(8,128)S(1)} async-done(((f32[32,16,128]{2,1,0:T(8,128)}), f32[32,16,128]{2,1,0:T(8,128)S(1)}, u32[]{:S(2)}, u32[]{:S(2)}) %all-to-all-start.1) | async-done | bytes 262176 | tf_op jit(solution)/shard_map/all_to_all | solution.py:133
  62.2 7.2 %all-to-all-done.2 = f32[32,2,16]{2,1,0:T(2,128)S(1)} async-done(((f32[32,2,16]{2,1,0:T(2,128)}), f32[32,2,16]{2,1,0:T(2,128)S(1)}, u32[]{:S(2)}, u32[]{:S(2)}) %all-to-all-start.2) | async-done | bytes 4128 | tf_op jit(solution)/shard_map/all_to_all | solution.py:31
  72.8 3.9 all-to-all-start.3
  81.3 4.4 all-to-all-done.3
  87.9 4.2 all-to-all-start.4
  93.4 7.7 %all-to-all-done.4 = f32[32,16,128]{2,1,0:T(8,128)S(1)} async-done(((f32[32,16,128]{2,1,0:T(8,128)}), f32[32,16,128]{2,1,0:T(8,128)S(1)}, u32[]{:S(2)}, u32[]{:S(2)}) %all-to-all-start.4) | async-done | bytes 262176 | tf_op jit(solution)/shard_map/all_to_all | solution.py:133
  122.5 4.7 collective-permute-start.6
  130.1 8.1 %all-to-all-start.6 = ((f32[32,16,128]{2,1,0:T(8,128)}), f32[32,16,128]{2,1,0:T(8,128)S(1)}, u32[]{:S(2)}, u32[]{:S(2)}) async-start(f32[32,16,128]{2,1,0:T(8,128)} %bitcast.36), calls=%async_computation.6 | async-start | bytes 524288 | tf_op jit(solution)/shard_map/all_to_all | solution.py:162
  141.6 5.5 all-to-all-done.6
  154.4 7.7 %all-to-all-done.7 = f32[32,16,128]{2,1,0:T(8,128)S(1)} async-done(((f32[32,16,128]{2,1,0:T(8,128)}), f32[32,16,128]{2,1,0:T(8,128)S(1)}, u32[]{:S(2)}, u32[]{:S(2)}) %all-to-all-start.7) | async-done | bytes 262176 | tf_op jit(solution)/shard_map/all_to_all | solution.py:133
  183.4 4.9 collective-permute-start.10
  191.2 8.1 %all-to-all-start.9 = ((f32[32,16,128]{2,1,0:T(8,128)}), f32[32,16,128]{2,1,0:T(8,128)S(1)}, u32[]{:S(2)}, u32[]{:S(2)}) async-start(f32[32,16,128]{2,1,0:T(8,128)} %bitcast.50), calls=%async_computation.9 | async-start | bytes 524288 | tf_op jit(solution)/shard_map/all_to_all | solution.py:162
  202.8 5.5 all-to-all-done.9
  215.5 7.7 %all-to-all-done.10 = f32[32,16,128]{2,1,0:T(8,128)S(1)} async-done(((f32[32,16,128]{2,1,0:T(8,128)}), f32[32,16,128]{2,1,0:T(8,128)S(1)}, u32[]{:S(2)}, u32[]{:S(2)}) %all-to-all-start.10) | async-done | bytes 262176 | tf_op jit(solution)/shard_map/all_to_all | solution.py:133
  244.5 4.7 collective-permute-start.14
  252.2 8.1 %all-to-all-start.12 = ((f32[32,16,128]{2,1,0:T(8,128)}), f32[32,16,128]{2,1,0:T(8,128)S(1)}, u32[]{:S(2)}, u32[]{:S(2)}) async-start(f32[32,16,128]{2,1,0:T(8,128)} %bitcast.64), calls=%async_computation.12 | async-start | bytes 524288 | tf_op jit(solution)/shard_map/all_to_all | solution.py:162
  263.7 5.5 all-to-all-done.12
  271.4 4.1 all-to-all-start.13
  276.8 7.6 %all-to-all-done.13 = f32[32,16,128]{2,1,0:T(8,128)S(1)} async-done(((f32[32,16,128]{2,1,0:T(8,128)}), f32[32,16,128]{2,1,0:T(8,128)S(1)}, u32[]{:S(2)}, u32[]{:S(2)}) %all-to-all-start.13) | async-done | bytes 262176 | tf_op jit(solution)/shard_map/all_to_all | solution.py:133
  305.7 4.7 collective-permute-start.18
  313.3 8.1 %all-to-all-start.15 = ((f32[32,16,128]{2,1,0:T(8,128)}), f32[32,16,128]{2,1,0:T(8,128)S(1)}, u32[]{:S(2)}, u32[]{:S(2)}) async-start(f32[32,16,128]{2,1,0:T(8,128)} %bitcast.78), calls=%async_computation.15 | async-start | bytes 524288 | tf_op jit(solution)/shard_map/all_to_all | solution.py:162
  324.9 5.5 all-to-all-done.15
  337.6 7.7 %all-to-all-done.16 = f32[32,16,128]{2,1,0:T(8,128)S(1)} async-done(((f32[32,16,128]{2,1,0:T(8,128)}), f32[32,16,128]{2,1,0:T(8,128)S(1)}, u32[]{:S(2)}, u32[]{:S(2)}) %all-to-all-start.16) | async-done | bytes 262176 | tf_op jit(solution)/shard_map/all_to_all | solution.py:133
  366.7 5.1 collective-permute-start.22
  374.7 8.1 %all-to-all-start.18 = ((f32[32,16,128]{2,1,0:T(8,128)}), f32[32,16,128]{2,1,0:T(8,128)S(1)}, u32[]{:S(2)}, u32[]{:S(2)}) async-start(f32[32,16,128]{2,1,0:T(8,128)} %bitcast.92), calls=%async_computation.18 | async-start | bytes 524288 | tf_op jit(solution)/shard_map/all_to_all | solution.py:162
  386.2 5.5 all-to-all-done.18
  399.0 7.7 %all-to-all-done.19 = f32[32,16,128]{2,1,0:T(8,128)S(1)} async-done(((f32[32,16,128]{2,1,0:T(8,128)}), f32[32,16,128]{2,1,0:T(8,128)S(1)}, u32[]{:S(2)}, u32[]{:S(2)}) %all-to-all-start.19) | async-done | bytes 262176 | tf_op jit(solution)/shard_map/all_to_all | solution.py:133
  413.1 3.8 all-to-all-start.20
  428.0 4.7 collective-permute-start.26
  435.6 8.1 %all-to-all-start.21 = ((f32[32,16,128]{2,1,0:T(8,128)}), f32[32,16,128]{2,1,0:T(8,128)S(1)}, u32[]{:S(2)}, u32[]{:S(2)}) async-start(f32[32,16,128]{2,1,0:T(8,128)} %bitcast.106), calls=%async_computation.21 | async-start | bytes 524288 | tf_op jit(solution)/shard_map/all_to_all | solution.py:162
  447.2 5.5 all-to-all-done.21
  454.8 4.0 all-to-all-start.22
  460.2 7.6 %all-to-all-done.22 = f32[32,16,128]{2,1,0:T(8,128)S(1)} async-done(((f32[32,16,128]{2,1,0:T(8,128)}), f32[32,16,128]{2,1,0:T(8,128)S(1)}, u32[]{:S(2)}, u32[]{:S(2)}) %all-to-all-start.22) | async-done | bytes 262176 | tf_op jit(solution)/shard_map/all_to_all | solution.py:133
  489.1 4.7 collective-permute-start.30
  496.7 8.1 %all-to-all-start.24 = ((f32[32,16,128]{2,1,0:T(8,128)}), f32[32,16,128]{2,1,0:T(8,128)S(1)}, u32[]{:S(2)}, u32[]{:S(2)}) async-start(f32[32,16,128]{2,1,0:T(8,128)} %bitcast.120), calls=%async_computation.24 | async-start | bytes 524288 | tf_op jit(solution)/shard_map/all_to_all | solution.py:162
  508.3 5.5 all-to-all-done.24
  521.0 7.7 %all-to-all-done.25 = f32[32,16,128]{2,1,0:T(8,128)S(1)} async-done(((f32[32,16,128]{2,1,0:T(8,128)}), f32[32,16,128]{2,1,0:T(8,128)S(1)}, u32[]{:S(2)}, u32[]{:S(2)}) %all-to-all-start.25) | async-done | bytes 262176 | tf_op jit(solution)/shard_map/all_to_all | solution.py:133
  535.1 3.8 all-to-all-start.26
  550.1 4.9 collective-permute-start.34
  557.9 8.1 %all-to-all-start.27 = ((f32[32,16,128]{2,1,0:T(8,128)}), f32[32,16,128]{2,1,0:T(8,128)S(1)}, u32[]{:S(2)}, u32[]{:S(2)}) async-start(f32[32,16,128]{2,1,0:T(8,128)} %bitcast.134), calls=%async_computation.27 | async-start | bytes 524288 | tf_op jit(solution)/shard_map/all_to_all | solution.py:162
  569.5 5.5 all-to-all-done.27
  582.2 7.7 %all-to-all-done.28 = f32[32,16,128]{2,1,0:T(8,128)S(1)} async-done(((f32[32,16,128]{2,1,0:T(8,128)}), f32[32,16,128]{2,1,0:T(8,128)S(1)}, u32[]{:S(2)}, u32[]{:S(2)}) %all-to-all-start.28) | async-done | bytes 262176 | tf_op jit(solution)/shard_map/all_to_all | solution.py:133
  609.5 4.6 collective-permute-start.38
  617.0 8.1 %all-to-all-start.30 = ((f32[32,16,128]{2,1,0:T(8,128)}), f32[32,16,128]{2,1,0:T(8,128)S(1)}, u32[]{:S(2)}, u32[]{:S(2)}) async-start(f32[32,16,128]{2,1,0:T(8,128)} %bitcast.148), calls=%async_computation.30 | async-start | bytes 524288 | tf_op jit(solution)/shard_map/all_to_all | solution.py:162
  628.8 5.3 all-to-all-done.30
  (1087 shorter events, 335.1 us)
Async XLA Ops:
  2.2 74.6 %collective-permute-start.1 = (f32[32,1,128]{2,1,0:T(1,128)}, f32[32,1,128]{2,1,0:T(1,128)}, u32[]{:S(2)}, u32[]{:S(2)}) collective-permute-start(f32[32,1,128]{2,1,0:T(1,128)} %get-tuple-element.167), channel_id=1, source_target_pairs={{0,8},{8,16},{16,24},{24,32},{32,40},{40,48},{48,56},{56,64},{64,7... | collective-permute-start | bytes 49160 | tf_op jit(solution)/shard_map/ppermute | solution.py:20
  5.9 70.9 %collective-permute-start = (f32[32,1,128]{2,1,0:T(1,128)}, f32[32,1,128]{2,1,0:T(1,128)}, u32[]{:S(2)}, u32[]{:S(2)}) collective-permute-start(f32[32,1,128]{2,1,0:T(1,128)} %get-tuple-element.166), channel_id=1, source_target_pairs={{8,0},{16,8},{24,16},{32,24},{40,32},{48,40},{56,48},{64,56},{72,6... | collective-permute-start | bytes 49160 | tf_op jit(solution)/shard_map/ppermute | solution.py:22
  10.8 66.0 %collective-permute-start.3 = (f32[32,64,1]{1,0,2:T(8,128)}, f32[32,64,1]{1,0,2:T(8,128)S(1)}, u32[]{:S(2)}, u32[]{:S(2)}) collective-permute-start(f32[32,64,1]{1,0,2:T(8,128)} %copy.334), channel_id=1, source_target_pairs={{1,0},{2,1},{3,2},{4,3},{5,4},{6,5},{7,6},{9,8},{10,9},{11,10},{12... | collective-permute-start | bytes 24584 | tf_op jit(solution)/shard_map/ppermute | solution.py:22
  13.0 63.7 %collective-permute-start.2 = (f32[32,64,1]{1,0,2:T(8,128)S(1)}, f32[32,64,1]{1,0,2:T(8,128)S(1)}, u32[]{:S(2)}, u32[]{:S(2)}) collective-permute-start(f32[32,64,1]{1,0,2:T(8,128)S(1)} %copy.333), channel_id=1, source_target_pairs={{0,1},{1,2},{2,3},{3,4},{4,5},{5,6},{6,7},{8,9},{9,10},{10,11},{11... | collective-permute-start | bytes 24584 | tf_op jit(solution)/shard_map/ppermute | solution.py:20
  107.5 19.7 %all-to-all-start.5 = ((f32[32,2,16]{2,1,0:T(2,128)}), f32[32,2,16]{2,1,0:T(2,128)S(1)}, u32[]{:S(2)}, u32[]{:S(2)}) async-start(f32[32,2,16]{2,1,0:T(2,128)} %broadcast_in_dim.156), calls=%async_computation.5 | async-start | bytes 65536 | tf_op jit(solution)/shard_map/all_to_all | solution.py:31
  111.9 26.4 %collective-permute-start.5 = (f32[32,1,128]{2,1,0:T(1,128)}, f32[32,1,128]{2,1,0:T(1,128)}, u32[]{:S(2)}, u32[]{:S(2)}) collective-permute-start(f32[32,1,128]{2,1,0:T(1,128)} %get-tuple-element.163), channel_id=1, source_target_pairs={{0,8},{8,16},{16,24},{24,32},{32,40},{40,48},{48,56},{56,64},{64,7... | collective-permute-start | bytes 49160 | tf_op jit(solution)/shard_map/ppermute | solution.py:20
  115.5 22.8 %collective-permute-start.4 = (f32[32,1,128]{2,1,0:T(1,128)}, f32[32,1,128]{2,1,0:T(1,128)}, u32[]{:S(2)}, u32[]{:S(2)}) collective-permute-start(f32[32,1,128]{2,1,0:T(1,128)} %get-tuple-element.162), channel_id=1, source_target_pairs={{8,0},{16,8},{24,16},{32,24},{40,32},{48,40},{56,48},{64,56},{72,6... | collective-permute-start | bytes 49160 | tf_op jit(solution)/shard_map/ppermute | solution.py:22
  119.6 18.7 %collective-permute-start.7 = (f32[32,64,1]{1,0,2:T(8,128)}, f32[32,64,1]{1,0,2:T(8,128)}, u32[]{:S(2)}, u32[]{:S(2)}) collective-permute-start(f32[32,64,1]{1,0,2:T(8,128)} %copy.206), channel_id=1, source_target_pairs={{1,0},{2,1},{3,2},{4,3},{5,4},{6,5},{7,6},{9,8},{10,9},{11,10},{12... | collective-permute-start | bytes 24584 | tf_op jit(solution)/shard_map/ppermute | solution.py:22
  130.1 17.0 %all-to-all-start.6 = ((f32[32,16,128]{2,1,0:T(8,128)}), f32[32,16,128]{2,1,0:T(8,128)S(1)}, u32[]{:S(2)}, u32[]{:S(2)}) async-start(f32[32,16,128]{2,1,0:T(8,128)} %bitcast.36), calls=%async_computation.6 | async-start | bytes 524288 | tf_op jit(solution)/shard_map/all_to_all | solution.py:162
  168.5 19.8 %all-to-all-start.8 = ((f32[32,2,16]{2,1,0:T(2,128)}), f32[32,2,16]{2,1,0:T(2,128)S(1)}, u32[]{:S(2)}, u32[]{:S(2)}) async-start(f32[32,2,16]{2,1,0:T(2,128)} %broadcast_in_dim.158), calls=%async_computation.8 | async-start | bytes 65536 | tf_op jit(solution)/shard_map/all_to_all | solution.py:31
  172.9 26.5 %collective-permute-start.9 = (f32[32,1,128]{2,1,0:T(1,128)}, f32[32,1,128]{2,1,0:T(1,128)}, u32[]{:S(2)}, u32[]{:S(2)}) collective-permute-start(f32[32,1,128]{2,1,0:T(1,128)} %get-tuple-element.159), channel_id=1, source_target_pairs={{0,8},{8,16},{16,24},{24,32},{32,40},{40,48},{48,56},{56,64},{64,7... | collective-permute-start | bytes 49160 | tf_op jit(solution)/shard_map/ppermute | solution.py:20
  176.4 23.0 %collective-permute-start.8 = (f32[32,1,128]{2,1,0:T(1,128)}, f32[32,1,128]{2,1,0:T(1,128)}, u32[]{:S(2)}, u32[]{:S(2)}) collective-permute-start(f32[32,1,128]{2,1,0:T(1,128)} %get-tuple-element.158), channel_id=1, source_target_pairs={{8,0},{16,8},{24,16},{32,24},{40,32},{48,40},{56,48},{64,56},{72,6... | collective-permute-start | bytes 49160 | tf_op jit(solution)/shard_map/ppermute | solution.py:22
  180.5 18.8 %collective-permute-start.11 = (f32[32,64,1]{1,0,2:T(8,128)}, f32[32,64,1]{1,0,2:T(8,128)}, u32[]{:S(2)}, u32[]{:S(2)}) collective-permute-start(f32[32,64,1]{1,0,2:T(8,128)} %copy.219), channel_id=1, source_target_pairs={{1,0},{2,1},{3,2},{4,3},{5,4},{6,5},{7,6},{9,8},{10,9},{11,10},{12... | collective-permute-start | bytes 24584 | tf_op jit(solution)/shard_map/ppermute | solution.py:22
  191.2 17.0 %all-to-all-start.9 = ((f32[32,16,128]{2,1,0:T(8,128)}), f32[32,16,128]{2,1,0:T(8,128)S(1)}, u32[]{:S(2)}, u32[]{:S(2)}) async-start(f32[32,16,128]{2,1,0:T(8,128)} %bitcast.50), calls=%async_computation.9 | async-start | bytes 524288 | tf_op jit(solution)/shard_map/all_to_all | solution.py:162
  229.6 19.7 %all-to-all-start.11 = ((f32[32,2,16]{2,1,0:T(2,128)}), f32[32,2,16]{2,1,0:T(2,128)S(1)}, u32[]{:S(2)}, u32[]{:S(2)}) async-start(f32[32,2,16]{2,1,0:T(2,128)} %broadcast_in_dim.160), calls=%async_computation.11 | async-start | bytes 65536 | tf_op jit(solution)/shard_map/all_to_all | solution.py:31
  234.0 26.4 %collective-permute-start.13 = (f32[32,1,128]{2,1,0:T(1,128)}, f32[32,1,128]{2,1,0:T(1,128)}, u32[]{:S(2)}, u32[]{:S(2)}) collective-permute-start(f32[32,1,128]{2,1,0:T(1,128)} %get-tuple-element.155), channel_id=1, source_target_pairs={{0,8},{8,16},{16,24},{24,32},{32,40},{40,48},{48,56},{56,64},{64,7... | collective-permute-start | bytes 49160 | tf_op jit(solution)/shard_map/ppermute | solution.py:20
  237.5 22.8 %collective-permute-start.12 = (f32[32,1,128]{2,1,0:T(1,128)}, f32[32,1,128]{2,1,0:T(1,128)}, u32[]{:S(2)}, u32[]{:S(2)}) collective-permute-start(f32[32,1,128]{2,1,0:T(1,128)} %get-tuple-element.154), channel_id=1, source_target_pairs={{8,0},{16,8},{24,16},{32,24},{40,32},{48,40},{56,48},{64,56},{72,6... | collective-permute-start | bytes 49160 | tf_op jit(solution)/shard_map/ppermute | solution.py:22
  241.7 18.7 %collective-permute-start.15 = (f32[32,64,1]{1,0,2:T(8,128)}, f32[32,64,1]{1,0,2:T(8,128)}, u32[]{:S(2)}, u32[]{:S(2)}) collective-permute-start(f32[32,64,1]{1,0,2:T(8,128)} %copy.232), channel_id=1, source_target_pairs={{1,0},{2,1},{3,2},{4,3},{5,4},{6,5},{7,6},{9,8},{10,9},{11,10},{12... | collective-permute-start | bytes 24584 | tf_op jit(solution)/shard_map/ppermute | solution.py:22
  252.2 17.0 %all-to-all-start.12 = ((f32[32,16,128]{2,1,0:T(8,128)}), f32[32,16,128]{2,1,0:T(8,128)S(1)}, u32[]{:S(2)}, u32[]{:S(2)}) async-start(f32[32,16,128]{2,1,0:T(8,128)} %bitcast.64), calls=%async_computation.12 | async-start | bytes 524288 | tf_op jit(solution)/shard_map/all_to_all | solution.py:162
  290.7 19.7 %all-to-all-start.14 = ((f32[32,2,16]{2,1,0:T(2,128)}), f32[32,2,16]{2,1,0:T(2,128)S(1)}, u32[]{:S(2)}, u32[]{:S(2)}) async-start(f32[32,2,16]{2,1,0:T(2,128)} %broadcast_in_dim.162), calls=%async_computation.14 | async-start | bytes 65536 | tf_op jit(solution)/shard_map/all_to_all | solution.py:31
  295.1 26.4 %collective-permute-start.17 = (f32[32,1,128]{2,1,0:T(1,128)}, f32[32,1,128]{2,1,0:T(1,128)}, u32[]{:S(2)}, u32[]{:S(2)}) collective-permute-start(f32[32,1,128]{2,1,0:T(1,128)} %get-tuple-element.151), channel_id=1, source_target_pairs={{0,8},{8,16},{16,24},{24,32},{32,40},{40,48},{48,56},{56,64},{64,7... | collective-permute-start | bytes 49160 | tf_op jit(solution)/shard_map/ppermute | solution.py:20
  298.7 22.9 %collective-permute-start.16 = (f32[32,1,128]{2,1,0:T(1,128)}, f32[32,1,128]{2,1,0:T(1,128)}, u32[]{:S(2)}, u32[]{:S(2)}) collective-permute-start(f32[32,1,128]{2,1,0:T(1,128)} %get-tuple-element.150), channel_id=1, source_target_pairs={{8,0},{16,8},{24,16},{32,24},{40,32},{48,40},{56,48},{64,56},{72,6... | collective-permute-start | bytes 49160 | tf_op jit(solution)/shard_map/ppermute | solution.py:22
  302.8 18.7 %collective-permute-start.19 = (f32[32,64,1]{1,0,2:T(8,128)}, f32[32,64,1]{1,0,2:T(8,128)}, u32[]{:S(2)}, u32[]{:S(2)}) collective-permute-start(f32[32,64,1]{1,0,2:T(8,128)} %copy.245), channel_id=1, source_target_pairs={{1,0},{2,1},{3,2},{4,3},{5,4},{6,5},{7,6},{9,8},{10,9},{11,10},{12... | collective-permute-start | bytes 24584 | tf_op jit(solution)/shard_map/ppermute | solution.py:22
  313.3 17.1 %all-to-all-start.15 = ((f32[32,16,128]{2,1,0:T(8,128)}), f32[32,16,128]{2,1,0:T(8,128)S(1)}, u32[]{:S(2)}, u32[]{:S(2)}) async-start(f32[32,16,128]{2,1,0:T(8,128)} %bitcast.78), calls=%async_computation.15 | async-start | bytes 524288 | tf_op jit(solution)/shard_map/all_to_all | solution.py:162
  351.7 20.1 %all-to-all-start.17 = ((f32[32,2,16]{2,1,0:T(2,128)}), f32[32,2,16]{2,1,0:T(2,128)S(1)}, u32[]{:S(2)}, u32[]{:S(2)}) async-start(f32[32,2,16]{2,1,0:T(2,128)} %broadcast_in_dim.164), calls=%async_computation.17 | async-start | bytes 65536 | tf_op jit(solution)/shard_map/all_to_all | solution.py:31
  356.1 26.8 %collective-permute-start.21 = (f32[32,1,128]{2,1,0:T(1,128)}, f32[32,1,128]{2,1,0:T(1,128)}, u32[]{:S(2)}, u32[]{:S(2)}) collective-permute-start(f32[32,1,128]{2,1,0:T(1,128)} %get-tuple-element.147), channel_id=1, source_target_pairs={{0,8},{8,16},{16,24},{24,32},{32,40},{40,48},{48,56},{56,64},{64,7... | collective-permute-start | bytes 49160 | tf_op jit(solution)/shard_map/ppermute | solution.py:20
  359.6 23.2 %collective-permute-start.20 = (f32[32,1,128]{2,1,0:T(1,128)}, f32[32,1,128]{2,1,0:T(1,128)}, u32[]{:S(2)}, u32[]{:S(2)}) collective-permute-start(f32[32,1,128]{2,1,0:T(1,128)} %get-tuple-element.146), channel_id=1, source_target_pairs={{8,0},{16,8},{24,16},{32,24},{40,32},{48,40},{56,48},{64,56},{72,6... | collective-permute-start | bytes 49160 | tf_op jit(solution)/shard_map/ppermute | solution.py:22
  363.8 19.1 %collective-permute-start.23 = (f32[32,64,1]{1,0,2:T(8,128)}, f32[32,64,1]{1,0,2:T(8,128)}, u32[]{:S(2)}, u32[]{:S(2)}) collective-permute-start(f32[32,64,1]{1,0,2:T(8,128)} %copy.258), channel_id=1, source_target_pairs={{1,0},{2,1},{3,2},{4,3},{5,4},{6,5},{7,6},{9,8},{10,9},{11,10},{12... | collective-permute-start | bytes 24584 | tf_op jit(solution)/shard_map/ppermute | solution.py:22
  413.1 19.7 %all-to-all-start.20 = ((f32[32,2,16]{2,1,0:T(2,128)}), f32[32,2,16]{2,1,0:T(2,128)S(1)}, u32[]{:S(2)}, u32[]{:S(2)}) async-start(f32[32,2,16]{2,1,0:T(2,128)} %broadcast_in_dim.166), calls=%async_computation.20 | async-start | bytes 65536 | tf_op jit(solution)/shard_map/all_to_all | solution.py:31
  417.4 26.4 %collective-permute-start.25 = (f32[32,1,128]{2,1,0:T(1,128)}, f32[32,1,128]{2,1,0:T(1,128)}, u32[]{:S(2)}, u32[]{:S(2)}) collective-permute-start(f32[32,1,128]{2,1,0:T(1,128)} %get-tuple-element.143), channel_id=1, source_target_pairs={{0,8},{8,16},{16,24},{24,32},{32,40},{40,48},{48,56},{56,64},{64,7... | collective-permute-start | bytes 49160 | tf_op jit(solution)/shard_map/ppermute | solution.py:20
  421.0 22.8 %collective-permute-start.24 = (f32[32,1,128]{2,1,0:T(1,128)}, f32[32,1,128]{2,1,0:T(1,128)}, u32[]{:S(2)}, u32[]{:S(2)}) collective-permute-start(f32[32,1,128]{2,1,0:T(1,128)} %get-tuple-element.142), channel_id=1, source_target_pairs={{8,0},{16,8},{24,16},{32,24},{40,32},{48,40},{56,48},{64,56},{72,6... | collective-permute-start | bytes 49160 | tf_op jit(solution)/shard_map/ppermute | solution.py:22
  425.1 18.7 %collective-permute-start.27 = (f32[32,64,1]{1,0,2:T(8,128)}, f32[32,64,1]{1,0,2:T(8,128)}, u32[]{:S(2)}, u32[]{:S(2)}) collective-permute-start(f32[32,64,1]{1,0,2:T(8,128)} %copy.271), channel_id=1, source_target_pairs={{1,0},{2,1},{3,2},{4,3},{5,4},{6,5},{7,6},{9,8},{10,9},{11,10},{12... | collective-permute-start | bytes 24584 | tf_op jit(solution)/shard_map/ppermute | solution.py:22
  435.6 17.0 %all-to-all-start.21 = ((f32[32,16,128]{2,1,0:T(8,128)}), f32[32,16,128]{2,1,0:T(8,128)S(1)}, u32[]{:S(2)}, u32[]{:S(2)}) async-start(f32[32,16,128]{2,1,0:T(8,128)} %bitcast.106), calls=%async_computation.21 | async-start | bytes 524288 | tf_op jit(solution)/shard_map/all_to_all | solution.py:162
  474.2 19.7 %all-to-all-start.23 = ((f32[32,2,16]{2,1,0:T(2,128)}), f32[32,2,16]{2,1,0:T(2,128)S(1)}, u32[]{:S(2)}, u32[]{:S(2)}) async-start(f32[32,2,16]{2,1,0:T(2,128)} %broadcast_in_dim.168), calls=%async_computation.23 | async-start | bytes 65536 | tf_op jit(solution)/shard_map/all_to_all | solution.py:31
  478.5 26.4 %collective-permute-start.29 = (f32[32,1,128]{2,1,0:T(1,128)}, f32[32,1,128]{2,1,0:T(1,128)}, u32[]{:S(2)}, u32[]{:S(2)}) collective-permute-start(f32[32,1,128]{2,1,0:T(1,128)} %get-tuple-element.139), channel_id=1, source_target_pairs={{0,8},{8,16},{16,24},{24,32},{32,40},{40,48},{48,56},{56,64},{64,7... | collective-permute-start | bytes 49160 | tf_op jit(solution)/shard_map/ppermute | solution.py:20
  482.1 22.9 %collective-permute-start.28 = (f32[32,1,128]{2,1,0:T(1,128)}, f32[32,1,128]{2,1,0:T(1,128)}, u32[]{:S(2)}, u32[]{:S(2)}) collective-permute-start(f32[32,1,128]{2,1,0:T(1,128)} %get-tuple-element.138), channel_id=1, source_target_pairs={{8,0},{16,8},{24,16},{32,24},{40,32},{48,40},{56,48},{64,56},{72,6... | collective-permute-start | bytes 49160 | tf_op jit(solution)/shard_map/ppermute | solution.py:22
  486.2 18.7 %collective-permute-start.31 = (f32[32,64,1]{1,0,2:T(8,128)}, f32[32,64,1]{1,0,2:T(8,128)}, u32[]{:S(2)}, u32[]{:S(2)}) collective-permute-start(f32[32,64,1]{1,0,2:T(8,128)} %copy.284), channel_id=1, source_target_pairs={{1,0},{2,1},{3,2},{4,3},{5,4},{6,5},{7,6},{9,8},{10,9},{11,10},{12... | collective-permute-start | bytes 24584 | tf_op jit(solution)/shard_map/ppermute | solution.py:22
  496.7 17.1 %all-to-all-start.24 = ((f32[32,16,128]{2,1,0:T(8,128)}), f32[32,16,128]{2,1,0:T(8,128)S(1)}, u32[]{:S(2)}, u32[]{:S(2)}) async-start(f32[32,16,128]{2,1,0:T(8,128)} %bitcast.120), calls=%async_computation.24 | async-start | bytes 524288 | tf_op jit(solution)/shard_map/all_to_all | solution.py:162
  535.1 19.9 %all-to-all-start.26 = ((f32[32,2,16]{2,1,0:T(2,128)}), f32[32,2,16]{2,1,0:T(2,128)S(1)}, u32[]{:S(2)}, u32[]{:S(2)}) async-start(f32[32,2,16]{2,1,0:T(2,128)} %broadcast_in_dim.170), calls=%async_computation.26 | async-start | bytes 65536 | tf_op jit(solution)/shard_map/all_to_all | solution.py:31
  539.5 26.6 %collective-permute-start.33 = (f32[32,1,128]{2,1,0:T(1,128)}, f32[32,1,128]{2,1,0:T(1,128)}, u32[]{:S(2)}, u32[]{:S(2)}) collective-permute-start(f32[32,1,128]{2,1,0:T(1,128)} %get-tuple-element.135), channel_id=1, source_target_pairs={{0,8},{8,16},{16,24},{24,32},{32,40},{40,48},{48,56},{56,64},{64,7... | collective-permute-start | bytes 49160 | tf_op jit(solution)/shard_map/ppermute | solution.py:20
  543.1 23.1 %collective-permute-start.32 = (f32[32,1,128]{2,1,0:T(1,128)}, f32[32,1,128]{2,1,0:T(1,128)}, u32[]{:S(2)}, u32[]{:S(2)}) collective-permute-start(f32[32,1,128]{2,1,0:T(1,128)} %get-tuple-element.134), channel_id=1, source_target_pairs={{8,0},{16,8},{24,16},{32,24},{40,32},{48,40},{56,48},{64,56},{72,6... | collective-permute-start | bytes 49160 | tf_op jit(solution)/shard_map/ppermute | solution.py:22
  547.2 18.9 %collective-permute-start.35 = (f32[32,64,1]{1,0,2:T(8,128)}, f32[32,64,1]{1,0,2:T(8,128)}, u32[]{:S(2)}, u32[]{:S(2)}) collective-permute-start(f32[32,64,1]{1,0,2:T(8,128)} %copy.297), channel_id=1, source_target_pairs={{1,0},{2,1},{3,2},{4,3},{5,4},{6,5},{7,6},{9,8},{10,9},{11,10},{12... | collective-permute-start | bytes 24584 | tf_op jit(solution)/shard_map/ppermute | solution.py:22
  557.9 17.0 %all-to-all-start.27 = ((f32[32,16,128]{2,1,0:T(8,128)}), f32[32,16,128]{2,1,0:T(8,128)S(1)}, u32[]{:S(2)}, u32[]{:S(2)}) async-start(f32[32,16,128]{2,1,0:T(8,128)} %bitcast.134), calls=%async_computation.27 | async-start | bytes 524288 | tf_op jit(solution)/shard_map/all_to_all | solution.py:162
  596.3 17.8 %all-to-all-start.29 = ((f32[32,2,16]{2,1,0:T(2,128)}), f32[32,2,16]{2,1,0:T(2,128)S(1)}, u32[]{:S(2)}, u32[]{:S(2)}) async-start(f32[32,2,16]{2,1,0:T(2,128)} %broadcast_in_dim.172), calls=%async_computation.29 | async-start | bytes 65536 | tf_op jit(solution)/shard_map/all_to_all | solution.py:31
  600.1 25.1 %collective-permute-start.37 = (f32[32,1,128]{2,1,0:T(1,128)S(1)}, f32[32,1,128]{2,1,0:T(1,128)S(1)}, u32[]{:S(2)}, u32[]{:S(2)}) collective-permute-start(f32[32,1,128]{2,1,0:T(1,128)S(1)} %get-tuple-element.131), channel_id=1, source_target_pairs={{0,8},{8,16},{16,24},{24,32},{32,40},{40,48},{48,56},{56,64},{64,7... | collective-permute-start | bytes 49160 | tf_op jit(solution)/shard_map/ppermute | solution.py:20
  603.6 21.6 %collective-permute-start.36 = (f32[32,1,128]{2,1,0:T(1,128)S(1)}, f32[32,1,128]{2,1,0:T(1,128)S(1)}, u32[]{:S(2)}, u32[]{:S(2)}) collective-permute-start(f32[32,1,128]{2,1,0:T(1,128)S(1)} %get-tuple-element.130), channel_id=1, source_target_pairs={{8,0},{16,8},{24,16},{32,24},{40,32},{48,40},{56,48},{64,56},{72,6... | collective-permute-start | bytes 49160 | tf_op jit(solution)/shard_map/ppermute | solution.py:22
  607.2 18.0 %collective-permute-start.39 = (f32[32,64,1]{1,0,2:T(8,128)S(1)}, f32[32,64,1]{1,0,2:T(8,128)S(1)}, u32[]{:S(2)}, u32[]{:S(2)}) collective-permute-start(f32[32,64,1]{1,0,2:T(8,128)S(1)} %copy.310), channel_id=1, source_target_pairs={{1,0},{2,1},{3,2},{4,3},{5,4},{6,5},{7,6},{9,8},{10,9},{11,10},{12... | collective-permute-start | bytes 24584 | tf_op jit(solution)/shard_map/ppermute | solution.py:22
  617.0 17.0 %all-to-all-start.30 = ((f32[32,16,128]{2,1,0:T(8,128)}), f32[32,16,128]{2,1,0:T(8,128)S(1)}, u32[]{:S(2)}, u32[]{:S(2)}) async-start(f32[32,16,128]{2,1,0:T(8,128)} %bitcast.148), calls=%async_computation.30 | async-start | bytes 524288 | tf_op jit(solution)/shard_map/all_to_all | solution.py:162
  (50 other events, 568.2 us)
where the time goes:
time: 648 us; the launch traced here: 636 us
  starting transfers between devices  283 us (44%)
  waiting for transfers between devices  142 us (22%)
  local copies, waits for them, and re-layouts  132 us (20%)
  matrix products  58.9 us (9%)
  other arithmetic  14.2 us (2%)
    ppermute x20, starting transfers between devices, extended(): lax.ppermute(tail, axis, [(i, (i + 1) % count) for i in range(ends)])  83.1 us
    all_to_all x10, waiting for transfers between devices, body(): lax.all_to_all(asked, 'flow', split_axis=0, concat_axis=0, tiled=True)  77.6 us
    all_to_all x10, starting transfers between devices, body(): lax.all_to_all(flux_slots, 'flow', split_axis=0, concat_axis=0, tiled=True)  77.2 us
    dot_general x97, matrix products, move_cols(): jnp.dot(values, matrix, precision=lax.Precision.HIGHEST, preferred_elemen...  56.6 us
    all_to_all x10, waiting for transfers between devices, body(): lax.all_to_all(flux_slots, 'flow', split_axis=0, concat_axis=0, tiled=True)  53.8 us
    slice x28, local copies, waits for them, and re-layouts, conduct(): edges = jnp.stack([solid_field[:, :, 0], solid_field[:, :, -1]], axis=2)  41.2 us
    all_to_all x10, starting transfers between devices, body(): lax.all_to_all(asked, 'flow', split_axis=0, concat_axis=0, tiled=True)  39 us
    ppermute x20, starting transfers between devices, extended(): lax.ppermute(head, axis, [((i + 1) % count, i) for i in range(ends)])  38.3 us
  transfers between devices with their start and end apart: 71, of which 22 were waited for; matrix products, arithmetic and copies ran while one was open for 19% of the time, Pallas kernels for 0%

commit v1 on v0

v1 whole, which is shorter than its diff:
```python
import functools

import jax
import jax.numpy as jnp
from jax import lax
from jax.experimental import pallas as pl
from jax.experimental.pallas import tpu as pltpu
from jax.sharding import PartitionSpec as P

STEPS = 10
KAPPA = 0.16
F32 = jnp.float32
BF16 = jnp.bfloat16
I32 = jnp.int32
HI = lax.Precision.HIGHEST
LANES = 128
SLOTS = 16
TILE = 8
VMEM_LIMIT = 56 << 20


def iota(dims, dim):
    return lax.broadcasted_iota(I32, dims, dim)


def dot(a, b):
    return jnp.dot(a, b, precision=HI, preferred_element_type=F32)


def mul(a, b):
    return jnp.dot(a, b, preferred_element_type=F32)


def parts(x, count):
    found = []
    for _ in range(count):
        found.append(x.astype(BF16))
        x = x - found[-1].astype(F32)
    return found


def dot_t(a, b):
    return lax.dot_general(
        a, b, (((1,), (1,)), ((), ())), precision=HI, preferred_element_type=F32
    )


def pick(values, index):
    return jnp.take_along_axis(values, index, axis=1, mode="promise_in_bounds")


def spec(dims, dtype=F32):
    return jax.ShapeDtypeStruct(dims, dtype)


class Copies:
    def __init__(self, sems):
        self.sems, self.used = sems, 0

    def start(self, source, target):
        copy = pltpu.make_async_copy(source, target, self.sems.at[self.used])
        self.used += 1
        copy.start()
        return copy


def call(kernel, ins, outs, scratch, copies, flops=0, nbytes=0, aliases=None):
    return pl.pallas_call(
        kernel,
        out_shape=outs,
        in_specs=[pl.BlockSpec(memory_space=pl.ANY) for _ in ins],
        out_specs=[pl.BlockSpec(memory_space=pl.ANY) for _ in outs],
        scratch_shapes=[pltpu.VMEM(s.shape, s.dtype) for s in scratch]
        + [pltpu.SemaphoreType.DMA((copies,))],
        compiler_params=pltpu.CompilerParams(vmem_limit_bytes=VMEM_LIMIT),
        cost_estimate=pl.CostEstimate(flops=flops, bytes_accessed=nbytes, transcendentals=0),
        input_output_aliases=aliases or {},
    )(*ins)


def load_segments(copies, cond_hbm, cond):
    return [
        copies.start(cond_hbm.at[:, pl.ds(s * LANES, LANES)], cond.at[:, s, :])
        for s in range(cond.shape[1])
    ]


def source_kernel(
    owner_hbm, row_hbm, cond_hbm, pay_hbm, place_hbm, owner, row, cond, pay, place, sems
):
    copies = Copies(sems)
    first = [copies.start(owner_hbm, owner), copies.start(row_hbm, row)]
    later = load_segments(copies, cond_hbm, cond)
    for copy in first:
        copy.wait()
    segs = owner.shape[0] * LANES
    n_flow = pay.shape[0]
    slots = n_flow * SLOTS
    sub, lane = iota((segs, segs), 0), iota((segs, segs), 1)
    own_row = jnp.concatenate([owner[0:1, :], owner[1:2, :]], axis=1)
    wall_row = jnp.concatenate([row[0:1, :], row[1:2, :]], axis=1)

    def column(line):
        return jnp.sum(jnp.where(sub == lane, line, 0).astype(F32), axis=1, keepdims=True)

    own_col = column(own_row).astype(I32)
    same = own_col == own_row
    rank_row = jnp.sum((same & (sub < lane)).astype(F32), axis=0, keepdims=True).astype(I32)
    rank_col = jnp.sum((same & (lane < sub)).astype(F32), axis=1, keepdims=True).astype(I32)
    slot_row = own_row * SLOTS + rank_row
    slot_col = own_col * SLOTS + rank_col
    place[...] = (iota((segs, slots), 1) == slot_col).astype(F32).astype(BF16)
    out = copies.start(place, place_hbm)
    lanes = iota((segs, LANES), 1)
    value = jnp.where(lanes < SLOTS, column(wall_row).astype(I32), iota((segs, LANES), 0))
    value = jnp.where((lanes < 2 * SLOTS) & (lanes % SLOTS == rank_col), value, 0)
    held = (iota((n_flow, segs), 0) == own_row).astype(F32)
    meta = mul(held.astype(BF16), value.astype(F32).astype(BF16))
    for copy in later:
        copy.wait()
    cond_rows = cond[...].reshape(segs, LANES)
    chosen = (iota((slots, segs), 0) == slot_row).astype(F32).astype(BF16)
    moved = sum(mul(chosen, part) for part in parts(cond_rows, 3))
    total = dot_t(jnp.ones((TILE, LANES), F32), cond_rows)[0:1]
    sub8 = iota((TILE, LANES), 0)
    common = jnp.zeros((TILE, LANES), F32)
    slot_f = slot_row.astype(F32)
    for half in range(2):
        cols = slice(half * LANES, (half + 1) * LANES)
        common = jnp.where(sub8 == 1 + half, slot_f[:, cols], common)
        common = jnp.where(sub8 == 3 + half, total[:, cols], common)
    for p in range(n_flow):
        pay[p, 0:SLOTS, :] = moved[p * SLOTS : (p + 1) * SLOTS]
        pay[p, SLOTS : SLOTS + TILE, :] = jnp.where(sub8 == 0, meta[p : p + 1], common)
    back = copies.start(pay, pay_hbm)
    out.wait()
    back.wait()


def outer_kernel(solid_hbm, bottom_hbm, cols_hbm, head_hbm, tail_hbm, solid, cols, head, tail, sems):
    copies = Copies(sems)
    copies.start(solid_hbm, solid).wait()
    nz, nx, ny = solid.shape
    back = [copies.start(solid.at[0], bottom_hbm)]
    lane = iota((nx, ny), 1)
    ends = jnp.where(lane < nz, 0, ny - 1)
    unroll = 4

    def some(i, found):
        for j in range(unroll):
            z = i * unroll + j
            layer = solid[z]
            head[pl.ds(z, 1), :] = layer[0:1]
            tail[pl.ds(z, 1), :] = layer[nx - 1 : nx]
            found = jnp.where(lane % nz == z, pick(layer, ends), found)
        return found

    found = lax.fori_loop(0, nz // unroll, some, jnp.zeros((nx, ny), F32))
    cols[...] = found
    head[0:1, :] = jnp.zeros((1, ny), F32)
    tail[0:1, :] = jnp.zeros((1, ny), F32)
    for source, target in ((cols, cols_hbm), (head, head_hbm), (tail, tail_hbm)):
        back.append(copies.start(source, target))
    for copy in back:
        copy.wait()


def owner_kernel(
    got_hbm, bottom_hbm, const_hbm,
    hit_hbm, hit_t_hbm, reply_hbm, weight_hbm, swell_hbm,
    index_hbm, scan_hbm, msg_hbm,
    got, bottom, const, hit, hit_t, reply, weight, swell, index, scan, msg, sems,
):
    copies = Copies(sems)
    for copy in [
        copies.start(got_hbm, got), copies.start(bottom_hbm, bottom), copies.start(const_hbm, const)
    ]:
        copy.wait()
    n_flow = got.shape[0]
    slots = n_flow * SLOTS
    block_rows = bottom.shape[0]
    meta = got[:, SLOTS, :]
    lane8, sub8 = iota((TILE, LANES), 1), iota((TILE, LANES), 0)
    mine = lane8 // SLOTS == sub8
    hits, caps = [], []
    n_grp = n_flow // TILE
    rows = iota((LANES, LANES), 0)
    cap8 = jnp.broadcast_to(const[0:1, :], (TILE, LANES))
    for g in range(n_grp):
        part = meta[g * TILE : (g + 1) * TILE]
        row = jnp.sum(jnp.where(mine, pick(part, lane8 % SLOTS), 0.0), axis=0, keepdims=True)
        seg = jnp.where(mine, pick(part, SLOTS + lane8 % SLOTS), 0.0)
        seg = jnp.sum(seg, axis=0, keepdims=True).astype(I32)
        seg8 = jnp.broadcast_to(seg, (TILE, LANES))
        index[4, g * TILE : (g + 1) * TILE, :] = seg8
        cap = pick(cap8, seg8 // 16)[0:1]
        hits.append((rows == row.astype(I32)).astype(F32))
        caps.append(jnp.transpose(jnp.broadcast_to(cap, (LANES, LANES))))
    all_hit = jnp.concatenate(hits, axis=1)
    own_hit = all_hit[0:block_rows]
    hit[...] = own_hit.astype(BF16)
    cond = got[:, 0:SLOTS, :].reshape(slots, LANES)
    sub_t, lane_t = iota((LANES, LANES), 0), iota((LANES, LANES), 1)
    after = sum(
        mul(part, (sub_t > lane_t).astype(F32).astype(BF16)) for part in parts(cond, 3)
    )
    decay = jnp.exp(-cond)
    own_rate = 1.0 - decay
    halves = parts(jnp.transpose(own_rate * jnp.exp(-after)), 2)
    for half in range(2):
        weight[half] = halves[half]
    write_message(bottom[...], weight, own_hit, msg)
    back = [copies.start(msg, msg_hbm), copies.start(weight, weight_hbm)]
    back.append(copies.start(hit, hit_hbm))
    hit_t[...] = jnp.transpose(all_hit).astype(BF16)
    back.append(copies.start(hit_t, hit_t_hbm))
    own_caprate = own_rate * jnp.concatenate(caps, axis=0)
    ahead = sum(
        mul(part, (sub_t < lane_t).astype(F32).astype(BF16)) for part in parts(cond, 3)
    )
    halves = parts(own_caprate * jnp.exp(-ahead), 2)
    for half in range(2):
        reply[half] = halves[half]
    back.append(copies.start(reply, reply_hbm))
    middle = jnp.sum(
        jnp.where(iota((slots, LANES), 1) < LANES // 2, cond, 0.0), axis=1, keepdims=True
    )
    swell[0] = own_rate * jnp.exp(ahead + cond - middle)
    swell[1] = jnp.exp(middle - ahead)
    swell[2] = own_caprate
    back.append(copies.start(swell, swell_hbm))
    lane_f, sub_f = iota((n_flow, LANES), 1), iota((n_flow, LANES), 0)
    inlet = jnp.broadcast_to(const[1:2, :], (n_flow, LANES))
    for half in range(2):
        slot = got[:, SLOTS + 1 + half, :].astype(I32)
        index[half] = (sub_f % TILE) * SLOTS + slot % SLOTS
        index[2 + half] = slot // SLOTS
        gain = jnp.exp(-got[:, SLOTS + 3 + half, :])
        inner = lane_f % 16
        for step in range(4):
            width = 1 << step
            scan[step, half] = jnp.where(inner >= width, gain, 0.0)
            gain = gain * jnp.where(inner >= width, pltpu.roll(gain, width, 1), 1.0)
        scan[10, half] = jnp.where(inner == 0, 1.0, pltpu.roll(gain, 1, 1))
        scan[9, half] = gain
        for step in range(5):
            width = 1 << step
            scan[4 + step, half] = jnp.where(sub_f >= width, gain, 0.0)
            gain = gain * jnp.where(sub_f >= width, pltpu.roll(gain, width, 0), 1.0)
        scan[11, half] = pick(inlet, lane_f // 16 + 8 * half)
    back += [copies.start(index, index_hbm), copies.start(scan, scan_hbm)]
    for copy in back:
        copy.wait()


def write_message(bottom, weight, hit, msg):
    high, low = parts(bottom, 2)
    ends = mul(high, weight[0]) + (mul(high, weight[1]) + mul(low, weight[0]))
    ends = jnp.sum(ends * hit, axis=0, keepdims=True)
    sub8 = iota((TILE, LANES), 0)
    tile = jnp.where(sub8 == 4, bottom[0:1], bottom[bottom.shape[0] - 1 :])
    for g in range(ends.shape[1] // LANES):
        tile = jnp.where(sub8 == g, ends[:, g * LANES : (g + 1) * LANES], tile)
    for p in range(msg.shape[0]):
        msg[p, 0:TILE, :] = tile


def march_kernel(
    bottom_hbm, hit_hbm, hit_t_hbm, swell_hbm, sink_hbm,
    bottom, hit, hit_t, swell, sink, flux, sems,
):
    copies = Copies(sems)
    first = [copies.start(bottom_hbm, bottom), copies.start(hit_t_hbm, hit_t)]
    slots = hit_t.shape[0]
    piece = slots // 4
    then = []
    for i in range(4):
        rows = pl.ds(i * piece, piece)
        then.append(copies.start(swell_hbm.at[:, rows, :], swell.at[:, rows, :]))
    last = copies.start(hit_hbm, hit)
    for copy in first:
        copy.wait()
    nx, ny = bottom.shape
    padded = jnp.concatenate([bottom[...], jnp.zeros((LANES - nx, ny), F32)], axis=0)
    wide = jnp.concatenate(parts(padded, 3), axis=1)
    earlier = (iota((LANES, LANES), 0) < iota((LANES, LANES), 1)).astype(F32).astype(BF16)
    for i in range(4):
        then[i].wait()
        rows = pl.ds(i * piece, piece)
        triple = mul(hit_t[rows, :], wide)
        temp = (triple[:, 0:ny] + triple[:, ny : 2 * ny]) + triple[:, 2 * ny :]
        high, low = parts(swell[0, rows, :] * temp, 2)
        before = swell[1, rows, :] * (mul(high, earlier) + mul(low, earlier))
        high, low = parts(swell[2, rows, :] * (temp - before), 2)
        flux[0, rows, :] = high
        flux[1, rows, :] = low
    last.wait()
    sink[...] = mul(hit[...], flux[0]) + mul(hit[...], flux[1])
    copies.start(sink, sink_hbm).wait()


def conduct_kernel(
    solid_hbm, bottom_hbm, heat_hbm, west_hbm, east_hbm, north_hbm, south_hbm, sink_hbm,
    out_hbm, base_hbm, cols_hbm, head_hbm, tail_hbm,
    solid, heat, west, east, sink, out, base, cols, head, tail, sems,
):
    nz, nx, ny = out.shape
    copies = Copies(sems)
    inner = pl.ds(8, nx)
    early = [
        copies.start(bottom_hbm, solid.at[1, inner, :]),
        copies.start(north_hbm, solid.at[pl.ds(1, nz), 7, :]),
        copies.start(south_hbm, solid.at[pl.ds(1, nz), 8 + nx, :]),
        copies.start(west_hbm, west),
        copies.start(east_hbm, east),
        copies.start(sink_hbm, sink),
    ]
    pieces = 4
    chunk = nz // pieces
    solids, heats = [], []
    for p in range(pieces):
        count = chunk if p < pieces - 1 else chunk - 1
        source = solid_hbm.at[pl.ds(p * chunk + 1, count)]
        solids.append(copies.start(source, solid.at[pl.ds(p * chunk + 2, count), inner, :]))
        piece = pl.ds(p * chunk, chunk)
        heats.append(copies.start(heat_hbm.at[piece], heat.at[piece]))
    me, lot = lax.axis_index("flow"), lax.axis_index("span")
    n_flow, n_span = lax.axis_size("flow"), lax.axis_size("span")
    lane = iota((nx, ny), 1)
    border = (lane == 0) | (lane == ny - 1)
    ends = jnp.where(lane < nz, 0, ny - 1)
    solid[0, inner, :] = jnp.zeros((nx, ny), F32)
    solid[nz + 1, inner, :] = jnp.zeros((nx, ny), F32)
    for copy in early:
        copy.wait()

    @pl.when(me == 0)
    def _():
        solid[pl.ds(1, nz), 7, :] = jnp.zeros((nz, ny), F32)

    @pl.when(me == n_flow - 1)
    def _():
        solid[pl.ds(1, nz), 8 + nx, :] = jnp.zeros((nz, ny), F32)

    halo = jnp.where((lane < nz) & (lot < n_span - 1), east[...], 0.0)
    halo = jnp.where((lane >= nz) & (lot > 0), west[...], halo)
    unroll = 4

    def some(start, i, found):
        for j in range(unroll):
            z = start + i * unroll + j
            mid = solid[z + 1, inner, :]
            side = pick(halo, jnp.where(lane == 0, nz, 0) + z)
            right, left = pltpu.roll(mid, 1, 1), pltpu.roll(mid, ny - 1, 1)
            across = jnp.where(border, side + jnp.where(lane == 0, left, right), left + right)
            total = across + (solid[z + 1, pl.ds(7, nx), :] + solid[z + 1, pl.ds(9, nx), :])
            total = total + (solid[z, inner, :] + solid[z + 2, inner, :])
            new = mid + KAPPA * (total - 6.0 * mid) + heat[z]
            out[z] = new
            head[pl.ds(z, 1), :] = new[0:1]
            tail[pl.ds(z, 1), :] = new[nx - 1 : nx]
            found = jnp.where(lane % nz == z, pick(new, ends), found)
        return found

    found = jnp.zeros((nx, ny), F32)
    back = []
    for p in range(pieces):
        solids[p].wait()
        heats[p].wait()
        found = lax.fori_loop(0, chunk // unroll, functools.partial(some, p * chunk), found)
        piece = pl.ds(p * chunk, chunk)
        back.append(copies.start(out.at[piece], out_hbm.at[piece]))
    cols[...] = found
    head[0:1, :] = jnp.zeros((1, ny), F32)
    tail[0:1, :] = jnp.zeros((1, ny), F32)
    base[...] = out[0] - sink[...]
    for source, target in (
        (cols, cols_hbm), (head, head_hbm), (tail, tail_hbm), (base, base_hbm)
    ):
        back.append(copies.start(source, target))
    for copy in back:
        copy.wait()


def entering(got, index, scan):
    n_flow = got.shape[0]
    ends = [[], []]
    for g in range(n_flow // TILE):
        rows = slice(g * TILE, (g + 1) * TILE)
        lanes = [index[half, rows, :] for half in range(2)]
        origin = [index[2 + half, rows, :] for half in range(2)]
        acc = [jnp.zeros((TILE, LANES), F32) for _ in range(2)]
        for o in range(n_flow):
            line = jnp.broadcast_to(got[o, g : g + 1, :], (TILE, LANES))
            for half in range(2):
                acc[half] = jnp.where(origin[half] == o, pick(line, lanes[half]), acc[half])
        for half in range(2):
            ends[half].append(acc[half])
    result = []
    sub, lane = iota((n_flow, LANES), 0), iota((n_flow, LANES), 1)
    for half in range(2):
        x = jnp.concatenate(ends[half], axis=0)
        for step in range(4):
            x = x + scan[step, half] * pltpu.roll(x, 1 << step, 1)
        inlet = scan[11, half]
        y = jnp.where(sub == 0, x + scan[9, half] * inlet, x)
        for step in range(5):
            y = y + scan[4 + step, half] * pltpu.roll(y, 1 << step, 0)
        carry = jnp.where(sub == 0, inlet, pltpu.roll(y, 1, 0))
        carry = pick(carry, lane // 16 * 16 + 15)
        earlier = jnp.where(lane % 16 == 0, 0.0, pltpu.roll(x, 1, 1))
        result.append(earlier + scan[10, half] * carry)
    return result


def hosted(enter, index):
    lane8, sub8 = iota((TILE, LANES), 1), iota((TILE, LANES), 0)
    found = []
    for g in range(enter[0].shape[0] // TILE):
        rows = slice(g * TILE, (g + 1) * TILE)
        seg = index[4, rows, :]
        low, high = (pick(enter[half][rows], seg % LANES) for half in range(2))
        value = jnp.where(lane8 // SLOTS == sub8, jnp.where(seg < LANES, low, high), 0.0)
        found.append(jnp.sum(value, axis=0, keepdims=True))
    return jnp.concatenate(found, axis=1)


def new_bottom(got, carry, base, hit, reply):
    me, n_flow = lax.axis_index("flow"), got.shape[0]
    nx, ny = base.shape
    high, low = parts(carry, 2)
    high, low = hit * high, hit * low
    bottom = base[...] + (mul(high, reply[0]) + (mul(high, reply[1]) + mul(low, reply[0])))
    north = got[jnp.maximum(me - 1, 0), 5:6, :]
    south = got[jnp.minimum(me + 1, n_flow - 1), 4:5, :]
    sub = iota((nx, ny), 0)
    halo = jnp.where((sub == 0) & (me > 0), north, 0.0)
    halo = halo + jnp.where((sub == nx - 1) & (me < n_flow - 1), south, 0.0)
    return bottom + KAPPA * halo


def after_kernel(
    last,
    got_hbm, base_hbm, plain_hbm, index_hbm, scan_hbm, hit_hbm, reply_hbm, weight_hbm,
    hit_t_hbm, bottom_hbm, msg_hbm, cols_hbm,
    got, base, plain, index, scan, hit, reply, weight, hit_t, bottom, msg, cols, sems,
):
    copies = Copies(sems)
    first = [copies.start(got_hbm, got), copies.start(index_hbm, index), copies.start(scan_hbm, scan)]
    then = [
        copies.start(hit_hbm, hit), copies.start(reply_hbm, reply), copies.start(base_hbm, base),
        copies.start(plain_hbm, plain), copies.start(weight_hbm, weight),
    ]
    if last:
        then.append(copies.start(hit_t_hbm, hit_t))
    for copy in first:
        copy.wait()
    carry = hosted(entering(got, index, scan), index)
    for copy in then:
        copy.wait()
    own_hit = hit[...]
    new = new_bottom(got, carry, base, own_hit, reply)
    bottom[...] = new
    back = [copies.start(bottom, bottom_hbm)]
    nx, ny = new.shape
    nz = LANES // 4
    lane = iota((nx, ny), 1)
    cols[...] = jnp.where(
        lane % nz == 0, pick(new, jnp.where(lane < nz, 0, ny - 1)), plain[...]
    )
    back.append(copies.start(cols, cols_hbm))
    if last:
        padded = jnp.concatenate([new, jnp.zeros((LANES - nx, ny), F32)], axis=0)
        temp = sum(mul(hit_t[...], part) for part in parts(padded, 3))
        for p in range(msg.shape[0]):
            msg[p, TILE : TILE + SLOTS, :] = temp[p * SLOTS : (p + 1) * SLOTS]
    write_message(new, weight, own_hit.astype(F32), msg)
    back.append(copies.start(msg, msg_hbm))
    for copy in back:
        copy.wait()


def final_kernel(
    got_hbm, base_hbm, index_hbm, scan_hbm, hit_hbm, reply_hbm,
    place_hbm, cond_hbm, solid_hbm, out_hbm, coolant_hbm,
    got, base, index, scan, hit, reply, place, cond, bottom, coolant, sems,
):
    del solid_hbm
    copies = Copies(sems)
    first = [copies.start(got_hbm, got), copies.start(index_hbm, index), copies.start(scan_hbm, scan)]
    then = [
        copies.start(hit_hbm, hit), copies.start(reply_hbm, reply), copies.start(base_hbm, base),
        copies.start(place_hbm, place),
    ]
    then += load_segments(copies, cond_hbm, cond)
    for copy in first:
        copy.wait()
    enter = entering(got, index, scan)
    carry = hosted(enter, index)
    for copy in then:
        copy.wait()
    bottom[...] = new_bottom(got, carry, base, hit[...], reply)
    back = [copies.start(bottom, out_hbm.at[0])]
    n_flow = got.shape[0]
    temps = got[:, TILE : TILE + SLOTS, :].reshape(n_flow * SLOTS, LANES)
    temp = sum(mul(place[...], part) for part in parts(temps, 3))
    segs = temp.shape[0]
    lane = iota((segs, LANES), 1)
    gain = jnp.exp(-cond[...].reshape(segs, LANES))
    shift = (1.0 - gain) * temp
    for step in range(7):
        width = 1 << step
        shift = shift + jnp.where(lane >= width, gain * pltpu.roll(shift, width, 1), 0.0)
        gain = gain * jnp.where(lane >= width, pltpu.roll(gain, width, 1), 1.0)
    own = iota((n_flow, LANES), 0) == lax.axis_index("flow")
    line = jnp.concatenate(
        [jnp.sum(jnp.where(own, part, 0.0), axis=0, keepdims=True) for part in enter], axis=1
    )
    same = iota((segs, segs), 0) == iota((segs, segs), 1)
    start = jnp.sum(jnp.where(same, line, 0.0), axis=1, keepdims=True)
    coolant[...] = (shift + gain * start).reshape(coolant.shape)
    for s in range(coolant.shape[1]):
        target = coolant_hbm.at[:, pl.ds(s * LANES, LANES)]
        back.append(copies.start(coolant.at[:, s, :], target))
    for copy in back:
        copy.wait()


def body(solid_start, heat_gen, conductance, heat_capacity, inlet_temp, wall_owner, wall_row):
    n_flow, n_span = lax.axis_size("flow"), lax.axis_size("span")
    nz, nx, ny = solid_start.shape
    channels, stations = conductance.shape
    segs = wall_owner.shape[0]
    slots = n_flow * SLOTS
    const = jnp.pad(
        jnp.stack([heat_capacity, inlet_temp]), ((0, TILE - 2), (0, LANES - channels))
    )

    def both_ways(ahead, back, axis, size):
        up = [(i, (i + 1) % size) for i in range(size)]
        down = [(i, (i - 1) % size) for i in range(size)]
        return lax.ppermute(ahead, axis, up), lax.ppermute(back, axis, down)

    def exchange(message):
        return lax.all_to_all(message, "flow", 0, 0, tiled=True)

    lines = spec((segs // LANES, LANES), I32)
    split = spec((channels, segs // channels, LANES))
    layer, edge = spec((nx, ny)), spec((nz, ny))
    block = spec((nz, nx, ny))
    pay_spec, place_spec = spec((n_flow, SLOTS + TILE, LANES)), spec((segs, slots), BF16)
    pay, place = call(
        source_kernel,
        (wall_owner.reshape(lines.shape), wall_row.reshape(lines.shape), conductance),
        (pay_spec, place_spec),
        (lines, lines, split, pay_spec, place_spec),
        20,
    )
    got = exchange(pay)
    bottom, cols, head, tail = call(
        outer_kernel, (solid_start,), (layer, layer, edge, edge), (block, layer, edge, edge), 5
    )
    hit_spec, hit_t_spec = spec((nx, slots), BF16), spec((slots, LANES), BF16)
    reply_spec, weight_spec = spec((2, slots, LANES), BF16), spec((2, LANES, slots), BF16)
    swell_spec = spec((3, slots, LANES))
    index_spec, scan_spec = spec((5, n_flow, LANES), I32), spec((12, 2, n_flow, LANES))
    msg_spec, long_spec = spec((n_flow, TILE, LANES)), spec((n_flow, TILE + SLOTS, LANES))
    constants = (
        hit_spec, hit_t_spec, reply_spec, weight_spec, swell_spec, index_spec, scan_spec, msg_spec,
    )
    hit, hit_t, reply, weight, swell, index, scan, message = call(
        owner_kernel,
        (got, bottom, const),
        constants,
        (pay_spec, layer, spec((TILE, LANES)), *constants),
        11,
    )

    def beside(solid, bottom, cols, north, south, message):
        got = exchange(message)
        west, east = both_ways(cols, cols, "span", n_span)
        (sink,) = call(
            march_kernel,
            (bottom, hit, hit_t, swell),
            (layer,),
            (layer, hit_spec, hit_t_spec, swell_spec, layer, reply_spec),
            8,
            flops=2_000_000,
            nbytes=3_000_000,
        )
        solid, base, cols, head, tail = call(
            conduct_kernel,
            (solid, bottom, heat_gen, west, east, north, south, sink),
            (block, layer, layer, edge, edge),
            (
                spec((nz + 2, nx + 16, ny)), block, layer, layer, layer,
                block, layer, layer, edge, edge,
            ),
            22,
            flops=4_000_000,
            nbytes=6_000_000,
            aliases={0: 0},
        )
        return got, solid, base, cols, head, tail

    def step(state, last=False):
        got, solid, base, cols, head, tail = beside(*state)
        north, south = both_ways(tail, head, "flow", n_flow)
        sent = long_spec if last else msg_spec
        bottom, message, cols = call(
            functools.partial(after_kernel, last),
            (got, base, cols, index, scan, hit, reply, weight, hit_t),
            (layer, sent, layer),
            (
                msg_spec, layer, layer, index_spec, scan_spec, hit_spec, reply_spec, weight_spec,
                hit_t_spec, layer, sent, layer,
            ),
            13,
            flops=4_000_000,
            nbytes=4_000_000,
        )
        return solid, bottom, cols, north, south, message

    north, south = both_ways(tail, head, "flow", n_flow)
    state = (solid_start, bottom, cols, north, south, message)
    state = lax.fori_loop(0, STEPS - 2, lambda turn, now: step(now), state)
    state = step(state, last=True)
    got, solid, base, _, _, _ = beside(*state)
    return call(
        final_kernel,
        (got, base, index, scan, hit, reply, place, conductance, solid),
        (block, spec((channels, stations))),
        (
            long_spec, layer, index_spec, scan_spec, hit_spec, reply_spec, place_spec, split,
            layer, split,
        ),
        8 + 2 * split.shape[1],
        aliases={8: 0},
    )


def solution(mesh):
    placed = (
        P(None, "flow", "span"),
        P(None, "flow", "span"),
        P("span", "flow"),
        P("span"),
        P("span"),
        P(("flow", "span"), None),
        P(("flow", "span"), None),
    )
    return jax.shard_map(
        body,
        mesh=mesh,
        in_specs=placed,
        out_specs=(P(None, "flow", "span"), P("span", "flow")),
        check_vma=False,
    )
```

time: 648 us -> 279 us (0.43); the launches traced: 636 us -> 274 us
  starting transfers between devices: 283 us -> 130 us
  waiting for transfers between devices: 142 us -> 13.2 us
  local copies, waits for them, and re-layouts: 132 us -> 15.5 us
  Pallas kernels: 0 us -> 114 us
  matrix products: 58.9 us -> 0 us
  other arithmetic: 14.2 us -> 0.6 us
    all_to_all x31 -> x11, waiting for transfers between devices: 142 us -> 5.7 us  [exchange(): return lax.all_to_all(message, 'flow', 0, 0, tiled=True)]
    pallas_call x0 -> x33, Pallas kernels: none -> 114 us  [call(): pl.pallas_call(kernel, out_shape=outs, in_specs=[pl.BlockSpec(memory_spac...]
    all_to_all x31 -> x11, starting transfers between devices: 162 us -> 85 us  [exchange(): return lax.all_to_all(message, 'flow', 0, 0, tiled=True)]
    ppermute x40, starting transfers between devices: 121 us -> 44.7 us  [both_ways(): return (lax.ppermute(ahead, axis, up), lax.ppermute(back, axis, down))]
    dot_general x107 -> x0, matrix products: 58.9 us -> none  [the longest x97 56.6 us: move_cols(): jnp.dot(values, matrix, precision=lax.Precision.HIGHEST, preferred_elemen...]
    slice x328 -> x0, local copies, waits for them, and re-layouts: 56.5 us -> none  [the longest x28 41.2 us: conduct(): edges = jnp.stack([solid_field[:, :, 0], solid_field[:, :, -1]], axis=2)]
    gather x30 -> x0, local copies, waits for them, and re-layouts: 32.3 us -> none  [the longest x20 21.9 us: body(): seg_temp = jnp.take(returned, slot_index, axis=0)]
    scatter x11 -> x0, local copies, waits for them, and re-layouts: 19.8 us -> none  [the longest x10 18.2 us: body(): jnp.zeros((flow_size * capacity, seg_cells), jnp.float32).at[slot_index]]
  transfers between devices with their start and end apart: 71 -> 51, of which waited for: 22 -> 11; matrix products, arithmetic and copies ran while one was open for 19% -> 0% of each run, Pallas kernels for 0% -> 38%
where the time goes in v1:
time: 279 us; the launch traced here: 274 us
  starting transfers between devices  130 us (47%)
  Pallas kernels  114 us (41%)
  local copies, waits for them, and re-layouts  15.5 us (6%)
  waiting for transfers between devices  13.2 us (5%)
    pallas_call x33, Pallas kernels, call(): pl.pallas_call(kernel, out_shape=outs, in_specs=[pl.BlockSpec(memory_spac...  114 us
    all_to_all x11, starting transfers between devices, exchange(): return lax.all_to_all(message, 'flow', 0, 0, tiled=True)  85 us
    ppermute x40, starting transfers between devices, both_ways(): return (lax.ppermute(ahead, axis, up), lax.ppermute(back, axis, down))  44.7 us
    while x48, local copies, waits for them, and re-layouts  10.1 us
    ppermute x40, waiting for transfers between devices, both_ways(): return (lax.ppermute(ahead, axis, up), lax.ppermute(back, axis, down))  7.5 us
    all_to_all x11, waiting for transfers between devices, exchange(): return lax.all_to_all(message, 'flow', 0, 0, tiled=True)  5.7 us
  transfers between devices with their start and end apart: 51, of which 11 were waited for; matrix products, arithmetic and copies ran while one was open for 0% of the time, Pallas kernels for 38%

profile of v1, /device:TPU:97, one launch (start us, length us, event | category | flops | bytes accessed | tf_op | source)
XLA Modules:
  0.0 274.4 jit_solution(17148936315124953564)
XLA Ops:
  4.4 7.9 %all-to-all-start.1 = ((f32[32,24,128]{2,1,0:T(8,128)}), f32[32,24,128]{2,1,0:T(8,128)S(1)}, u32[]{:S(2)}, u32[]{:S(2)}) async-start(f32[32,24,128]{2,1,0:T(8,128)} %get-tuple-element.120), calls=%async_computation.1 | async-start | bytes 786432 | tf_op jit(solution)/shard_map/all_to_all | solution.py:545
  16.9 5.7 %all-to-all-done.1.got_hbm = f32[32,24,128]{2,1,0:T(8,128)S(1)} async-done(((f32[32,24,128]{2,1,0:T(8,128)}), f32[32,24,128]{2,1,0:T(8,128)S(1)}, u32[]{:S(2)}, u32[]{:S(2)}) %all-to-all-start.1) | async-done | bytes 393248 | tf_op jit(solution)/shard_map/all_to_all | solution.py:545
  23.3 3.6 %shard_map.88 = (bf16[64,512]{1,0:T(8,128)(2,1)}, bf16[512,128]{1,0:T(8,128)(2,1)S(1)}, bf16[2,512,128]{2,1,0:T(8,128)(2,1)}, bf16[2,128,512]{2,1,0:T(8,128)(2,1...) custom-call(f32[32,24,128]{2,1,0:T(8,128)} %copy-done.6, ...), custom_call_target="tpu_custom_call" | custom-call | tf_op jit(solution)/shard_map/pallas_call | solution.py:68
  26.9 197.7 %while.20 = (s32[]{:T(128)}, f32[32,64,128]{2,1,0:T(8,128)S(1)}, f32[64,128]{1,0:T(8,128)}, f32[64,128]{1,0:T(8,128)}, f32[32,128]{1,0:T(8,128)S(1)}, /*index=5*...) while((s32[]{:T(128)}, f32[32,64,128]{2,1,0:T(8,128)S(1)}, ...), condition=%wide.region_1.2_spmd, body=%wide.region_0.1_spmd.sunk | while | flops 10000002 | bytes 14573289 | solution.py:626
  27.0 3.8 %all-to-all-start = ((f32[32,8,128]{2,1,0:T(8,128)}), f32[32,8,128]{2,1,0:T(8,128)S(1)}, u32[]{:S(2)}, u32[]{:S(2)}) async-start(f32[32,8,128]{2,1,0:T(8,128)} %get-tuple-element.305), calls=%async_computation | async-start | bytes 262144 | tf_op jit(solution)/shard_map/while/body/eval_jaxpr/all_to_all | solution.py:545
  30.8 2.9 %collective-permute-start = (f32[64,128]{1,0:T(8,128)}, f32[64,128]{1,0:T(8,128)S(1)}, u32[]{:S(2)}, u32[]{:S(2)}) collective-permute-start(f32[64,128]{1,0:T(8,128)} %get-tuple-element.302), channel_id=1, source_target_pairs={{0,1},{1,2},{2,3},{3,4},{4,5},{5,6},{6,7},{7,0},{8,9},{9,10},{10,1... | collective-permute-start | bytes 98312 | tf_op jit(solution)/shard_map/while/body/eval_jaxpr/ppermute | solution.py:542
  33.7 2.9 %eval_jaxpr.3.sink_hbm = f32[64,128]{1,0:T(8,128)} custom-call(f32[64,128]{1,0:T(8,128)} %get-tuple-element.301.bottom_hbm, bf16[64,512]{1,0:T(8,128)(2,1)} %get-tuple-element.322.hit_hbm, bf16[512,128]{1,0:T(8,128)(2,1)S(1)} %get-tuple-element.323.hit_t_hbm, f32[3,512,128]{2,1,0:T(8,128)S(1)} %get-tuple-element.324.swell_hbm), custom_call_target="tpu_custom_call" | custom-call | flops 2000000 | bytes 3000000 | tf_op jit(solution)/shard_map/while/body/eval_jaxpr/pallas_call | solution.py:68
  38.8 4.4 %eval_jaxpr.4 = (f32[32,64,128]{2,1,0:T(8,128)S(1)}, f32[64,128]{1,0:T(8,128)}, f32[64,128]{1,0:T(8,128)}, f32[32,128]{1,0:T(8,128)}, f32[32,128]{1,0:T(8,128)}) custom-call(f32[32,64,128]{2,1,0:T(8,128)S(1)} %get-tuple-element.300.solid_hbm, f32[64,128]{1,0:T(8,128)} %get-tuple-element.301.bottom_hbm, ...), custom_call_target="tpu_custom_call", output_to_operand_aliasing={{0}: (0, {})} | custom-call | flops 4000000 | bytes 6000000 | tf_op jit(solution)/shard_map/while/body/eval_jaxpr/pallas_call | solution.py:68
  43.2 2.8 %collective-permute-start.2 = (f32[32,128]{1,0:T(8,128)}, f32[32,128]{1,0:T(8,128)S(1)}, u32[]{:S(2)}, u32[]{:S(2)}) collective-permute-start(f32[32,128]{1,0:T(8,128)} %get-tuple-element.280), channel_id=1, source_target_pairs={{0,8},{8,16},{16,24},{24,32},{32,40},{40,48},{48,56},{56,64},{64,7... | collective-permute-start | bytes 49160 | tf_op jit(solution)/shard_map/while/body/eval_jaxpr/ppermute | solution.py:542
  46.7 3.2 %eval_jaxpr.5 = (f32[64,128]{1,0:T(8,128)}, f32[32,8,128]{2,1,0:T(8,128)}, f32[64,128]{1,0:T(8,128)}) custom-call(f32[32,8,128]{2,1,0:T(8,128)} %copy-done.2, f32[64,128]{1,0:T(8,128)} %get-tuple-element.276.base_hbm, f32[64,128]{1,0:T(8,128)} %get-tuple-element.277.plain_hbm, s32[5,32,128]{2,1,0:T(8,128)} %get-tuple-element.326.index_hbm, ...), custom_call_target="tpu_custom_call" | custom-call | flops 4000000 | bytes 4000000 | tf_op jit(solution)/shard_map/while/body/eval_jaxpr/pallas_call | solution.py:68
  49.9 8.2 %all-to-all-start = ((f32[32,8,128]{2,1,0:T(8,128)}), f32[32,8,128]{2,1,0:T(8,128)S(1)}, u32[]{:S(2)}, u32[]{:S(2)}) async-start(f32[32,8,128]{2,1,0:T(8,128)} %get-tuple-element.305), calls=%async_computation | async-start | bytes 262144 | tf_op jit(solution)/shard_map/while/body/eval_jaxpr/all_to_all | solution.py:545
  59.7 2.9 %eval_jaxpr.3.sink_hbm = f32[64,128]{1,0:T(8,128)} custom-call(f32[64,128]{1,0:T(8,128)} %get-tuple-element.301.bottom_hbm, bf16[64,512]{1,0:T(8,128)(2,1)} %get-tuple-element.322.hit_hbm, bf16[512,128]{1,0:T(8,128)(2,1)S(1)} %get-tuple-element.323.hit_t_hbm, f32[3,512,128]{2,1,0:T(8,128)S(1)} %get-tuple-element.324.swell_hbm), custom_call_target="tpu_custom_call" | custom-call | flops 2000000 | bytes 3000000 | tf_op jit(solution)/shard_map/while/body/eval_jaxpr/pallas_call | solution.py:68
  63.9 4.4 %eval_jaxpr.4 = (f32[32,64,128]{2,1,0:T(8,128)S(1)}, f32[64,128]{1,0:T(8,128)}, f32[64,128]{1,0:T(8,128)}, f32[32,128]{1,0:T(8,128)}, f32[32,128]{1,0:T(8,128)}) custom-call(f32[32,64,128]{2,1,0:T(8,128)S(1)} %get-tuple-element.300.solid_hbm, f32[64,128]{1,0:T(8,128)} %get-tuple-element.301.bottom_hbm, ...), custom_call_target="tpu_custom_call", output_to_operand_aliasing={{0}: (0, {})} | custom-call | flops 4000000 | bytes 6000000 | tf_op jit(solution)/shard_map/while/body/eval_jaxpr/pallas_call | solution.py:68
  68.2 2.8 %collective-permute-start.2 = (f32[32,128]{1,0:T(8,128)}, f32[32,128]{1,0:T(8,128)S(1)}, u32[]{:S(2)}, u32[]{:S(2)}) collective-permute-start(f32[32,128]{1,0:T(8,128)} %get-tuple-element.280), channel_id=1, source_target_pairs={{0,8},{8,16},{16,24},{24,32},{32,40},{40,48},{48,56},{56,64},{64,7... | collective-permute-start | bytes 49160 | tf_op jit(solution)/shard_map/while/body/eval_jaxpr/ppermute | solution.py:542
  71.8 3.2 %eval_jaxpr.5 = (f32[64,128]{1,0:T(8,128)}, f32[32,8,128]{2,1,0:T(8,128)}, f32[64,128]{1,0:T(8,128)}) custom-call(f32[32,8,128]{2,1,0:T(8,128)} %copy-done.2, f32[64,128]{1,0:T(8,128)} %get-tuple-element.276.base_hbm, f32[64,128]{1,0:T(8,128)} %get-tuple-element.277.plain_hbm, s32[5,32,128]{2,1,0:T(8,128)} %get-tuple-element.326.index_hbm, ...), custom_call_target="tpu_custom_call" | custom-call | flops 4000000 | bytes 4000000 | tf_op jit(solution)/shard_map/while/body/eval_jaxpr/pallas_call | solution.py:68
  75.0 8.1 %all-to-all-start = ((f32[32,8,128]{2,1,0:T(8,128)}), f32[32,8,128]{2,1,0:T(8,128)S(1)}, u32[]{:S(2)}, u32[]{:S(2)}) async-start(f32[32,8,128]{2,1,0:T(8,128)} %get-tuple-element.305), calls=%async_computation | async-start | bytes 262144 | tf_op jit(solution)/shard_map/while/body/eval_jaxpr/all_to_all | solution.py:545
  84.6 2.9 %eval_jaxpr.3.sink_hbm = f32[64,128]{1,0:T(8,128)} custom-call(f32[64,128]{1,0:T(8,128)} %get-tuple-element.301.bottom_hbm, bf16[64,512]{1,0:T(8,128)(2,1)} %get-tuple-element.322.hit_hbm, bf16[512,128]{1,0:T(8,128)(2,1)S(1)} %get-tuple-element.323.hit_t_hbm, f32[3,512,128]{2,1,0:T(8,128)S(1)} %get-tuple-element.324.swell_hbm), custom_call_target="tpu_custom_call" | custom-call | flops 2000000 | bytes 3000000 | tf_op jit(solution)/shard_map/while/body/eval_jaxpr/pallas_call | solution.py:68
  88.8 4.4 %eval_jaxpr.4 = (f32[32,64,128]{2,1,0:T(8,128)S(1)}, f32[64,128]{1,0:T(8,128)}, f32[64,128]{1,0:T(8,128)}, f32[32,128]{1,0:T(8,128)}, f32[32,128]{1,0:T(8,128)}) custom-call(f32[32,64,128]{2,1,0:T(8,128)S(1)} %get-tuple-element.300.solid_hbm, f32[64,128]{1,0:T(8,128)} %get-tuple-element.301.bottom_hbm, ...), custom_call_target="tpu_custom_call", output_to_operand_aliasing={{0}: (0, {})} | custom-call | flops 4000000 | bytes 6000000 | tf_op jit(solution)/shard_map/while/body/eval_jaxpr/pallas_call | solution.py:68
  93.2 2.8 %collective-permute-start.2 = (f32[32,128]{1,0:T(8,128)}, f32[32,128]{1,0:T(8,128)S(1)}, u32[]{:S(2)}, u32[]{:S(2)}) collective-permute-start(f32[32,128]{1,0:T(8,128)} %get-tuple-element.280), channel_id=1, source_target_pairs={{0,8},{8,16},{16,24},{24,32},{32,40},{40,48},{48,56},{56,64},{64,7... | collective-permute-start | bytes 49160 | tf_op jit(solution)/shard_map/while/body/eval_jaxpr/ppermute | solution.py:542
  96.7 3.2 %eval_jaxpr.5 = (f32[64,128]{1,0:T(8,128)}, f32[32,8,128]{2,1,0:T(8,128)}, f32[64,128]{1,0:T(8,128)}) custom-call(f32[32,8,128]{2,1,0:T(8,128)} %copy-done.2, f32[64,128]{1,0:T(8,128)} %get-tuple-element.276.base_hbm, f32[64,128]{1,0:T(8,128)} %get-tuple-element.277.plain_hbm, s32[5,32,128]{2,1,0:T(8,128)} %get-tuple-element.326.index_hbm, ...), custom_call_target="tpu_custom_call" | custom-call | flops 4000000 | bytes 4000000 | tf_op jit(solution)/shard_map/while/body/eval_jaxpr/pallas_call | solution.py:68
  99.9 8.1 %all-to-all-start = ((f32[32,8,128]{2,1,0:T(8,128)}), f32[32,8,128]{2,1,0:T(8,128)S(1)}, u32[]{:S(2)}, u32[]{:S(2)}) async-start(f32[32,8,128]{2,1,0:T(8,128)} %get-tuple-element.305), calls=%async_computation | async-start | bytes 262144 | tf_op jit(solution)/shard_map/while/body/eval_jaxpr/all_to_all | solution.py:545
  109.6 2.9 %eval_jaxpr.3.sink_hbm = f32[64,128]{1,0:T(8,128)} custom-call(f32[64,128]{1,0:T(8,128)} %get-tuple-element.301.bottom_hbm, bf16[64,512]{1,0:T(8,128)(2,1)} %get-tuple-element.322.hit_hbm, bf16[512,128]{1,0:T(8,128)(2,1)S(1)} %get-tuple-element.323.hit_t_hbm, f32[3,512,128]{2,1,0:T(8,128)S(1)} %get-tuple-element.324.swell_hbm), custom_call_target="tpu_custom_call" | custom-call | flops 2000000 | bytes 3000000 | tf_op jit(solution)/shard_map/while/body/eval_jaxpr/pallas_call | solution.py:68
  113.8 4.4 %eval_jaxpr.4 = (f32[32,64,128]{2,1,0:T(8,128)S(1)}, f32[64,128]{1,0:T(8,128)}, f32[64,128]{1,0:T(8,128)}, f32[32,128]{1,0:T(8,128)}, f32[32,128]{1,0:T(8,128)}) custom-call(f32[32,64,128]{2,1,0:T(8,128)S(1)} %get-tuple-element.300.solid_hbm, f32[64,128]{1,0:T(8,128)} %get-tuple-element.301.bottom_hbm, ...), custom_call_target="tpu_custom_call", output_to_operand_aliasing={{0}: (0, {})} | custom-call | flops 4000000 | bytes 6000000 | tf_op jit(solution)/shard_map/while/body/eval_jaxpr/pallas_call | solution.py:68
  121.7 3.2 %eval_jaxpr.5 = (f32[64,128]{1,0:T(8,128)}, f32[32,8,128]{2,1,0:T(8,128)}, f32[64,128]{1,0:T(8,128)}) custom-call(f32[32,8,128]{2,1,0:T(8,128)} %copy-done.2, f32[64,128]{1,0:T(8,128)} %get-tuple-element.276.base_hbm, f32[64,128]{1,0:T(8,128)} %get-tuple-element.277.plain_hbm, s32[5,32,128]{2,1,0:T(8,128)} %get-tuple-element.326.index_hbm, ...), custom_call_target="tpu_custom_call" | custom-call | flops 4000000 | bytes 4000000 | tf_op jit(solution)/shard_map/while/body/eval_jaxpr/pallas_call | solution.py:68
  124.9 8.1 %all-to-all-start = ((f32[32,8,128]{2,1,0:T(8,128)}), f32[32,8,128]{2,1,0:T(8,128)S(1)}, u32[]{:S(2)}, u32[]{:S(2)}) async-start(f32[32,8,128]{2,1,0:T(8,128)} %get-tuple-element.305), calls=%async_computation | async-start | bytes 262144 | tf_op jit(solution)/shard_map/while/body/eval_jaxpr/all_to_all | solution.py:545
  134.5 2.9 %eval_jaxpr.3.sink_hbm = f32[64,128]{1,0:T(8,128)} custom-call(f32[64,128]{1,0:T(8,128)} %get-tuple-element.301.bottom_hbm, bf16[64,512]{1,0:T(8,128)(2,1)} %get-tuple-element.322.hit_hbm, bf16[512,128]{1,0:T(8,128)(2,1)S(1)} %get-tuple-element.323.hit_t_hbm, f32[3,512,128]{2,1,0:T(8,128)S(1)} %get-tuple-element.324.swell_hbm), custom_call_target="tpu_custom_call" | custom-call | flops 2000000 | bytes 3000000 | tf_op jit(solution)/shard_map/while/body/eval_jaxpr/pallas_call | solution.py:68
  138.7 4.4 %eval_jaxpr.4 = (f32[32,64,128]{2,1,0:T(8,128)S(1)}, f32[64,128]{1,0:T(8,128)}, f32[64,128]{1,0:T(8,128)}, f32[32,128]{1,0:T(8,128)}, f32[32,128]{1,0:T(8,128)}) custom-call(f32[32,64,128]{2,1,0:T(8,128)S(1)} %get-tuple-element.300.solid_hbm, f32[64,128]{1,0:T(8,128)} %get-tuple-element.301.bottom_hbm, ...), custom_call_target="tpu_custom_call", output_to_operand_aliasing={{0}: (0, {})} | custom-call | flops 4000000 | bytes 6000000 | tf_op jit(solution)/shard_map/while/body/eval_jaxpr/pallas_call | solution.py:68
  146.6 3.2 %eval_jaxpr.5 = (f32[64,128]{1,0:T(8,128)}, f32[32,8,128]{2,1,0:T(8,128)}, f32[64,128]{1,0:T(8,128)}) custom-call(f32[32,8,128]{2,1,0:T(8,128)} %copy-done.2, f32[64,128]{1,0:T(8,128)} %get-tuple-element.276.base_hbm, f32[64,128]{1,0:T(8,128)} %get-tuple-element.277.plain_hbm, s32[5,32,128]{2,1,0:T(8,128)} %get-tuple-element.326.index_hbm, ...), custom_call_target="tpu_custom_call" | custom-call | flops 4000000 | bytes 4000000 | tf_op jit(solution)/shard_map/while/body/eval_jaxpr/pallas_call | solution.py:68
  149.8 8.1 %all-to-all-start = ((f32[32,8,128]{2,1,0:T(8,128)}), f32[32,8,128]{2,1,0:T(8,128)S(1)}, u32[]{:S(2)}, u32[]{:S(2)}) async-start(f32[32,8,128]{2,1,0:T(8,128)} %get-tuple-element.305), calls=%async_computation | async-start | bytes 262144 | tf_op jit(solution)/shard_map/while/body/eval_jaxpr/all_to_all | solution.py:545
  159.5 2.9 %eval_jaxpr.3.sink_hbm = f32[64,128]{1,0:T(8,128)} custom-call(f32[64,128]{1,0:T(8,128)} %get-tuple-element.301.bottom_hbm, bf16[64,512]{1,0:T(8,128)(2,1)} %get-tuple-element.322.hit_hbm, bf16[512,128]{1,0:T(8,128)(2,1)S(1)} %get-tuple-element.323.hit_t_hbm, f32[3,512,128]{2,1,0:T(8,128)S(1)} %get-tuple-element.324.swell_hbm), custom_call_target="tpu_custom_call" | custom-call | flops 2000000 | bytes 3000000 | tf_op jit(solution)/shard_map/while/body/eval_jaxpr/pallas_call | solution.py:68
  163.7 4.4 %eval_jaxpr.4 = (f32[32,64,128]{2,1,0:T(8,128)S(1)}, f32[64,128]{1,0:T(8,128)}, f32[64,128]{1,0:T(8,128)}, f32[32,128]{1,0:T(8,128)}, f32[32,128]{1,0:T(8,128)}) custom-call(f32[32,64,128]{2,1,0:T(8,128)S(1)} %get-tuple-element.300.solid_hbm, f32[64,128]{1,0:T(8,128)} %get-tuple-element.301.bottom_hbm, ...), custom_call_target="tpu_custom_call", output_to_operand_aliasing={{0}: (0, {})} | custom-call | flops 4000000 | bytes 6000000 | tf_op jit(solution)/shard_map/while/body/eval_jaxpr/pallas_call | solution.py:68
  171.6 3.2 %eval_jaxpr.5 = (f32[64,128]{1,0:T(8,128)}, f32[32,8,128]{2,1,0:T(8,128)}, f32[64,128]{1,0:T(8,128)}) custom-call(f32[32,8,128]{2,1,0:T(8,128)} %copy-done.2, f32[64,128]{1,0:T(8,128)} %get-tuple-element.276.base_hbm, f32[64,128]{1,0:T(8,128)} %get-tuple-element.277.plain_hbm, s32[5,32,128]{2,1,0:T(8,128)} %get-tuple-element.326.index_hbm, ...), custom_call_target="tpu_custom_call" | custom-call | flops 4000000 | bytes 4000000 | tf_op jit(solution)/shard_map/while/body/eval_jaxpr/pallas_call | solution.py:68
  174.8 8.1 %all-to-all-start = ((f32[32,8,128]{2,1,0:T(8,128)}), f32[32,8,128]{2,1,0:T(8,128)S(1)}, u32[]{:S(2)}, u32[]{:S(2)}) async-start(f32[32,8,128]{2,1,0:T(8,128)} %get-tuple-element.305), calls=%async_computation | async-start | bytes 262144 | tf_op jit(solution)/shard_map/while/body/eval_jaxpr/all_to_all | solution.py:545
  184.4 2.9 %eval_jaxpr.3.sink_hbm = f32[64,128]{1,0:T(8,128)} custom-call(f32[64,128]{1,0:T(8,128)} %get-tuple-element.301.bottom_hbm, bf16[64,512]{1,0:T(8,128)(2,1)} %get-tuple-element.322.hit_hbm, bf16[512,128]{1,0:T(8,128)(2,1)S(1)} %get-tuple-element.323.hit_t_hbm, f32[3,512,128]{2,1,0:T(8,128)S(1)} %get-tuple-element.324.swell_hbm), custom_call_target="tpu_custom_call" | custom-call | flops 2000000 | bytes 3000000 | tf_op jit(solution)/shard_map/while/body/eval_jaxpr/pallas_call | solution.py:68
  188.6 4.4 %eval_jaxpr.4 = (f32[32,64,128]{2,1,0:T(8,128)S(1)}, f32[64,128]{1,0:T(8,128)}, f32[64,128]{1,0:T(8,128)}, f32[32,128]{1,0:T(8,128)}, f32[32,128]{1,0:T(8,128)}) custom-call(f32[32,64,128]{2,1,0:T(8,128)S(1)} %get-tuple-element.300.solid_hbm, f32[64,128]{1,0:T(8,128)} %get-tuple-element.301.bottom_hbm, ...), custom_call_target="tpu_custom_call", output_to_operand_aliasing={{0}: (0, {})} | custom-call | flops 4000000 | bytes 6000000 | tf_op jit(solution)/shard_map/while/body/eval_jaxpr/pallas_call | solution.py:68
  196.5 3.2 %eval_jaxpr.5 = (f32[64,128]{1,0:T(8,128)}, f32[32,8,128]{2,1,0:T(8,128)}, f32[64,128]{1,0:T(8,128)}) custom-call(f32[32,8,128]{2,1,0:T(8,128)} %copy-done.2, f32[64,128]{1,0:T(8,128)} %get-tuple-element.276.base_hbm, f32[64,128]{1,0:T(8,128)} %get-tuple-element.277.plain_hbm, s32[5,32,128]{2,1,0:T(8,128)} %get-tuple-element.326.index_hbm, ...), custom_call_target="tpu_custom_call" | custom-call | flops 4000000 | bytes 4000000 | tf_op jit(solution)/shard_map/while/body/eval_jaxpr/pallas_call | solution.py:68
  199.7 8.1 %all-to-all-start = ((f32[32,8,128]{2,1,0:T(8,128)}), f32[32,8,128]{2,1,0:T(8,128)S(1)}, u32[]{:S(2)}, u32[]{:S(2)}) async-start(f32[32,8,128]{2,1,0:T(8,128)} %get-tuple-element.305), calls=%async_computation | async-start | bytes 262144 | tf_op jit(solution)/shard_map/while/body/eval_jaxpr/all_to_all | solution.py:545
  209.4 2.9 %eval_jaxpr.3.sink_hbm = f32[64,128]{1,0:T(8,128)} custom-call(f32[64,128]{1,0:T(8,128)} %get-tuple-element.301.bottom_hbm, bf16[64,512]{1,0:T(8,128)(2,1)} %get-tuple-element.322.hit_hbm, bf16[512,128]{1,0:T(8,128)(2,1)S(1)} %get-tuple-element.323.hit_t_hbm, f32[3,512,128]{2,1,0:T(8,128)S(1)} %get-tuple-element.324.swell_hbm), custom_call_target="tpu_custom_call" | custom-call | flops 2000000 | bytes 3000000 | tf_op jit(solution)/shard_map/while/body/eval_jaxpr/pallas_call | solution.py:68
  213.6 4.4 %eval_jaxpr.4 = (f32[32,64,128]{2,1,0:T(8,128)S(1)}, f32[64,128]{1,0:T(8,128)}, f32[64,128]{1,0:T(8,128)}, f32[32,128]{1,0:T(8,128)}, f32[32,128]{1,0:T(8,128)}) custom-call(f32[32,64,128]{2,1,0:T(8,128)S(1)} %get-tuple-element.300.solid_hbm, f32[64,128]{1,0:T(8,128)} %get-tuple-element.301.bottom_hbm, ...), custom_call_target="tpu_custom_call", output_to_operand_aliasing={{0}: (0, {})} | custom-call | flops 4000000 | bytes 6000000 | tf_op jit(solution)/shard_map/while/body/eval_jaxpr/pallas_call | solution.py:68
  221.5 3.2 %eval_jaxpr.5 = (f32[64,128]{1,0:T(8,128)}, f32[32,8,128]{2,1,0:T(8,128)}, f32[64,128]{1,0:T(8,128)}) custom-call(f32[32,8,128]{2,1,0:T(8,128)} %copy-done.2, f32[64,128]{1,0:T(8,128)} %get-tuple-element.276.base_hbm, f32[64,128]{1,0:T(8,128)} %get-tuple-element.277.plain_hbm, s32[5,32,128]{2,1,0:T(8,128)} %get-tuple-element.326.index_hbm, ...), custom_call_target="tpu_custom_call" | custom-call | flops 4000000 | bytes 4000000 | tf_op jit(solution)/shard_map/while/body/eval_jaxpr/pallas_call | solution.py:68
  225.3 8.1 %all-to-all-start.2 = ((f32[32,8,128]{2,1,0:T(8,128)}), f32[32,8,128]{2,1,0:T(8,128)}, u32[]{:S(2)}, u32[]{:S(2)}) async-start(f32[32,8,128]{2,1,0:T(8,128)} %get-tuple-element.129), calls=%async_computation.2 | async-start | bytes 262144 | tf_op jit(solution)/shard_map/all_to_all | solution.py:545
  235.0 2.9 %shard_map.89.sink_hbm = f32[64,128]{1,0:T(8,128)} custom-call(f32[64,128]{1,0:T(8,128)} %get-tuple-element.131.bottom_hbm, bf16[64,512]{1,0:T(8,128)(2,1)S(1)} %copy-done.3, bf16[512,128]{1,0:T(8,128)(2,1)S(1)} %get-tuple-element.333, f32[3,512,128]{2,1,0:T(8,128)S(1)} %get-tuple-element.332), custom_call_target="tpu_custom_call" | custom-call | flops 2000000 | bytes 3000000 | tf_op jit(solution)/shard_map/pallas_call | solution.py:68
  239.1 4.4 %shard_map.90 = (f32[32,64,128]{2,1,0:T(8,128)S(1)}, f32[64,128]{1,0:T(8,128)}, f32[64,128]{1,0:T(8,128)}, f32[32,128]{1,0:T(8,128)}, f32[32,128]{1,0:T(8,128)}) custom-call(f32[32,64,128]{2,1,0:T(8,128)S(1)} %get-tuple-element.130.solid_hbm, f32[64,128]{1,0:T(8,128)} %get-tuple-element.131.bottom_hbm, ...), custom_call_target="tpu_custom_call", output_to_operand_aliasing={{0}: (0, {})} | custom-call | flops 4000000 | bytes 6000000 | tf_op jit(solution)/shard_map/pallas_call | solution.py:68
  243.5 3.4 %shard_map.91 = (f32[64,128]{1,0:T(8,128)}, f32[32,24,128]{2,1,0:T(8,128)}, f32[64,128]{1,0:T(8,128)}) custom-call(f32[32,8,128]{2,1,0:T(8,128)} %all-to-all-done.2.got_hbm, f32[64,128]{1,0:T(8,128)} %get-tuple-element.135.base_hbm, f32[64,128]{1,0:T(8,128)} %get-tuple-element.136.plain_hbm, s32[5,32,128]{2,1,0:T(8,128)S(1)} %copy-done.5, ...), custom_call_target="tpu_custom_call" | custom-call | flops 4000000 | bytes 4000000 | tf_op jit(solution)/shard_map/pallas_call | solution.py:68
  246.9 8.5 %all-to-all-start.3 = ((f32[32,24,128]{2,1,0:T(8,128)}), f32[32,24,128]{2,1,0:T(8,128)}, u32[]{:S(2)}, u32[]{:S(2)}) async-start(f32[32,24,128]{2,1,0:T(8,128)} %get-tuple-element.137), calls=%async_computation.3 | async-start | bytes 786432 | tf_op jit(solution)/shard_map/all_to_all | solution.py:545
  260.3 2.9 %shard_map.92.sink_hbm = f32[64,128]{1,0:T(8,128)} custom-call(f32[64,128]{1,0:T(8,128)} %get-tuple-element.139.bottom_hbm, bf16[64,512]{1,0:T(8,128)(2,1)S(1)} %copy-done.3, bf16[512,128]{1,0:T(8,128)(2,1)S(1)} %get-tuple-element.333, f32[3,512,128]{2,1,0:T(8,128)S(1)} %get-tuple-element.332), custom_call_target="tpu_custom_call" | custom-call | flops 2000000 | bytes 3000000 | tf_op jit(solution)/shard_map/pallas_call | solution.py:68
  264.7 4.4 %shard_map.93 = (f32[32,64,128]{2,1,0:T(8,128)S(1)}, f32[64,128]{1,0:T(8,128)}, f32[64,128]{1,0:T(8,128)}, f32[32,128]{1,0:T(8,128)}, f32[32,128]{1,0:T(8,128)}) custom-call(f32[32,64,128]{2,1,0:T(8,128)S(1)} %get-tuple-element.138.solid_hbm, f32[64,128]{1,0:T(8,128)} %get-tuple-element.139.bottom_hbm, ...), custom_call_target="tpu_custom_call", output_to_operand_aliasing={{0}: (0, {})} | custom-call | flops 4000000 | bytes 6000000 | tf_op jit(solution)/shard_map/pallas_call | solution.py:68
  270.1 4.1 %shard_map.94 = (f32[32,64,128]{2,1,0:T(8,128)}, f32[16,2048]{1,0:T(8,128)}) custom-call(f32[32,24,128]{2,1,0:T(8,128)} %all-to-all-done.3.got_hbm, f32[64,128]{1,0:T(8,128)} %get-tuple-element.143.base_hbm, s32[5,32,128]{2,1,0:T(8,128)S(1)} %copy-done.5, f32[12,2,32,128]{3,2,1,0:T(8,128)S(1)} %get-tuple-element.334, ...), custom_call_target="tpu_custom_call", output_to_operand_aliasing={{0}: (8, {})} | custom-call | tf_op jit(solution)/shard_map/pallas_call | solution.py:68
  (172 shorter events, 60.9 us)
Async XLA Ops:
  4.4 18.2 %all-to-all-start.1 = ((f32[32,24,128]{2,1,0:T(8,128)}), f32[32,24,128]{2,1,0:T(8,128)S(1)}, u32[]{:S(2)}, u32[]{:S(2)}) async-start(f32[32,24,128]{2,1,0:T(8,128)} %get-tuple-element.120), calls=%async_computation.1 | async-start | bytes 786432 | tf_op jit(solution)/shard_map/all_to_all | solution.py:545
  13.9 13.1 %collective-permute-start.4 = (f32[32,128]{1,0:T(8,128)}, f32[32,128]{1,0:T(8,128)S(1)}, u32[]{:S(2)}, u32[]{:S(2)}) collective-permute-start(f32[32,128]{1,0:T(8,128)} %get-tuple-element.118), channel_id=1, source_target_pairs={{0,8},{8,16},{16,24},{24,32},{32,40},{40,48},{48,56},{56,64},{64,7... | collective-permute-start | bytes 49160 | tf_op jit(solution)/shard_map/ppermute | solution.py:542
  15.6 11.4 %collective-permute-start.5 = (f32[32,128]{1,0:T(8,128)}, f32[32,128]{1,0:T(8,128)}, u32[]{:S(2)}, u32[]{:S(2)}) collective-permute-start(f32[32,128]{1,0:T(8,128)} %get-tuple-element.119), channel_id=1, source_target_pairs={{0,248},{8,0},{16,8},{24,16},{32,24},{40,32},{48,40},{56,48},{64,5... | collective-permute-start | bytes 49160 | tf_op jit(solution)/shard_map/ppermute | solution.py:542
  27.0 19.1 %all-to-all-start = ((f32[32,8,128]{2,1,0:T(8,128)}), f32[32,8,128]{2,1,0:T(8,128)S(1)}, u32[]{:S(2)}, u32[]{:S(2)}) async-start(f32[32,8,128]{2,1,0:T(8,128)} %get-tuple-element.305), calls=%async_computation | async-start | bytes 262144 | tf_op jit(solution)/shard_map/while/body/eval_jaxpr/all_to_all | solution.py:545
  30.8 5.9 %collective-permute-start = (f32[64,128]{1,0:T(8,128)}, f32[64,128]{1,0:T(8,128)S(1)}, u32[]{:S(2)}, u32[]{:S(2)}) collective-permute-start(f32[64,128]{1,0:T(8,128)} %get-tuple-element.302), channel_id=1, source_target_pairs={{0,1},{1,2},{2,3},{3,4},{4,5},{5,6},{6,7},{7,0},{8,9},{9,10},{10,1... | collective-permute-start | bytes 98312 | tf_op jit(solution)/shard_map/while/body/eval_jaxpr/ppermute | solution.py:542
  33.7 4.5 %collective-permute-start.1 = (f32[64,128]{1,0:T(8,128)}, f32[64,128]{1,0:T(8,128)S(1)}, u32[]{:S(2)}, u32[]{:S(2)}) collective-permute-start(f32[64,128]{1,0:T(8,128)} %get-tuple-element.302), channel_id=1, source_target_pairs={{0,7},{1,0},{2,1},{3,2},{4,3},{5,4},{6,5},{7,6},{8,15},{9,8},{10,9... | collective-permute-start | bytes 98312 | tf_op jit(solution)/shard_map/while/body/eval_jaxpr/ppermute | solution.py:542
  43.2 6.7 %collective-permute-start.2 = (f32[32,128]{1,0:T(8,128)}, f32[32,128]{1,0:T(8,128)S(1)}, u32[]{:S(2)}, u32[]{:S(2)}) collective-permute-start(f32[32,128]{1,0:T(8,128)} %get-tuple-element.280), channel_id=1, source_target_pairs={{0,8},{8,16},{16,24},{24,32},{32,40},{40,48},{48,56},{56,64},{64,7... | collective-permute-start | bytes 49160 | tf_op jit(solution)/shard_map/while/body/eval_jaxpr/ppermute | solution.py:542
  46.0 3.9 %collective-permute-start.3 = (f32[32,128]{1,0:T(8,128)}, f32[32,128]{1,0:T(8,128)}, u32[]{:S(2)}, u32[]{:S(2)}) collective-permute-start(f32[32,128]{1,0:T(8,128)} %get-tuple-element.281), channel_id=1, source_target_pairs={{0,248},{8,0},{16,8},{24,16},{32,24},{40,32},{48,40},{56,48},{64,5... | collective-permute-start | bytes 49160 | tf_op jit(solution)/shard_map/while/body/eval_jaxpr/ppermute | solution.py:542
  49.9 21.2 %all-to-all-start = ((f32[32,8,128]{2,1,0:T(8,128)}), f32[32,8,128]{2,1,0:T(8,128)S(1)}, u32[]{:S(2)}, u32[]{:S(2)}) async-start(f32[32,8,128]{2,1,0:T(8,128)} %get-tuple-element.305), calls=%async_computation | async-start | bytes 262144 | tf_op jit(solution)/shard_map/while/body/eval_jaxpr/all_to_all | solution.py:545
  58.1 4.5 %collective-permute-start = (f32[64,128]{1,0:T(8,128)}, f32[64,128]{1,0:T(8,128)S(1)}, u32[]{:S(2)}, u32[]{:S(2)}) collective-permute-start(f32[64,128]{1,0:T(8,128)} %get-tuple-element.302), channel_id=1, source_target_pairs={{0,1},{1,2},{2,3},{3,4},{4,5},{5,6},{6,7},{7,0},{8,9},{9,10},{10,1... | collective-permute-start | bytes 98312 | tf_op jit(solution)/shard_map/while/body/eval_jaxpr/ppermute | solution.py:542
  58.8 4.5 %collective-permute-start.1 = (f32[64,128]{1,0:T(8,128)}, f32[64,128]{1,0:T(8,128)S(1)}, u32[]{:S(2)}, u32[]{:S(2)}) collective-permute-start(f32[64,128]{1,0:T(8,128)} %get-tuple-element.302), channel_id=1, source_target_pairs={{0,7},{1,0},{2,1},{3,2},{4,3},{5,4},{6,5},{7,6},{8,15},{9,8},{10,9... | collective-permute-start | bytes 98312 | tf_op jit(solution)/shard_map/while/body/eval_jaxpr/ppermute | solution.py:542
  68.2 6.7 %collective-permute-start.2 = (f32[32,128]{1,0:T(8,128)}, f32[32,128]{1,0:T(8,128)S(1)}, u32[]{:S(2)}, u32[]{:S(2)}) collective-permute-start(f32[32,128]{1,0:T(8,128)} %get-tuple-element.280), channel_id=1, source_target_pairs={{0,8},{8,16},{16,24},{24,32},{32,40},{40,48},{48,56},{56,64},{64,7... | collective-permute-start | bytes 49160 | tf_op jit(solution)/shard_map/while/body/eval_jaxpr/ppermute | solution.py:542
  75.0 21.1 %all-to-all-start = ((f32[32,8,128]{2,1,0:T(8,128)}), f32[32,8,128]{2,1,0:T(8,128)S(1)}, u32[]{:S(2)}, u32[]{:S(2)}) async-start(f32[32,8,128]{2,1,0:T(8,128)} %get-tuple-element.305), calls=%async_computation | async-start | bytes 262144 | tf_op jit(solution)/shard_map/while/body/eval_jaxpr/all_to_all | solution.py:545
  83.1 4.5 %collective-permute-start = (f32[64,128]{1,0:T(8,128)}, f32[64,128]{1,0:T(8,128)S(1)}, u32[]{:S(2)}, u32[]{:S(2)}) collective-permute-start(f32[64,128]{1,0:T(8,128)} %get-tuple-element.302), channel_id=1, source_target_pairs={{0,1},{1,2},{2,3},{3,4},{4,5},{5,6},{6,7},{7,0},{8,9},{9,10},{10,1... | collective-permute-start | bytes 98312 | tf_op jit(solution)/shard_map/while/body/eval_jaxpr/ppermute | solution.py:542
  83.7 4.5 %collective-permute-start.1 = (f32[64,128]{1,0:T(8,128)}, f32[64,128]{1,0:T(8,128)S(1)}, u32[]{:S(2)}, u32[]{:S(2)}) collective-permute-start(f32[64,128]{1,0:T(8,128)} %get-tuple-element.302), channel_id=1, source_target_pairs={{0,7},{1,0},{2,1},{3,2},{4,3},{5,4},{6,5},{7,6},{8,15},{9,8},{10,9... | collective-permute-start | bytes 98312 | tf_op jit(solution)/shard_map/while/body/eval_jaxpr/ppermute | solution.py:542
  93.2 6.7 %collective-permute-start.2 = (f32[32,128]{1,0:T(8,128)}, f32[32,128]{1,0:T(8,128)S(1)}, u32[]{:S(2)}, u32[]{:S(2)}) collective-permute-start(f32[32,128]{1,0:T(8,128)} %get-tuple-element.280), channel_id=1, source_target_pairs={{0,8},{8,16},{16,24},{24,32},{32,40},{40,48},{48,56},{56,64},{64,7... | collective-permute-start | bytes 49160 | tf_op jit(solution)/shard_map/while/body/eval_jaxpr/ppermute | solution.py:542
  96.0 3.9 %collective-permute-start.3 = (f32[32,128]{1,0:T(8,128)}, f32[32,128]{1,0:T(8,128)}, u32[]{:S(2)}, u32[]{:S(2)}) collective-permute-start(f32[32,128]{1,0:T(8,128)} %get-tuple-element.281), channel_id=1, source_target_pairs={{0,248},{8,0},{16,8},{24,16},{32,24},{40,32},{48,40},{56,48},{64,5... | collective-permute-start | bytes 49160 | tf_op jit(solution)/shard_map/while/body/eval_jaxpr/ppermute | solution.py:542
  99.9 21.1 %all-to-all-start = ((f32[32,8,128]{2,1,0:T(8,128)}), f32[32,8,128]{2,1,0:T(8,128)S(1)}, u32[]{:S(2)}, u32[]{:S(2)}) async-start(f32[32,8,128]{2,1,0:T(8,128)} %get-tuple-element.305), calls=%async_computation | async-start | bytes 262144 | tf_op jit(solution)/shard_map/while/body/eval_jaxpr/all_to_all | solution.py:545
  108.0 4.5 %collective-permute-start = (f32[64,128]{1,0:T(8,128)}, f32[64,128]{1,0:T(8,128)S(1)}, u32[]{:S(2)}, u32[]{:S(2)}) collective-permute-start(f32[64,128]{1,0:T(8,128)} %get-tuple-element.302), channel_id=1, source_target_pairs={{0,1},{1,2},{2,3},{3,4},{4,5},{5,6},{6,7},{7,0},{8,9},{9,10},{10,1... | collective-permute-start | bytes 98312 | tf_op jit(solution)/shard_map/while/body/eval_jaxpr/ppermute | solution.py:542
  108.7 4.5 %collective-permute-start.1 = (f32[64,128]{1,0:T(8,128)}, f32[64,128]{1,0:T(8,128)S(1)}, u32[]{:S(2)}, u32[]{:S(2)}) collective-permute-start(f32[64,128]{1,0:T(8,128)} %get-tuple-element.302), channel_id=1, source_target_pairs={{0,7},{1,0},{2,1},{3,2},{4,3},{5,4},{6,5},{7,6},{8,15},{9,8},{10,9... | collective-permute-start | bytes 98312 | tf_op jit(solution)/shard_map/while/body/eval_jaxpr/ppermute | solution.py:542
  118.1 6.7 %collective-permute-start.2 = (f32[32,128]{1,0:T(8,128)}, f32[32,128]{1,0:T(8,128)S(1)}, u32[]{:S(2)}, u32[]{:S(2)}) collective-permute-start(f32[32,128]{1,0:T(8,128)} %get-tuple-element.280), channel_id=1, source_target_pairs={{0,8},{8,16},{16,24},{24,32},{32,40},{40,48},{48,56},{56,64},{64,7... | collective-permute-start | bytes 49160 | tf_op jit(solution)/shard_map/while/body/eval_jaxpr/ppermute | solution.py:542
  121.0 3.9 %collective-permute-start.3 = (f32[32,128]{1,0:T(8,128)}, f32[32,128]{1,0:T(8,128)}, u32[]{:S(2)}, u32[]{:S(2)}) collective-permute-start(f32[32,128]{1,0:T(8,128)} %get-tuple-element.281), channel_id=1, source_target_pairs={{0,248},{8,0},{16,8},{24,16},{32,24},{40,32},{48,40},{56,48},{64,5... | collective-permute-start | bytes 49160 | tf_op jit(solution)/shard_map/while/body/eval_jaxpr/ppermute | solution.py:542
  124.9 21.1 %all-to-all-start = ((f32[32,8,128]{2,1,0:T(8,128)}), f32[32,8,128]{2,1,0:T(8,128)S(1)}, u32[]{:S(2)}, u32[]{:S(2)}) async-start(f32[32,8,128]{2,1,0:T(8,128)} %get-tuple-element.305), calls=%async_computation | async-start | bytes 262144 | tf_op jit(solution)/shard_map/while/body/eval_jaxpr/all_to_all | solution.py:545
  133.0 4.5 %collective-permute-start = (f32[64,128]{1,0:T(8,128)}, f32[64,128]{1,0:T(8,128)S(1)}, u32[]{:S(2)}, u32[]{:S(2)}) collective-permute-start(f32[64,128]{1,0:T(8,128)} %get-tuple-element.302), channel_id=1, source_target_pairs={{0,1},{1,2},{2,3},{3,4},{4,5},{5,6},{6,7},{7,0},{8,9},{9,10},{10,1... | collective-permute-start | bytes 98312 | tf_op jit(solution)/shard_map/while/body/eval_jaxpr/ppermute | solution.py:542
  133.6 4.5 %collective-permute-start.1 = (f32[64,128]{1,0:T(8,128)}, f32[64,128]{1,0:T(8,128)S(1)}, u32[]{:S(2)}, u32[]{:S(2)}) collective-permute-start(f32[64,128]{1,0:T(8,128)} %get-tuple-element.302), channel_id=1, source_target_pairs={{0,7},{1,0},{2,1},{3,2},{4,3},{5,4},{6,5},{7,6},{8,15},{9,8},{10,9... | collective-permute-start | bytes 98312 | tf_op jit(solution)/shard_map/while/body/eval_jaxpr/ppermute | solution.py:542
  143.1 6.7 %collective-permute-start.2 = (f32[32,128]{1,0:T(8,128)}, f32[32,128]{1,0:T(8,128)S(1)}, u32[]{:S(2)}, u32[]{:S(2)}) collective-permute-start(f32[32,128]{1,0:T(8,128)} %get-tuple-element.280), channel_id=1, source_target_pairs={{0,8},{8,16},{16,24},{24,32},{32,40},{40,48},{48,56},{56,64},{64,7... | collective-permute-start | bytes 49160 | tf_op jit(solution)/shard_map/while/body/eval_jaxpr/ppermute | solution.py:542
  145.9 3.9 %collective-permute-start.3 = (f32[32,128]{1,0:T(8,128)}, f32[32,128]{1,0:T(8,128)}, u32[]{:S(2)}, u32[]{:S(2)}) collective-permute-start(f32[32,128]{1,0:T(8,128)} %get-tuple-element.281), channel_id=1, source_target_pairs={{0,248},{8,0},{16,8},{24,16},{32,24},{40,32},{48,40},{56,48},{64,5... | collective-permute-start | bytes 49160 | tf_op jit(solution)/shard_map/while/body/eval_jaxpr/ppermute | solution.py:542
  149.8 21.1 %all-to-all-start = ((f32[32,8,128]{2,1,0:T(8,128)}), f32[32,8,128]{2,1,0:T(8,128)S(1)}, u32[]{:S(2)}, u32[]{:S(2)}) async-start(f32[32,8,128]{2,1,0:T(8,128)} %get-tuple-element.305), calls=%async_computation | async-start | bytes 262144 | tf_op jit(solution)/shard_map/while/body/eval_jaxpr/all_to_all | solution.py:545
  157.9 4.5 %collective-permute-start = (f32[64,128]{1,0:T(8,128)}, f32[64,128]{1,0:T(8,128)S(1)}, u32[]{:S(2)}, u32[]{:S(2)}) collective-permute-start(f32[64,128]{1,0:T(8,128)} %get-tuple-element.302), channel_id=1, source_target_pairs={{0,1},{1,2},{2,3},{3,4},{4,5},{5,6},{6,7},{7,0},{8,9},{9,10},{10,1... | collective-permute-start | bytes 98312 | tf_op jit(solution)/shard_map/while/body/eval_jaxpr/ppermute | solution.py:542
  158.6 4.5 %collective-permute-start.1 = (f32[64,128]{1,0:T(8,128)}, f32[64,128]{1,0:T(8,128)S(1)}, u32[]{:S(2)}, u32[]{:S(2)}) collective-permute-start(f32[64,128]{1,0:T(8,128)} %get-tuple-element.302), channel_id=1, source_target_pairs={{0,7},{1,0},{2,1},{3,2},{4,3},{5,4},{6,5},{7,6},{8,15},{9,8},{10,9... | collective-permute-start | bytes 98312 | tf_op jit(solution)/shard_map/while/body/eval_jaxpr/ppermute | solution.py:542
  168.0 6.7 %collective-permute-start.2 = (f32[32,128]{1,0:T(8,128)}, f32[32,128]{1,0:T(8,128)S(1)}, u32[]{:S(2)}, u32[]{:S(2)}) collective-permute-start(f32[32,128]{1,0:T(8,128)} %get-tuple-element.280), channel_id=1, source_target_pairs={{0,8},{8,16},{16,24},{24,32},{32,40},{40,48},{48,56},{56,64},{64,7... | collective-permute-start | bytes 49160 | tf_op jit(solution)/shard_map/while/body/eval_jaxpr/ppermute | solution.py:542
  174.8 21.1 %all-to-all-start = ((f32[32,8,128]{2,1,0:T(8,128)}), f32[32,8,128]{2,1,0:T(8,128)S(1)}, u32[]{:S(2)}, u32[]{:S(2)}) async-start(f32[32,8,128]{2,1,0:T(8,128)} %get-tuple-element.305), calls=%async_computation | async-start | bytes 262144 | tf_op jit(solution)/shard_map/while/body/eval_jaxpr/all_to_all | solution.py:545
  182.9 4.5 %collective-permute-start = (f32[64,128]{1,0:T(8,128)}, f32[64,128]{1,0:T(8,128)S(1)}, u32[]{:S(2)}, u32[]{:S(2)}) collective-permute-start(f32[64,128]{1,0:T(8,128)} %get-tuple-element.302), channel_id=1, source_target_pairs={{0,1},{1,2},{2,3},{3,4},{4,5},{5,6},{6,7},{7,0},{8,9},{9,10},{10,1... | collective-permute-start | bytes 98312 | tf_op jit(solution)/shard_map/while/body/eval_jaxpr/ppermute | solution.py:542
  183.5 4.5 %collective-permute-start.1 = (f32[64,128]{1,0:T(8,128)}, f32[64,128]{1,0:T(8,128)S(1)}, u32[]{:S(2)}, u32[]{:S(2)}) collective-permute-start(f32[64,128]{1,0:T(8,128)} %get-tuple-element.302), channel_id=1, source_target_pairs={{0,7},{1,0},{2,1},{3,2},{4,3},{5,4},{6,5},{7,6},{8,15},{9,8},{10,9... | collective-permute-start | bytes 98312 | tf_op jit(solution)/shard_map/while/body/eval_jaxpr/ppermute | solution.py:542
  193.0 6.7 %collective-permute-start.2 = (f32[32,128]{1,0:T(8,128)}, f32[32,128]{1,0:T(8,128)S(1)}, u32[]{:S(2)}, u32[]{:S(2)}) collective-permute-start(f32[32,128]{1,0:T(8,128)} %get-tuple-element.280), channel_id=1, source_target_pairs={{0,8},{8,16},{16,24},{24,32},{32,40},{40,48},{48,56},{56,64},{64,7... | collective-permute-start | bytes 49160 | tf_op jit(solution)/shard_map/while/body/eval_jaxpr/ppermute | solution.py:542
  195.8 3.9 %collective-permute-start.3 = (f32[32,128]{1,0:T(8,128)}, f32[32,128]{1,0:T(8,128)}, u32[]{:S(2)}, u32[]{:S(2)}) collective-permute-start(f32[32,128]{1,0:T(8,128)} %get-tuple-element.281), channel_id=1, source_target_pairs={{0,248},{8,0},{16,8},{24,16},{32,24},{40,32},{48,40},{56,48},{64,5... | collective-permute-start | bytes 49160 | tf_op jit(solution)/shard_map/while/body/eval_jaxpr/ppermute | solution.py:542
  199.7 21.1 %all-to-all-start = ((f32[32,8,128]{2,1,0:T(8,128)}), f32[32,8,128]{2,1,0:T(8,128)S(1)}, u32[]{:S(2)}, u32[]{:S(2)}) async-start(f32[32,8,128]{2,1,0:T(8,128)} %get-tuple-element.305), calls=%async_computation | async-start | bytes 262144 | tf_op jit(solution)/shard_map/while/body/eval_jaxpr/all_to_all | solution.py:545
  207.8 4.5 %collective-permute-start = (f32[64,128]{1,0:T(8,128)}, f32[64,128]{1,0:T(8,128)S(1)}, u32[]{:S(2)}, u32[]{:S(2)}) collective-permute-start(f32[64,128]{1,0:T(8,128)} %get-tuple-element.302), channel_id=1, source_target_pairs={{0,1},{1,2},{2,3},{3,4},{4,5},{5,6},{6,7},{7,0},{8,9},{9,10},{10,1... | collective-permute-start | bytes 98312 | tf_op jit(solution)/shard_map/while/body/eval_jaxpr/ppermute | solution.py:542
  208.5 4.5 %collective-permute-start.1 = (f32[64,128]{1,0:T(8,128)}, f32[64,128]{1,0:T(8,128)S(1)}, u32[]{:S(2)}, u32[]{:S(2)}) collective-permute-start(f32[64,128]{1,0:T(8,128)} %get-tuple-element.302), channel_id=1, source_target_pairs={{0,7},{1,0},{2,1},{3,2},{4,3},{5,4},{6,5},{7,6},{8,15},{9,8},{10,9... | collective-permute-start | bytes 98312 | tf_op jit(solution)/shard_map/while/body/eval_jaxpr/ppermute | solution.py:542
  217.9 6.7 %collective-permute-start.2 = (f32[32,128]{1,0:T(8,128)}, f32[32,128]{1,0:T(8,128)S(1)}, u32[]{:S(2)}, u32[]{:S(2)}) collective-permute-start(f32[32,128]{1,0:T(8,128)} %get-tuple-element.280), channel_id=1, source_target_pairs={{0,8},{8,16},{16,24},{24,32},{32,40},{40,48},{48,56},{56,64},{64,7... | collective-permute-start | bytes 49160 | tf_op jit(solution)/shard_map/while/body/eval_jaxpr/ppermute | solution.py:542
  220.8 3.9 %collective-permute-start.3 = (f32[32,128]{1,0:T(8,128)}, f32[32,128]{1,0:T(8,128)}, u32[]{:S(2)}, u32[]{:S(2)}) collective-permute-start(f32[32,128]{1,0:T(8,128)} %get-tuple-element.281), channel_id=1, source_target_pairs={{0,248},{8,0},{16,8},{24,16},{32,24},{40,32},{48,40},{56,48},{64,5... | collective-permute-start | bytes 49160 | tf_op jit(solution)/shard_map/while/body/eval_jaxpr/ppermute | solution.py:542
  225.3 18.2 %all-to-all-start.2 = ((f32[32,8,128]{2,1,0:T(8,128)}), f32[32,8,128]{2,1,0:T(8,128)}, u32[]{:S(2)}, u32[]{:S(2)}) async-start(f32[32,8,128]{2,1,0:T(8,128)} %get-tuple-element.129), calls=%async_computation.2 | async-start | bytes 262144 | tf_op jit(solution)/shard_map/all_to_all | solution.py:545
  233.4 4.5 %collective-permute-start.6 = (f32[64,128]{1,0:T(8,128)S(1)}, f32[64,128]{1,0:T(8,128)S(1)}, u32[]{:S(2)}, u32[]{:S(2)}) collective-permute-start(f32[64,128]{1,0:T(8,128)S(1)} %copy-done.19), channel_id=1, source_target_pairs={{0,1},{1,2},{2,3},{3,4},{4,5},{5,6},{6,7},{7,0},{8,9},{9,10},{10,1... | collective-permute-start | bytes 98312 | tf_op jit(solution)/shard_map/ppermute | solution.py:542
  234.1 4.4 %collective-permute-start.7 = (f32[64,128]{1,0:T(8,128)S(1)}, f32[64,128]{1,0:T(8,128)S(1)}, u32[]{:S(2)}, u32[]{:S(2)}) collective-permute-start(f32[64,128]{1,0:T(8,128)S(1)} %copy-done.19), channel_id=1, source_target_pairs={{0,7},{1,0},{2,1},{3,2},{4,3},{5,4},{6,5},{7,6},{8,15},{9,8},{10,9... | collective-permute-start | bytes 98312 | tf_op jit(solution)/shard_map/ppermute | solution.py:542
  246.9 22.3 %all-to-all-start.3 = ((f32[32,24,128]{2,1,0:T(8,128)}), f32[32,24,128]{2,1,0:T(8,128)}, u32[]{:S(2)}, u32[]{:S(2)}) async-start(f32[32,24,128]{2,1,0:T(8,128)} %get-tuple-element.137), calls=%async_computation.3 | async-start | bytes 786432 | tf_op jit(solution)/shard_map/all_to_all | solution.py:545
  255.4 8.7 %collective-permute-start.9 = (f32[64,128]{1,0:T(8,128)}, f32[64,128]{1,0:T(8,128)S(1)}, u32[]{:S(2)}, u32[]{:S(2)}) collective-permute-start(f32[64,128]{1,0:T(8,128)} %get-tuple-element.140), channel_id=1, source_target_pairs={{0,7},{1,0},{2,1},{3,2},{4,3},{5,4},{6,5},{7,6},{8,15},{9,8},{10,9... | collective-permute-start | bytes 98312 | tf_op jit(solution)/shard_map/ppermute | solution.py:542
  255.4 8.6 %collective-permute-start.8 = (f32[64,128]{1,0:T(8,128)}, f32[64,128]{1,0:T(8,128)S(1)}, u32[]{:S(2)}, u32[]{:S(2)}) collective-permute-start(f32[64,128]{1,0:T(8,128)} %get-tuple-element.140), channel_id=1, source_target_pairs={{0,1},{1,2},{2,3},{3,4},{4,5},{5,6},{6,7},{7,0},{8,9},{9,10},{10,1... | collective-permute-start | bytes 98312 | tf_op jit(solution)/shard_map/ppermute | solution.py:542
  258.1 5.1 %collective-permute-start.10 = (f32[32,128]{1,0:T(8,128)}, f32[32,128]{1,0:T(8,128)S(1)}, u32[]{:S(2)}, u32[]{:S(2)}) collective-permute-start(f32[32,128]{1,0:T(8,128)} %get-tuple-element.141), channel_id=1, source_target_pairs={{0,8},{8,16},{16,24},{24,32},{32,40},{40,48},{48,56},{56,64},{64,7... | collective-permute-start | bytes 49160 | tf_op jit(solution)/shard_map/ppermute | solution.py:542
  (44 other events, 90.9 us)

commit v2 on v1

v2 whole, which is shorter than its diff:
```python
import functools

import jax
import jax.numpy as jnp
from jax import lax
from jax.experimental import pallas as pl
from jax.experimental.pallas import tpu as pltpu
from jax.sharding import PartitionSpec as P

STEPS = 10
KAPPA = 0.16
F32 = jnp.float32
BF16 = jnp.bfloat16
I32 = jnp.int32
HI = lax.Precision.HIGHEST
LANES = 128
SLOTS = 16
TILE = 8
VMEM_LIMIT = 16 << 20


def iota(dims, dim):
    return lax.broadcasted_iota(I32, dims, dim)


def dot(a, b):
    return jnp.dot(a, b, precision=HI, preferred_element_type=F32)


def mul(a, b):
    return jnp.dot(a, b, preferred_element_type=F32)


def parts(x, count):
    found = []
    for _ in range(count):
        found.append(x.astype(BF16))
        x = x - found[-1].astype(F32)
    return found


def dot_t(a, b):
    return lax.dot_general(
        a, b, (((1,), (1,)), ((), ())), precision=HI, preferred_element_type=F32
    )


def pick(values, index):
    return jnp.take_along_axis(values, index, axis=1, mode="promise_in_bounds")


def spec(dims, dtype=F32):
    return jax.ShapeDtypeStruct(dims, dtype)


class Copies:
    def __init__(self, sems):
        self.sems, self.used = sems, 0

    def start(self, source, target):
        copy = pltpu.make_async_copy(source, target, self.sems.at[self.used])
        self.used += 1
        copy.start()
        return copy


def call(kernel, ins, outs, scratch, copies, held=(), held_out=(), flops=0, nbytes=0, aliases=None):
    return pl.pallas_call(
        kernel,
        out_shape=outs,
        in_specs=[
            pl.BlockSpec(memory_space=pltpu.VMEM if k in held else pltpu.HBM)
            for k in range(len(ins))
        ],
        out_specs=[
            pl.BlockSpec(memory_space=pltpu.VMEM if k in held_out else pltpu.HBM)
            for k in range(len(outs))
        ],
        scratch_shapes=[pltpu.VMEM(s.shape, s.dtype) for s in scratch]
        + [pltpu.SemaphoreType.DMA((copies,))],
        compiler_params=pltpu.CompilerParams(vmem_limit_bytes=VMEM_LIMIT),
        cost_estimate=pl.CostEstimate(flops=flops, bytes_accessed=nbytes, transcendentals=0),
        input_output_aliases=aliases or {},
    )(*ins)


def load_segments(copies, cond_hbm, cond):
    return [
        copies.start(cond_hbm.at[:, pl.ds(s * LANES, LANES)], cond.at[:, s, :])
        for s in range(cond.shape[1])
    ]


def source_kernel(
    owner_hbm, row_hbm, cond_hbm, pay_hbm, place_hbm, owner, row, cond, pay, place, sems
):
    copies = Copies(sems)
    first = [copies.start(owner_hbm, owner), copies.start(row_hbm, row)]
    later = load_segments(copies, cond_hbm, cond)
    for copy in first:
        copy.wait()
    segs = owner.shape[0] * LANES
    n_flow = pay.shape[0]
    slots = n_flow * SLOTS
    sub, lane = iota((segs, segs), 0), iota((segs, segs), 1)
    own_row = jnp.concatenate([owner[0:1, :], owner[1:2, :]], axis=1)
    wall_row = jnp.concatenate([row[0:1, :], row[1:2, :]], axis=1)

    def column(line):
        return jnp.sum(jnp.where(sub == lane, line, 0).astype(F32), axis=1, keepdims=True)

    own_col = column(own_row).astype(I32)
    same = own_col == own_row
    rank_row = jnp.sum((same & (sub < lane)).astype(F32), axis=0, keepdims=True).astype(I32)
    rank_col = jnp.sum((same & (lane < sub)).astype(F32), axis=1, keepdims=True).astype(I32)
    slot_row = own_row * SLOTS + rank_row
    slot_col = own_col * SLOTS + rank_col
    place[...] = (iota((segs, slots), 1) == slot_col).astype(F32).astype(BF16)
    out = copies.start(place, place_hbm)
    lanes = iota((segs, LANES), 1)
    value = jnp.where(lanes < SLOTS, column(wall_row).astype(I32), iota((segs, LANES), 0))
    value = jnp.where((lanes < 2 * SLOTS) & (lanes % SLOTS == rank_col), value, 0)
    held = (iota((n_flow, segs), 0) == own_row).astype(F32)
    meta = mul(held.astype(BF16), value.astype(F32).astype(BF16))
    for copy in later:
        copy.wait()
    cond_rows = cond[...].reshape(segs, LANES)
    chosen = (iota((slots, segs), 0) == slot_row).astype(F32).astype(BF16)
    moved = sum(mul(chosen, part) for part in parts(cond_rows, 3))
    total = dot_t(jnp.ones((TILE, LANES), F32), cond_rows)[0:1]
    sub8 = iota((TILE, LANES), 0)
    common = jnp.zeros((TILE, LANES), F32)
    slot_f = slot_row.astype(F32)
    for half in range(2):
        cols = slice(half * LANES, (half + 1) * LANES)
        common = jnp.where(sub8 == 1 + half, slot_f[:, cols], common)
        common = jnp.where(sub8 == 3 + half, total[:, cols], common)
    for p in range(n_flow):
        pay[p, 0:SLOTS, :] = moved[p * SLOTS : (p + 1) * SLOTS]
        pay[p, SLOTS : SLOTS + TILE, :] = jnp.where(sub8 == 0, meta[p : p + 1], common)
    back = copies.start(pay, pay_hbm)
    out.wait()
    back.wait()


def outer_kernel(solid_hbm, heat_hbm, solid, heat, cols_hbm, cols, sems):
    copies = Copies(sems)
    nz, nx, ny = heat.shape
    inner = pl.ds(8, nx)
    warm = copies.start(heat_hbm, heat)
    copies.start(solid_hbm, solid.at[pl.ds(1, nz), inner, :]).wait()
    lane = iota((nx, ny), 1)
    ends = jnp.where(lane < nz, 0, ny - 1)
    solid[0, inner, :] = jnp.zeros((nx, ny), F32)
    solid[nz + 1, inner, :] = jnp.zeros((nx, ny), F32)
    solid[pl.ds(1, nz), 7, :] = jnp.zeros((nz, ny), F32)
    solid[pl.ds(1, nz), 8 + nx, :] = jnp.zeros((nz, ny), F32)
    unroll = 4

    def some(i, found):
        for j in range(unroll):
            z = i * unroll + j
            found = jnp.where(lane % nz == z, pick(solid[z + 1, inner, :], ends), found)
        return found

    cols[...] = lax.fori_loop(0, nz // unroll, some, jnp.zeros((nx, ny), F32))
    back = copies.start(cols, cols_hbm)
    warm.wait()
    back.wait()


def owner_kernel(
    got_hbm, solid, const_hbm,
    hit, hit_t, reply, weight, swell, index, scan, msg_hbm,
    got, const, msg, edges, sems,
):
    copies = Copies(sems)
    for copy in [copies.start(got_hbm, got), copies.start(const_hbm, const)]:
        copy.wait()
    bottom = solid[1, pl.ds(8, hit.shape[0]), :]
    n_flow = got.shape[0]
    slots = n_flow * SLOTS
    block_rows = bottom.shape[0]
    meta = got[:, SLOTS, :]
    lane8, sub8 = iota((TILE, LANES), 1), iota((TILE, LANES), 0)
    mine = lane8 // SLOTS == sub8
    hits, caps = [], []
    n_grp = n_flow // TILE
    rows = iota((LANES, LANES), 0)
    cap8 = jnp.broadcast_to(const[0:1, :], (TILE, LANES))
    for g in range(n_grp):
        part = meta[g * TILE : (g + 1) * TILE]
        row = jnp.sum(jnp.where(mine, pick(part, lane8 % SLOTS), 0.0), axis=0, keepdims=True)
        seg = jnp.where(mine, pick(part, SLOTS + lane8 % SLOTS), 0.0)
        seg = jnp.sum(seg, axis=0, keepdims=True).astype(I32)
        seg8 = jnp.broadcast_to(seg, (TILE, LANES))
        index[4, g * TILE : (g + 1) * TILE, :] = seg8
        cap = pick(cap8, seg8 // 16)[0:1]
        hits.append((rows == row.astype(I32)).astype(F32))
        caps.append(jnp.transpose(jnp.broadcast_to(cap, (LANES, LANES))))
    all_hit = jnp.concatenate(hits, axis=1)
    own_hit = all_hit[0:block_rows]
    hit[...] = own_hit.astype(BF16)
    cond = got[:, 0:SLOTS, :].reshape(slots, LANES)
    sub_t, lane_t = iota((LANES, LANES), 0), iota((LANES, LANES), 1)
    after = sum(
        mul(part, (sub_t > lane_t).astype(F32).astype(BF16)) for part in parts(cond, 3)
    )
    decay = jnp.exp(-cond)
    own_rate = 1.0 - decay
    halves = parts(jnp.transpose(own_rate * jnp.exp(-after)), 2)
    for half in range(2):
        weight[half] = halves[half]
    write_shifts(bottom, weight, own_hit, msg)
    back = send_message(copies, solid, msg, edges, msg_hbm)
    hit_t[...] = jnp.transpose(all_hit).astype(BF16)
    own_caprate = own_rate * jnp.concatenate(caps, axis=0)
    ahead = sum(
        mul(part, (sub_t < lane_t).astype(F32).astype(BF16)) for part in parts(cond, 3)
    )
    halves = parts(own_caprate * jnp.exp(-ahead), 2)
    for half in range(2):
        reply[half] = halves[half]
    middle = jnp.sum(
        jnp.where(iota((slots, LANES), 1) < LANES // 2, cond, 0.0), axis=1, keepdims=True
    )
    swell[0] = own_rate * jnp.exp(ahead + cond - middle)
    swell[1] = jnp.exp(middle - ahead)
    swell[2] = own_caprate
    lane_f, sub_f = iota((n_flow, LANES), 1), iota((n_flow, LANES), 0)
    inlet = jnp.broadcast_to(const[1:2, :], (n_flow, LANES))
    for half in range(2):
        slot = got[:, SLOTS + 1 + half, :].astype(I32)
        index[half] = (sub_f % TILE) * SLOTS + slot % SLOTS
        index[2 + half] = slot // SLOTS
        gain = jnp.exp(-got[:, SLOTS + 3 + half, :])
        inner = lane_f % 16
        for step in range(4):
            width = 1 << step
            scan[step, half] = jnp.where(inner >= width, gain, 0.0)
            gain = gain * jnp.where(inner >= width, pltpu.roll(gain, width, 1), 1.0)
        scan[10, half] = jnp.where(inner == 0, 1.0, pltpu.roll(gain, 1, 1))
        scan[9, half] = gain
        for step in range(5):
            width = 1 << step
            scan[4 + step, half] = jnp.where(sub_f >= width, gain, 0.0)
            gain = gain * jnp.where(sub_f >= width, pltpu.roll(gain, width, 0), 1.0)
        scan[11, half] = pick(inlet, lane_f // 16 + 8 * half)
    for copy in back:
        copy.wait()


def write_shifts(bottom, weight, hit, msg):
    high, low = parts(bottom, 2)
    ends = mul(high, weight[0]) + (mul(high, weight[1]) + mul(low, weight[0]))
    ends = jnp.sum(ends * hit, axis=0, keepdims=True)
    sub8 = iota((TILE, LANES), 0)
    tile = jnp.zeros((TILE, LANES), F32)
    for g in range(ends.shape[1] // LANES):
        tile = jnp.where(sub8 == g, ends[:, g * LANES : (g + 1) * LANES], tile)
    for p in range(msg.shape[0]):
        msg[p, 0:TILE, :] = tile


def send_message(copies, solid, msg, edges, msg_hbm):
    n_flow, me = msg.shape[0], lax.axis_index("flow")
    nz, nx = edges.shape[1], solid.shape[1] - 16
    edges[0] = solid[pl.ds(1, nz), 8, :]
    edges[1] = solid[pl.ds(1, nz), 7 + nx, :]
    rows = pl.ds(TILE, nz)
    return [
        copies.start(edges.at[0], msg_hbm.at[lax.rem(me + n_flow - 1, n_flow), rows, :]),
        copies.start(edges.at[1], msg_hbm.at[lax.rem(me + 1, n_flow), rows, :]),
        copies.start(msg.at[:, pl.ds(0, TILE), :], msg_hbm.at[:, pl.ds(0, TILE), :]),
    ]


def take_message(copies, got_hbm, got, edges):
    n_flow, me = got.shape[0], lax.axis_index("flow")
    rows = pl.ds(TILE, edges.shape[1])
    return [
        copies.start(got_hbm.at[:, pl.ds(0, TILE), :], got),
        copies.start(got_hbm.at[lax.rem(me + n_flow - 1, n_flow), rows, :], edges.at[0]),
        copies.start(got_hbm.at[lax.rem(me + 1, n_flow), rows, :], edges.at[1]),
    ]


def add_outer_rows(solid, edges):
    n_flow, me = lax.axis_size("flow"), lax.axis_index("flow")
    nz, nx = edges.shape[1], solid.shape[1] - 16
    north = jnp.where(me > 0, KAPPA * edges[0], 0.0)
    south = jnp.where(me < n_flow - 1, KAPPA * edges[1], 0.0)
    layers = pl.ds(1, nz)
    solid[layers, 8, :] = solid[layers, 8, :] + north
    solid[layers, 7 + nx, :] = solid[layers, 7 + nx, :] + south
    return north, south


def march_kernel(solid, hit, hit_t, swell, sink, flux, sems):
    del sems
    slots = hit_t.shape[0]
    piece = slots // 4
    nx, ny = sink.shape
    bottom = solid[1, pl.ds(8, nx), :]
    padded = jnp.concatenate([bottom, jnp.zeros((LANES - nx, ny), F32)], axis=0)
    wide = jnp.concatenate(parts(padded, 3), axis=1)
    earlier = (iota((LANES, LANES), 0) < iota((LANES, LANES), 1)).astype(F32).astype(BF16)
    for i in range(4):
        rows = pl.ds(i * piece, piece)
        triple = mul(hit_t[rows, :], wide)
        temp = (triple[:, 0:ny] + triple[:, ny : 2 * ny]) + triple[:, 2 * ny :]
        high, low = parts(swell[0, rows, :] * temp, 2)
        before = swell[1, rows, :] * (mul(high, earlier) + mul(low, earlier))
        high, low = parts(swell[2, rows, :] * (temp - before), 2)
        flux[0, rows, :] = high
        flux[1, rows, :] = low
    sink[...] = mul(hit[...], flux[0]) + mul(hit[...], flux[1])


def conduct_kernel(
    old, heat, west_hbm, east_hbm, sink, solid, cols_hbm, west, east, cols, sems
):
    del old
    nz, nx, ny = heat.shape
    copies = Copies(sems)
    inner = pl.ds(8, nx)
    for copy in [
        copies.start(west_hbm, west), copies.start(east_hbm, east)
    ]:
        copy.wait()
    lot, n_span = lax.axis_index("span"), lax.axis_size("span")
    lane = iota((nx, ny), 1)
    border = (lane == 0) | (lane == ny - 1)
    ends = jnp.where(lane < nz, 0, ny - 1)
    halo = jnp.where((lane < nz) & (lot < n_span - 1), east[...], 0.0)
    halo = jnp.where((lane >= nz) & (lot > 0), west[...], halo)
    unroll = 4

    def some(i, state):
        found, low = state
        for j in range(unroll):
            z = i * unroll + j
            mid = solid[z + 1, inner, :]
            side = pick(halo, jnp.where(lane == 0, nz, 0) + z)
            right, left = pltpu.roll(mid, 1, 1), pltpu.roll(mid, ny - 1, 1)
            across = jnp.where(border, side + jnp.where(lane == 0, left, right), left + right)
            total = across + (solid[z + 1, pl.ds(7, nx), :] + solid[z + 1, pl.ds(9, nx), :])
            total = total + (low + solid[z + 2, inner, :])
            new = mid + KAPPA * (total - 6.0 * mid) + heat[z]
            solid[z + 1, inner, :] = new
            found = jnp.where(lane % nz == z, pick(new, ends), found)
            low = mid
        return found, low

    zero = jnp.zeros((nx, ny), F32)
    cols[...], _ = lax.fori_loop(0, nz // unroll, some, (zero, zero))
    back = copies.start(cols, cols_hbm)
    solid[1, inner, :] = solid[1, inner, :] - sink[...]
    back.wait()


def entering(got, index, scan):
    n_flow = got.shape[0]
    ends = [[], []]
    for g in range(n_flow // TILE):
        rows = slice(g * TILE, (g + 1) * TILE)
        lanes = [index[half, rows, :] for half in range(2)]
        origin = [index[2 + half, rows, :] for half in range(2)]
        acc = [jnp.zeros((TILE, LANES), F32) for _ in range(2)]
        for o in range(n_flow):
            line = jnp.broadcast_to(got[o, g : g + 1, :], (TILE, LANES))
            for half in range(2):
                acc[half] = jnp.where(origin[half] == o, pick(line, lanes[half]), acc[half])
        for half in range(2):
            ends[half].append(acc[half])
    result = []
    sub, lane = iota((n_flow, LANES), 0), iota((n_flow, LANES), 1)
    for half in range(2):
        x = jnp.concatenate(ends[half], axis=0)
        for step in range(4):
            x = x + scan[step, half] * pltpu.roll(x, 1 << step, 1)
        inlet = scan[11, half]
        y = jnp.where(sub == 0, x + scan[9, half] * inlet, x)
        for step in range(5):
            y = y + scan[4 + step, half] * pltpu.roll(y, 1 << step, 0)
        carry = jnp.where(sub == 0, inlet, pltpu.roll(y, 1, 0))
        carry = pick(carry, lane // 16 * 16 + 15)
        earlier = jnp.where(lane % 16 == 0, 0.0, pltpu.roll(x, 1, 1))
        result.append(earlier + scan[10, half] * carry)
    return result


def hosted(enter, index):
    lane8, sub8 = iota((TILE, LANES), 1), iota((TILE, LANES), 0)
    found = []
    for g in range(enter[0].shape[0] // TILE):
        rows = slice(g * TILE, (g + 1) * TILE)
        seg = index[4, rows, :]
        low, high = (pick(enter[half][rows], seg % LANES) for half in range(2))
        value = jnp.where(lane8 // SLOTS == sub8, jnp.where(seg < LANES, low, high), 0.0)
        found.append(jnp.sum(value, axis=0, keepdims=True))
    return jnp.concatenate(found, axis=1)


def new_bottom(carry, base, hit, reply):
    high, low = parts(carry, 2)
    high, low = hit * high, hit * low
    return base + (mul(high, reply[0]) + (mul(high, reply[1]) + mul(low, reply[0])))


def after_kernel(
    last,
    got_hbm, old, plain_hbm, index, scan, hit, reply, weight, hit_t,
    solid, msg_hbm, cols_hbm,
    got, edges, plain, msg, cols, sems,
):
    del old
    copies = Copies(sems)
    first, *then = take_message(copies, got_hbm, got, edges)
    then.append(copies.start(plain_hbm, plain))
    first.wait()
    carry = hosted(entering(got, index, scan), index)
    own_hit = hit[...]
    nx = own_hit.shape[0]
    inner = pl.ds(8, nx)
    for copy in then:
        copy.wait()
    north, south = add_outer_rows(solid, edges)
    new = new_bottom(carry, solid[1, inner, :], own_hit, reply)
    solid[1, inner, :] = new
    write_shifts(new, weight, own_hit.astype(F32), msg)
    back = send_message(copies, solid, msg, edges, msg_hbm)
    nx, ny = new.shape
    nz = edges.shape[1]
    if last:
        padded = jnp.concatenate([new, jnp.zeros((LANES - nx, ny), F32)], axis=0)
        temp = sum(mul(hit_t[...], part) for part in parts(padded, 3))
        for p in range(msg.shape[0]):
            msg[p, TILE : TILE + SLOTS, :] = temp[p * SLOTS : (p + 1) * SLOTS]
        rows = pl.ds(TILE + nz, SLOTS)
        back.append(copies.start(msg.at[:, pl.ds(TILE, SLOTS), :], msg_hbm.at[:, rows, :]))
    sub, lane = iota((nx, ny), 0), iota((nx, ny), 1)
    sub_z, lane_z = iota((nz, ny), 0), iota((nz, ny), 1)

    def ends_of(rows):
        both = jnp.where(lane_z < nz, rows[:, 0:1], rows[:, ny - 1 : ny])
        both = jnp.where((lane_z % nz == sub_z) & (lane_z < 2 * nz), both, 0.0)
        return jnp.sum(both, axis=0, keepdims=True)

    value = plain[...] + jnp.where(sub == 0, ends_of(north), 0.0)
    value = value + jnp.where(sub == nx - 1, ends_of(south), 0.0)
    cols[...] = jnp.where(lane % nz == 0, pick(new, jnp.where(lane < nz, 0, ny - 1)), value)
    back.append(copies.start(cols, cols_hbm))
    for copy in back:
        copy.wait()


def final_kernel(
    got_hbm, solid_hbm, place_hbm, cond_hbm, index, scan, hit, reply, out_hbm, coolant_hbm,
    got, edges, temps, place, cond, solid, coolant, sems,
):
    copies = Copies(sems)
    nz, nx = out_hbm.shape[0], out_hbm.shape[1]
    inner = pl.ds(8, nx)
    first, *then = take_message(copies, got_hbm, got, edges)
    whole = copies.start(solid_hbm, solid)
    rows = pl.ds(TILE + nz, SLOTS)
    then += [copies.start(got_hbm.at[:, rows, :], temps), copies.start(place_hbm, place)]
    then += load_segments(copies, cond_hbm, cond)
    first.wait()
    enter = entering(got, index, scan)
    carry = hosted(enter, index)
    for copy in [whole, *then]:
        copy.wait()
    add_outer_rows(solid, edges)
    solid[1, inner, :] = new_bottom(carry, solid[1, inner, :], hit[...], reply)
    back = [copies.start(solid.at[pl.ds(1, nz), inner, :], out_hbm)]
    n_flow = got.shape[0]
    stacked = temps[...].reshape(n_flow * SLOTS, LANES)
    temp = sum(mul(place[...], part) for part in parts(stacked, 3))
    segs = temp.shape[0]
    lane = iota((segs, LANES), 1)
    gain = jnp.exp(-cond[...].reshape(segs, LANES))
    shift = (1.0 - gain) * temp
    for step in range(7):
        width = 1 << step
        shift = shift + jnp.where(lane >= width, gain * pltpu.roll(shift, width, 1), 0.0)
        gain = gain * jnp.where(lane >= width, pltpu.roll(gain, width, 1), 1.0)
    own = iota((n_flow, LANES), 0) == lax.axis_index("flow")
    line = jnp.concatenate(
        [jnp.sum(jnp.where(own, part, 0.0), axis=0, keepdims=True) for part in enter], axis=1
    )
    same = iota((segs, segs), 0) == iota((segs, segs), 1)
    start = jnp.sum(jnp.where(same, line, 0.0), axis=1, keepdims=True)
    coolant[...] = (shift + gain * start).reshape(coolant.shape)
    for s in range(coolant.shape[1]):
        target = coolant_hbm.at[:, pl.ds(s * LANES, LANES)]
        back.append(copies.start(coolant.at[:, s, :], target))
    for copy in back:
        copy.wait()


def body(solid_start, heat_gen, conductance, heat_capacity, inlet_temp, wall_owner, wall_row):
    n_flow, n_span = lax.axis_size("flow"), lax.axis_size("span")
    nz, nx, ny = solid_start.shape
    channels, stations = conductance.shape
    segs = wall_owner.shape[0]
    slots = n_flow * SLOTS
    const = jnp.pad(
        jnp.stack([heat_capacity, inlet_temp]), ((0, TILE - 2), (0, LANES - channels))
    )

    def beside_span(cols):
        up = [(i, (i + 1) % n_span) for i in range(n_span)]
        down = [(i, (i - 1) % n_span) for i in range(n_span)]
        return lax.ppermute(cols, "span", up), lax.ppermute(cols, "span", down)

    def exchange(message):
        return lax.all_to_all(message, "flow", 0, 0, tiled=True)

    lines = spec((segs // LANES, LANES), I32)
    split = spec((channels, segs // channels, LANES))
    layer, edges_spec = spec((nx, ny)), spec((2, nz, ny))
    block = spec((nz, nx, ny))
    pay_spec, place_spec = spec((n_flow, SLOTS + TILE, LANES)), spec((segs, slots), BF16)
    pay, place = call(
        source_kernel,
        (wall_owner.reshape(lines.shape), wall_row.reshape(lines.shape), conductance),
        (pay_spec, place_spec),
        (lines, lines, split, pay_spec, place_spec),
        20,
    )
    got = exchange(pay)
    room = spec((nz + 2, nx + 16, ny))
    solid, heat, cols = call(
        outer_kernel, (solid_start, heat_gen), (room, block, layer), (layer,), 3, held_out=(0, 1)
    )
    hit_spec, hit_t_spec = spec((nx, slots), BF16), spec((slots, LANES), BF16)
    reply_spec, weight_spec = spec((2, slots, LANES), BF16), spec((2, LANES, slots), BF16)
    swell_spec = spec((3, slots, LANES))
    index_spec, scan_spec = spec((5, n_flow, LANES), I32), spec((12, 2, n_flow, LANES))
    msg_spec = spec((n_flow, TILE + nz, LANES))
    long_spec = spec((n_flow, TILE + nz + SLOTS, LANES))
    short_spec, temps_spec = spec((n_flow, TILE, LANES)), spec((n_flow, SLOTS, LANES))
    constants = (
        hit_spec, hit_t_spec, reply_spec, weight_spec, swell_spec, index_spec, scan_spec, msg_spec,
    )
    hit, hit_t, reply, weight, swell, index, scan, message = call(
        owner_kernel,
        (got, solid, const),
        constants,
        (pay_spec, spec((TILE, LANES)), short_spec, edges_spec),
        5,
        held=(1,),
        held_out=range(7),
    )

    def beside(solid, cols, message):
        got = exchange(message)
        west, east = beside_span(cols)
        (sink,) = call(
            march_kernel,
            (solid, hit, hit_t, swell),
            (layer,),
            (reply_spec,),
            1,
            held=range(4),
            held_out=(0,),
            flops=2_000_000,
            nbytes=3_000_000,
        )
        solid, cols = call(
            conduct_kernel,
            (solid, heat, west, east, sink),
            (room, layer),
            (layer, layer, layer),
            3,
            held=(0, 1, 4),
            held_out=(0,),
            flops=4_000_000,
            nbytes=6_000_000,
            aliases={0: 0},
        )
        return got, solid, cols

    def step(state, last=False):
        got, solid, cols = beside(*state)
        solid, message, cols = call(
            functools.partial(after_kernel, last),
            (got, solid, cols, index, scan, hit, reply, weight, hit_t),
            (room, long_spec if last else msg_spec, layer),
            (
                short_spec, edges_spec, layer,
                spec((n_flow, TILE + SLOTS, LANES)) if last else short_spec, layer,
            ),
            9,
            held=(1, *range(3, 9)),
            held_out=(0,),
            flops=4_000_000,
            nbytes=4_000_000,
            aliases={1: 0},
        )
        return solid, cols, message

    state = lax.fori_loop(0, STEPS - 2, lambda turn, now: step(now), (solid, cols, message))
    got, solid, _ = beside(*step(state, last=True))
    return call(
        final_kernel,
        (got, solid, place, conductance, index, scan, hit, reply),
        (block, spec((channels, stations))),
        (short_spec, edges_spec, temps_spec, place_spec, split, room, split),
        7 + 2 * split.shape[1],
        held=(4, 5, 6, 7),
    )


def solution(mesh):
    placed = (
        P(None, "flow", "span"),
        P(None, "flow", "span"),
        P("span", "flow"),
        P("span"),
        P("span"),
        P(("flow", "span"), None),
        P(("flow", "span"), None),
    )
    return jax.shard_map(
        body,
        mesh=mesh,
        in_specs=placed,
        out_specs=(P(None, "flow", "span"), P("span", "flow")),
        check_vma=False,
    )
```

time: 279 us -> 241 us (0.86)
  starting transfers between devices: 130 us -> 69.3 us
  waiting for transfers between devices: 13.2 us -> 70.3 us
  Pallas kernels: 114 us -> 92.7 us
  local copies, waits for them, and re-layouts: 15.5 us -> 4.75 us
    all_to_all x11, waiting for transfers between devices: 5.7 us -> 52.2 us  [exchange(): return lax.all_to_all(message, 'flow', 0, 0, tiled=True)]
    all_to_all x11, starting transfers between devices: 85 us -> 51.3 us  [exchange(): return lax.all_to_all(message, 'flow', 0, 0, tiled=True)]
    ppermute x40 -> x20, starting transfers between devices: 44.7 us -> 18 us  [beside_span(): return (lax.ppermute(cols, 'span', up), lax.ppermute(cols, 'span', down))]
    pallas_call x33, Pallas kernels: 114 us -> 92.7 us  [call(): pl.pallas_call(kernel, out_shape=outs, in_specs=[pl.BlockSpec(memory_spac...]
    ppermute x40 -> x20, waiting for transfers between devices: 7.5 us -> 18.1 us  [beside_span(): return (lax.ppermute(cols, 'span', up), lax.ppermute(cols, 'span', down))]
    while x48 -> x0, local copies, waits for them, and re-layouts: 10.1 us -> none
  transfers between devices with their start and end apart: 51 -> 31, of which waited for: 11 -> 20; matrix products, arithmetic and copies ran while one was open for 0% -> 0% of each run, Pallas kernels for 38% -> 21%
where the time goes in v2:
time: 241 us; the launch traced here: 239 us
  Pallas kernels  92.7 us (38%)
  waiting for transfers between devices  70.3 us (29%)
  starting transfers between devices  69.3 us (29%)
  local copies, waits for them, and re-layouts  4.75 us (2%)
    pallas_call x33, Pallas kernels, call(): pl.pallas_call(kernel, out_shape=outs, in_specs=[pl.BlockSpec(memory_spac...  92.7 us
    all_to_all x11, waiting for transfers between devices, exchange(): return lax.all_to_all(message, 'flow', 0, 0, tiled=True)  52.2 us
    all_to_all x11, starting transfers between devices, exchange(): return lax.all_to_all(message, 'flow', 0, 0, tiled=True)  51.3 us
    ppermute x20, waiting for transfers between devices, beside_span(): return (lax.ppermute(cols, 'span', up), lax.ppermute(cols, 'span', down))  18.1 us
    ppermute x20, starting transfers between devices, beside_span(): return (lax.ppermute(cols, 'span', up), lax.ppermute(cols, 'span', down))  18 us
  transfers between devices with their start and end apart: 31, of which 20 were waited for; matrix products, arithmetic and copies ran while one was open for 0% of the time, Pallas kernels for 21%

profile of v2, /device:TPU:97, one launch (start us, length us, event | category | flops | bytes accessed | tf_op | source)
XLA Modules:
  0.0 238.6 jit_solution(8486467703535963610)
XLA Ops:
  4.9 7.8 %all-to-all-start.1 = ((f32[32,24,128]{2,1,0:T(8,128)}), f32[32,24,128]{2,1,0:T(8,128)S(1)}, u32[]{:S(2)}, u32[]{:S(2)}) async-start(f32[32,24,128]{2,1,0:T(8,128)} %get-tuple-element.92), calls=%async_computation.1 | async-start | bytes 786432 | tf_op jit(solution)/shard_map/all_to_all | solution.py:519
  16.9 6.0 %all-to-all-done.1.got_hbm = f32[32,24,128]{2,1,0:T(8,128)S(1)} async-done(((f32[32,24,128]{2,1,0:T(8,128)}), f32[32,24,128]{2,1,0:T(8,128)S(1)}, u32[]{:S(2)}, u32[]{:S(2)}) %all-to-all-start.1) | async-done | bytes 393248 | tf_op jit(solution)/shard_map/all_to_all | solution.py:519
  22.9 3.4 %shard_map.88 = (bf16[64,512]{1,0:T(8,128)(2,1)S(1)}, bf16[512,128]{1,0:T(8,128)(2,1)}, bf16[2,512,128]{2,1,0:T(8,128)(2,1)}, bf16[2,128,512]{2,1,0:T(8,128)(2,1...) custom-call(f32[32,24,128]{2,1,0:T(8,128)S(1)} %all-to-all-done.1.got_h, ...), custom_call_target="tpu_custom_call" | custom-call | tf_op jit(solution)/shard_map/pallas_call | solution.py:68
  26.4 166.7 %while.14 = (s32[]{:T(128)}, f32[34,80,128]{2,1,0:T(8,128)S(1)}, f32[64,128]{1,0:T(8,128)}, f32[32,40,128]{2,1,0:T(8,128)}, bf16[64,512]{1,0:T(8,128)(2,1)S(1)},...) while((s32[]{:T(128)}, f32[34,80,128]{2,1,0:T(8,128)S(1)}, ...), condition=%wide.region_1.2_spmd, body=%wide.region_0.1_spmd.sunk | while | flops 10000002 | bytes 15228461 | solution.py:605
  26.4 3.9 %all-to-all-start = ((f32[32,40,128]{2,1,0:T(8,128)}), f32[32,40,128]{2,1,0:T(8,128)S(1)}, u32[]{:S(2)}, u32[]{:S(2)}) async-start(f32[32,40,128]{2,1,0:T(8,128)} %get-tuple-element.235), calls=%async_computation | async-start | bytes 1310720 | tf_op jit(solution)/shard_map/while/body/eval_jaxpr/all_to_all | solution.py:519
  30.3 2.9 %collective-permute-start = (f32[64,128]{1,0:T(8,128)}, f32[64,128]{1,0:T(8,128)S(1)}, u32[]{:S(2)}, u32[]{:S(2)}) collective-permute-start(f32[64,128]{1,0:T(8,128)} %get-tuple-element.234), channel_id=1, source_target_pairs={{0,1},{1,2},{2,3},{3,4},{4,5},{5,6},{6,7},{7,0},{8,9},{9,10},{10,1... | collective-permute-start | bytes 98312 | tf_op jit(solution)/shard_map/while/body/eval_jaxpr/ppermute | solution.py:516
  35.4 2.3 collective-permute-done.1.east_hbm
  37.7 2.7 %eval_jaxpr.4 = (f32[34,80,128]{2,1,0:T(8,128)S(1)}, f32[64,128]{1,0:T(8,128)S(1)}) custom-call(f32[34,80,128]{2,1,0:T(8,128)S(1)} %get-tuple-element.233.solid.old, f32[32,64,128]{2,1,0:T(8,128)S(1)} %get-tuple-element.252.heat, f32[64,128]{1,0:T(8,128)S(1)} %collective-permute-done.west_hbm, ...), custom_call_target="tpu_custom_call", output_to_operand_aliasing={{0}: (0, {})} | custom-call | flops 4000000 | bytes 6000000 | tf_op jit(solution)/shard_map/while/body/eval_jaxpr/pallas_call | solution.py:68
  40.5 2.9 %all-to-all-done.got_hbm = f32[32,40,128]{2,1,0:T(8,128)S(1)} async-done(((f32[32,40,128]{2,1,0:T(8,128)}), f32[32,40,128]{2,1,0:T(8,128)S(1)}, u32[]{:S(2)}, u32[]{:S(2)}) %all-to-all-start) | async-done | bytes 655392 | tf_op jit(solution)/shard_map/while/body/eval_jaxpr/all_to_all | solution.py:519
  43.3 3.5 %eval_jaxpr.5 = (f32[34,80,128]{2,1,0:T(8,128)S(1)}, f32[32,40,128]{2,1,0:T(8,128)}, f32[64,128]{1,0:T(8,128)}) custom-call(f32[32,40,128]{2,1,0:T(8,128)S(1)} %all-to-all-done.got_hbm, f32[34,80,128]{2,1,0:T(8,128)S(1)} %get-tuple-element.214.old, f32[64,128]{1,0:T(8,128)S(1)} %get-tuple-element.215.plain_hbm, ...), custom_call_target="tpu_custom_call", output_to_operand_aliasing={{0}: (1, {})} | custom-call | flops 4000000 | bytes 4000000 | tf_op jit(solution)/shard_map/while/body/eval_jaxpr/pallas_call | solution.py:68
  46.8 5.8 %all-to-all-start = ((f32[32,40,128]{2,1,0:T(8,128)}), f32[32,40,128]{2,1,0:T(8,128)S(1)}, u32[]{:S(2)}, u32[]{:S(2)}) async-start(f32[32,40,128]{2,1,0:T(8,128)} %get-tuple-element.235), calls=%async_computation | async-start | bytes 1310720 | tf_op jit(solution)/shard_map/while/body/eval_jaxpr/all_to_all | solution.py:519
  58.4 2.7 %eval_jaxpr.4 = (f32[34,80,128]{2,1,0:T(8,128)S(1)}, f32[64,128]{1,0:T(8,128)S(1)}) custom-call(f32[34,80,128]{2,1,0:T(8,128)S(1)} %get-tuple-element.233.solid.old, f32[32,64,128]{2,1,0:T(8,128)S(1)} %get-tuple-element.252.heat, f32[64,128]{1,0:T(8,128)S(1)} %collective-permute-done.west_hbm, ...), custom_call_target="tpu_custom_call", output_to_operand_aliasing={{0}: (0, {})} | custom-call | flops 4000000 | bytes 6000000 | tf_op jit(solution)/shard_map/while/body/eval_jaxpr/pallas_call | solution.py:68
  61.1 4.4 %all-to-all-done.got_hbm = f32[32,40,128]{2,1,0:T(8,128)S(1)} async-done(((f32[32,40,128]{2,1,0:T(8,128)}), f32[32,40,128]{2,1,0:T(8,128)S(1)}, u32[]{:S(2)}, u32[]{:S(2)}) %all-to-all-start) | async-done | bytes 655392 | tf_op jit(solution)/shard_map/while/body/eval_jaxpr/all_to_all | solution.py:519
  65.6 3.5 %eval_jaxpr.5 = (f32[34,80,128]{2,1,0:T(8,128)S(1)}, f32[32,40,128]{2,1,0:T(8,128)}, f32[64,128]{1,0:T(8,128)}) custom-call(f32[32,40,128]{2,1,0:T(8,128)S(1)} %all-to-all-done.got_hbm, f32[34,80,128]{2,1,0:T(8,128)S(1)} %get-tuple-element.214.old, f32[64,128]{1,0:T(8,128)S(1)} %get-tuple-element.215.plain_hbm, ...), custom_call_target="tpu_custom_call", output_to_operand_aliasing={{0}: (1, {})} | custom-call | flops 4000000 | bytes 4000000 | tf_op jit(solution)/shard_map/while/body/eval_jaxpr/pallas_call | solution.py:68
  69.1 4.2 %all-to-all-start = ((f32[32,40,128]{2,1,0:T(8,128)}), f32[32,40,128]{2,1,0:T(8,128)S(1)}, u32[]{:S(2)}, u32[]{:S(2)}) async-start(f32[32,40,128]{2,1,0:T(8,128)} %get-tuple-element.235), calls=%async_computation | async-start | bytes 1310720 | tf_op jit(solution)/shard_map/while/body/eval_jaxpr/all_to_all | solution.py:519
  79.0 2.7 %eval_jaxpr.4 = (f32[34,80,128]{2,1,0:T(8,128)S(1)}, f32[64,128]{1,0:T(8,128)S(1)}) custom-call(f32[34,80,128]{2,1,0:T(8,128)S(1)} %get-tuple-element.233.solid.old, f32[32,64,128]{2,1,0:T(8,128)S(1)} %get-tuple-element.252.heat, f32[64,128]{1,0:T(8,128)S(1)} %collective-permute-done.west_hbm, ...), custom_call_target="tpu_custom_call", output_to_operand_aliasing={{0}: (0, {})} | custom-call | flops 4000000 | bytes 6000000 | tf_op jit(solution)/shard_map/while/body/eval_jaxpr/pallas_call | solution.py:68
  81.8 4.4 %all-to-all-done.got_hbm = f32[32,40,128]{2,1,0:T(8,128)S(1)} async-done(((f32[32,40,128]{2,1,0:T(8,128)}), f32[32,40,128]{2,1,0:T(8,128)S(1)}, u32[]{:S(2)}, u32[]{:S(2)}) %all-to-all-start) | async-done | bytes 655392 | tf_op jit(solution)/shard_map/while/body/eval_jaxpr/all_to_all | solution.py:519
  86.2 3.5 %eval_jaxpr.5 = (f32[34,80,128]{2,1,0:T(8,128)S(1)}, f32[32,40,128]{2,1,0:T(8,128)}, f32[64,128]{1,0:T(8,128)}) custom-call(f32[32,40,128]{2,1,0:T(8,128)S(1)} %all-to-all-done.got_hbm, f32[34,80,128]{2,1,0:T(8,128)S(1)} %get-tuple-element.214.old, f32[64,128]{1,0:T(8,128)S(1)} %get-tuple-element.215.plain_hbm, ...), custom_call_target="tpu_custom_call", output_to_operand_aliasing={{0}: (1, {})} | custom-call | flops 4000000 | bytes 4000000 | tf_op jit(solution)/shard_map/while/body/eval_jaxpr/pallas_call | solution.py:68
  89.7 4.2 %all-to-all-start = ((f32[32,40,128]{2,1,0:T(8,128)}), f32[32,40,128]{2,1,0:T(8,128)S(1)}, u32[]{:S(2)}, u32[]{:S(2)}) async-start(f32[32,40,128]{2,1,0:T(8,128)} %get-tuple-element.235), calls=%async_computation | async-start | bytes 1310720 | tf_op jit(solution)/shard_map/while/body/eval_jaxpr/all_to_all | solution.py:519
  95.5 2.2 eval_jaxpr.3.sink
  99.7 2.7 %eval_jaxpr.4 = (f32[34,80,128]{2,1,0:T(8,128)S(1)}, f32[64,128]{1,0:T(8,128)S(1)}) custom-call(f32[34,80,128]{2,1,0:T(8,128)S(1)} %get-tuple-element.233.solid.old, f32[32,64,128]{2,1,0:T(8,128)S(1)} %get-tuple-element.252.heat, f32[64,128]{1,0:T(8,128)S(1)} %collective-permute-done.west_hbm, ...), custom_call_target="tpu_custom_call", output_to_operand_aliasing={{0}: (0, {})} | custom-call | flops 4000000 | bytes 6000000 | tf_op jit(solution)/shard_map/while/body/eval_jaxpr/pallas_call | solution.py:68
  102.4 4.4 %all-to-all-done.got_hbm = f32[32,40,128]{2,1,0:T(8,128)S(1)} async-done(((f32[32,40,128]{2,1,0:T(8,128)}), f32[32,40,128]{2,1,0:T(8,128)S(1)}, u32[]{:S(2)}, u32[]{:S(2)}) %all-to-all-start) | async-done | bytes 655392 | tf_op jit(solution)/shard_map/while/body/eval_jaxpr/all_to_all | solution.py:519
  106.9 3.5 %eval_jaxpr.5 = (f32[34,80,128]{2,1,0:T(8,128)S(1)}, f32[32,40,128]{2,1,0:T(8,128)}, f32[64,128]{1,0:T(8,128)}) custom-call(f32[32,40,128]{2,1,0:T(8,128)S(1)} %all-to-all-done.got_hbm, f32[34,80,128]{2,1,0:T(8,128)S(1)} %get-tuple-element.214.old, f32[64,128]{1,0:T(8,128)S(1)} %get-tuple-element.215.plain_hbm, ...), custom_call_target="tpu_custom_call", output_to_operand_aliasing={{0}: (1, {})} | custom-call | flops 4000000 | bytes 4000000 | tf_op jit(solution)/shard_map/while/body/eval_jaxpr/pallas_call | solution.py:68
  110.4 4.2 %all-to-all-start = ((f32[32,40,128]{2,1,0:T(8,128)}), f32[32,40,128]{2,1,0:T(8,128)S(1)}, u32[]{:S(2)}, u32[]{:S(2)}) async-start(f32[32,40,128]{2,1,0:T(8,128)} %get-tuple-element.235), calls=%async_computation | async-start | bytes 1310720 | tf_op jit(solution)/shard_map/while/body/eval_jaxpr/all_to_all | solution.py:519
  120.4 2.7 %eval_jaxpr.4 = (f32[34,80,128]{2,1,0:T(8,128)S(1)}, f32[64,128]{1,0:T(8,128)S(1)}) custom-call(f32[34,80,128]{2,1,0:T(8,128)S(1)} %get-tuple-element.233.solid.old, f32[32,64,128]{2,1,0:T(8,128)S(1)} %get-tuple-element.252.heat, f32[64,128]{1,0:T(8,128)S(1)} %collective-permute-done.west_hbm, ...), custom_call_target="tpu_custom_call", output_to_operand_aliasing={{0}: (0, {})} | custom-call | flops 4000000 | bytes 6000000 | tf_op jit(solution)/shard_map/while/body/eval_jaxpr/pallas_call | solution.py:68
  123.1 4.4 %all-to-all-done.got_hbm = f32[32,40,128]{2,1,0:T(8,128)S(1)} async-done(((f32[32,40,128]{2,1,0:T(8,128)}), f32[32,40,128]{2,1,0:T(8,128)S(1)}, u32[]{:S(2)}, u32[]{:S(2)}) %all-to-all-start) | async-done | bytes 655392 | tf_op jit(solution)/shard_map/while/body/eval_jaxpr/all_to_all | solution.py:519
  127.6 3.5 %eval_jaxpr.5 = (f32[34,80,128]{2,1,0:T(8,128)S(1)}, f32[32,40,128]{2,1,0:T(8,128)}, f32[64,128]{1,0:T(8,128)}) custom-call(f32[32,40,128]{2,1,0:T(8,128)S(1)} %all-to-all-done.got_hbm, f32[34,80,128]{2,1,0:T(8,128)S(1)} %get-tuple-element.214.old, f32[64,128]{1,0:T(8,128)S(1)} %get-tuple-element.215.plain_hbm, ...), custom_call_target="tpu_custom_call", output_to_operand_aliasing={{0}: (1, {})} | custom-call | flops 4000000 | bytes 4000000 | tf_op jit(solution)/shard_map/while/body/eval_jaxpr/pallas_call | solution.py:68
  131.1 4.2 %all-to-all-start = ((f32[32,40,128]{2,1,0:T(8,128)}), f32[32,40,128]{2,1,0:T(8,128)S(1)}, u32[]{:S(2)}, u32[]{:S(2)}) async-start(f32[32,40,128]{2,1,0:T(8,128)} %get-tuple-element.235), calls=%async_computation | async-start | bytes 1310720 | tf_op jit(solution)/shard_map/while/body/eval_jaxpr/all_to_all | solution.py:519
  141.0 2.7 %eval_jaxpr.4 = (f32[34,80,128]{2,1,0:T(8,128)S(1)}, f32[64,128]{1,0:T(8,128)S(1)}) custom-call(f32[34,80,128]{2,1,0:T(8,128)S(1)} %get-tuple-element.233.solid.old, f32[32,64,128]{2,1,0:T(8,128)S(1)} %get-tuple-element.252.heat, f32[64,128]{1,0:T(8,128)S(1)} %collective-permute-done.west_hbm, ...), custom_call_target="tpu_custom_call", output_to_operand_aliasing={{0}: (0, {})} | custom-call | flops 4000000 | bytes 6000000 | tf_op jit(solution)/shard_map/while/body/eval_jaxpr/pallas_call | solution.py:68
  143.8 4.4 %all-to-all-done.got_hbm = f32[32,40,128]{2,1,0:T(8,128)S(1)} async-done(((f32[32,40,128]{2,1,0:T(8,128)}), f32[32,40,128]{2,1,0:T(8,128)S(1)}, u32[]{:S(2)}, u32[]{:S(2)}) %all-to-all-start) | async-done | bytes 655392 | tf_op jit(solution)/shard_map/while/body/eval_jaxpr/all_to_all | solution.py:519
  148.2 3.5 %eval_jaxpr.5 = (f32[34,80,128]{2,1,0:T(8,128)S(1)}, f32[32,40,128]{2,1,0:T(8,128)}, f32[64,128]{1,0:T(8,128)}) custom-call(f32[32,40,128]{2,1,0:T(8,128)S(1)} %all-to-all-done.got_hbm, f32[34,80,128]{2,1,0:T(8,128)S(1)} %get-tuple-element.214.old, f32[64,128]{1,0:T(8,128)S(1)} %get-tuple-element.215.plain_hbm, ...), custom_call_target="tpu_custom_call", output_to_operand_aliasing={{0}: (1, {})} | custom-call | flops 4000000 | bytes 4000000 | tf_op jit(solution)/shard_map/while/body/eval_jaxpr/pallas_call | solution.py:68
  151.7 4.2 %all-to-all-start = ((f32[32,40,128]{2,1,0:T(8,128)}), f32[32,40,128]{2,1,0:T(8,128)S(1)}, u32[]{:S(2)}, u32[]{:S(2)}) async-start(f32[32,40,128]{2,1,0:T(8,128)} %get-tuple-element.235), calls=%async_computation | async-start | bytes 1310720 | tf_op jit(solution)/shard_map/while/body/eval_jaxpr/all_to_all | solution.py:519
  161.7 2.7 %eval_jaxpr.4 = (f32[34,80,128]{2,1,0:T(8,128)S(1)}, f32[64,128]{1,0:T(8,128)S(1)}) custom-call(f32[34,80,128]{2,1,0:T(8,128)S(1)} %get-tuple-element.233.solid.old, f32[32,64,128]{2,1,0:T(8,128)S(1)} %get-tuple-element.252.heat, f32[64,128]{1,0:T(8,128)S(1)} %collective-permute-done.west_hbm, ...), custom_call_target="tpu_custom_call", output_to_operand_aliasing={{0}: (0, {})} | custom-call | flops 4000000 | bytes 6000000 | tf_op jit(solution)/shard_map/while/body/eval_jaxpr/pallas_call | solution.py:68
  164.4 4.4 %all-to-all-done.got_hbm = f32[32,40,128]{2,1,0:T(8,128)S(1)} async-done(((f32[32,40,128]{2,1,0:T(8,128)}), f32[32,40,128]{2,1,0:T(8,128)S(1)}, u32[]{:S(2)}, u32[]{:S(2)}) %all-to-all-start) | async-done | bytes 655392 | tf_op jit(solution)/shard_map/while/body/eval_jaxpr/all_to_all | solution.py:519
  168.9 3.5 %eval_jaxpr.5 = (f32[34,80,128]{2,1,0:T(8,128)S(1)}, f32[32,40,128]{2,1,0:T(8,128)}, f32[64,128]{1,0:T(8,128)}) custom-call(f32[32,40,128]{2,1,0:T(8,128)S(1)} %all-to-all-done.got_hbm, f32[34,80,128]{2,1,0:T(8,128)S(1)} %get-tuple-element.214.old, f32[64,128]{1,0:T(8,128)S(1)} %get-tuple-element.215.plain_hbm, ...), custom_call_target="tpu_custom_call", output_to_operand_aliasing={{0}: (1, {})} | custom-call | flops 4000000 | bytes 4000000 | tf_op jit(solution)/shard_map/while/body/eval_jaxpr/pallas_call | solution.py:68
  172.4 4.2 %all-to-all-start = ((f32[32,40,128]{2,1,0:T(8,128)}), f32[32,40,128]{2,1,0:T(8,128)S(1)}, u32[]{:S(2)}, u32[]{:S(2)}) async-start(f32[32,40,128]{2,1,0:T(8,128)} %get-tuple-element.235), calls=%async_computation | async-start | bytes 1310720 | tf_op jit(solution)/shard_map/while/body/eval_jaxpr/all_to_all | solution.py:519
  182.4 2.7 %eval_jaxpr.4 = (f32[34,80,128]{2,1,0:T(8,128)S(1)}, f32[64,128]{1,0:T(8,128)S(1)}) custom-call(f32[34,80,128]{2,1,0:T(8,128)S(1)} %get-tuple-element.233.solid.old, f32[32,64,128]{2,1,0:T(8,128)S(1)} %get-tuple-element.252.heat, f32[64,128]{1,0:T(8,128)S(1)} %collective-permute-done.west_hbm, ...), custom_call_target="tpu_custom_call", output_to_operand_aliasing={{0}: (0, {})} | custom-call | flops 4000000 | bytes 6000000 | tf_op jit(solution)/shard_map/while/body/eval_jaxpr/pallas_call | solution.py:68
  185.1 4.4 %all-to-all-done.got_hbm = f32[32,40,128]{2,1,0:T(8,128)S(1)} async-done(((f32[32,40,128]{2,1,0:T(8,128)}), f32[32,40,128]{2,1,0:T(8,128)S(1)}, u32[]{:S(2)}, u32[]{:S(2)}) %all-to-all-start) | async-done | bytes 655392 | tf_op jit(solution)/shard_map/while/body/eval_jaxpr/all_to_all | solution.py:519
  189.5 3.5 %eval_jaxpr.5 = (f32[34,80,128]{2,1,0:T(8,128)S(1)}, f32[32,40,128]{2,1,0:T(8,128)}, f32[64,128]{1,0:T(8,128)}) custom-call(f32[32,40,128]{2,1,0:T(8,128)S(1)} %all-to-all-done.got_hbm, f32[34,80,128]{2,1,0:T(8,128)S(1)} %get-tuple-element.214.old, f32[64,128]{1,0:T(8,128)S(1)} %get-tuple-element.215.plain_hbm, ...), custom_call_target="tpu_custom_call", output_to_operand_aliasing={{0}: (1, {})} | custom-call | flops 4000000 | bytes 4000000 | tf_op jit(solution)/shard_map/while/body/eval_jaxpr/pallas_call | solution.py:68
  193.1 4.2 %all-to-all-start.2 = ((f32[32,40,128]{2,1,0:T(8,128)}), f32[32,40,128]{2,1,0:T(8,128)S(1)}, u32[]{:S(2)}, u32[]{:S(2)}) async-start(f32[32,40,128]{2,1,0:T(8,128)} %get-tuple-element.102), calls=%async_computation.2 | async-start | bytes 1310720 | tf_op jit(solution)/shard_map/all_to_all | solution.py:519
  203.0 2.7 %shard_map.90 = (f32[34,80,128]{2,1,0:T(8,128)S(1)}, f32[64,128]{1,0:T(8,128)S(1)}) custom-call(f32[34,80,128]{2,1,0:T(8,128)S(1)} %get-tuple-element.103.solid.old, f32[32,64,128]{2,1,0:T(8,128)S(1)} %get-tuple-element.270, f32[64,128]{1,0:T(8,128)S(1)} %collective-permute-done.2.west_hbm, ...), custom_call_target="tpu_custom_call", output_to_operand_aliasing={{0}: (0, {})} | custom-call | flops 4000000 | bytes 6000000 | tf_op jit(solution)/shard_map/pallas_call | solution.py:68
  205.8 4.4 %all-to-all-done.2.got_hbm = f32[32,40,128]{2,1,0:T(8,128)S(1)} async-done(((f32[32,40,128]{2,1,0:T(8,128)}), f32[32,40,128]{2,1,0:T(8,128)S(1)}, u32[]{:S(2)}, u32[]{:S(2)}) %all-to-all-start.2) | async-done | bytes 655392 | tf_op jit(solution)/shard_map/all_to_all | solution.py:519
  210.2 3.6 %shard_map.91 = (f32[34,80,128]{2,1,0:T(8,128)S(1)}, f32[32,56,128]{2,1,0:T(8,128)}, f32[64,128]{1,0:T(8,128)S(1)}) custom-call(f32[32,40,128]{2,1,0:T(8,128)S(1)} %all-to-all-done.2.got_hbm, f32[34,80,128]{2,1,0:T(8,128)S(1)} %get-tuple-element.105.old, f32[64,128]{1,0:T(8,128)S(1)} %get-tuple-element.106.plain_hbm, ...), custom_call_target="tpu_custom_call", output_to_operand_aliasing={{0}: (1, {})} | custom-call | flops 4000000 | bytes 4000000 | tf_op jit(solution)/shard_map/pallas_call | solution.py:68
  213.9 4.4 %all-to-all-start.3 = ((f32[32,56,128]{2,1,0:T(8,128)}), f32[32,56,128]{2,1,0:T(8,128)S(1)}, u32[]{:S(2)}, u32[]{:S(2)}) async-start(f32[32,56,128]{2,1,0:T(8,128)} %get-tuple-element.107), calls=%async_computation.3 | async-start | bytes 1835008 | tf_op jit(solution)/shard_map/all_to_all | solution.py:519
  218.3 2.7 %collective-permute-start.4 = (f32[64,128]{1,0:T(8,128)S(1)}, f32[64,128]{1,0:T(8,128)S(1)}, u32[]{:S(2)}, u32[]{:S(2)}) collective-permute-start(f32[64,128]{1,0:T(8,128)S(1)} %get-tuple-element.109), channel_id=1, source_target_pairs={{0,1},{1,2},{2,3},{3,4},{4,5},{5,6},{6,7},{7,0},{8,9},{9,10},{10,1... | collective-permute-start | bytes 98312 | tf_op jit(solution)/shard_map/ppermute | solution.py:516
  223.0 3.4 %shard_map.93 = (f32[34,80,128]{2,1,0:T(8,128)S(1)}, f32[64,128]{1,0:T(8,128)}) custom-call(f32[34,80,128]{2,1,0:T(8,128)S(1)} %get-tuple-element.108.solid.old, f32[32,64,128]{2,1,0:T(8,128)S(1)} %copy-done.7, f32[64,128]{1,0:T(8,128)S(1)} %collective-permute-done.4.west_hbm, ...), custom_call_target="tpu_custom_call", output_to_operand_aliasing={{0}: (0, {})} | custom-call | flops 4000000 | bytes 6000000 | tf_op jit(solution)/shard_map/pallas_call | solution.py:68
  226.3 7.7 %all-to-all-done.3.got_hbm = f32[32,56,128]{2,1,0:T(8,128)S(1)} async-done(((f32[32,56,128]{2,1,0:T(8,128)}), f32[32,56,128]{2,1,0:T(8,128)S(1)}, u32[]{:S(2)}, u32[]{:S(2)}) %all-to-all-start.3) | async-done | bytes 917536 | tf_op jit(solution)/shard_map/all_to_all | solution.py:519
  234.0 4.4 %shard_map.94 = (f32[32,64,128]{2,1,0:T(8,128)}, f32[16,2048]{1,0:T(8,128)}) custom-call(f32[32,56,128]{2,1,0:T(8,128)S(1)} %all-to-all-done.3.got_hbm, f32[34,80,128]{2,1,0:T(8,128)S(1)} %get-tuple-element.110.solid_hbm, bf16[256,512]{1,0:T(8,128)(2,1)S(1)} %get-tuple-element.111.place_hbm, f32[16,2048]{1,0:T(8,128)S(1)} %copy-done.3, ...), custom_call_target="tpu_custom_call" | custom-call | tf_op jit(solution)/shard_map/pallas_call | solution.py:68
  (77 shorter events, 56.0 us)
Async XLA Ops:
  0.6 0.9 copy-start.2
  1.5 0.7 copy-start.4
  2.2 0.7 copy-start.5
  4.9 11.9 %copy-start.12 = (f32[16]{0:T(128)S(1)}, f32[16]{0:T(128)}, u32[]{:S(2)}) copy-start(f32[16]{0:T(128)} %param.13) | copy-start | bytes 196
  4.9 11.9 %copy-start.13 = (f32[16]{0:T(128)S(1)}, f32[16]{0:T(128)}, u32[]{:S(2)}) copy-start(f32[16]{0:T(128)} %param.12) | copy-start | bytes 196
  4.9 18.0 %all-to-all-start.1 = ((f32[32,24,128]{2,1,0:T(8,128)}), f32[32,24,128]{2,1,0:T(8,128)S(1)}, u32[]{:S(2)}, u32[]{:S(2)}) async-start(f32[32,24,128]{2,1,0:T(8,128)} %get-tuple-element.92), calls=%async_computation.1 | async-start | bytes 786432 | tf_op jit(solution)/shard_map/all_to_all | solution.py:519
  12.7 1.2 copy-start
  14.0 1.2 copy-start.1
  26.4 16.9 %all-to-all-start = ((f32[32,40,128]{2,1,0:T(8,128)}), f32[32,40,128]{2,1,0:T(8,128)S(1)}, u32[]{:S(2)}, u32[]{:S(2)}) async-start(f32[32,40,128]{2,1,0:T(8,128)} %get-tuple-element.235), calls=%async_computation | async-start | bytes 1310720 | tf_op jit(solution)/shard_map/while/body/eval_jaxpr/all_to_all | solution.py:519
  30.3 5.1 %collective-permute-start = (f32[64,128]{1,0:T(8,128)}, f32[64,128]{1,0:T(8,128)S(1)}, u32[]{:S(2)}, u32[]{:S(2)}) collective-permute-start(f32[64,128]{1,0:T(8,128)} %get-tuple-element.234), channel_id=1, source_target_pairs={{0,1},{1,2},{2,3},{3,4},{4,5},{5,6},{6,7},{7,0},{8,9},{9,10},{10,1... | collective-permute-start | bytes 98312 | tf_op jit(solution)/shard_map/while/body/eval_jaxpr/ppermute | solution.py:516
  33.2 4.5 %collective-permute-start.1 = (f32[64,128]{1,0:T(8,128)}, f32[64,128]{1,0:T(8,128)S(1)}, u32[]{:S(2)}, u32[]{:S(2)}) collective-permute-start(f32[64,128]{1,0:T(8,128)} %get-tuple-element.234), channel_id=1, source_target_pairs={{0,7},{1,0},{2,1},{3,2},{4,3},{5,4},{6,5},{7,6},{8,15},{9,8},{10,9... | collective-permute-start | bytes 98312 | tf_op jit(solution)/shard_map/while/body/eval_jaxpr/ppermute | solution.py:516
  46.8 18.7 %all-to-all-start = ((f32[32,40,128]{2,1,0:T(8,128)}), f32[32,40,128]{2,1,0:T(8,128)S(1)}, u32[]{:S(2)}, u32[]{:S(2)}) async-start(f32[32,40,128]{2,1,0:T(8,128)} %get-tuple-element.235), calls=%async_computation | async-start | bytes 1310720 | tf_op jit(solution)/shard_map/while/body/eval_jaxpr/all_to_all | solution.py:519
  52.6 3.7 %collective-permute-start = (f32[64,128]{1,0:T(8,128)}, f32[64,128]{1,0:T(8,128)S(1)}, u32[]{:S(2)}, u32[]{:S(2)}) collective-permute-start(f32[64,128]{1,0:T(8,128)} %get-tuple-element.234), channel_id=1, source_target_pairs={{0,1},{1,2},{2,3},{3,4},{4,5},{5,6},{6,7},{7,0},{8,9},{9,10},{10,1... | collective-permute-start | bytes 98312 | tf_op jit(solution)/shard_map/while/body/eval_jaxpr/ppermute | solution.py:516
  53.9 4.5 %collective-permute-start.1 = (f32[64,128]{1,0:T(8,128)}, f32[64,128]{1,0:T(8,128)S(1)}, u32[]{:S(2)}, u32[]{:S(2)}) collective-permute-start(f32[64,128]{1,0:T(8,128)} %get-tuple-element.234), channel_id=1, source_target_pairs={{0,7},{1,0},{2,1},{3,2},{4,3},{5,4},{6,5},{7,6},{8,15},{9,8},{10,9... | collective-permute-start | bytes 98312 | tf_op jit(solution)/shard_map/while/body/eval_jaxpr/ppermute | solution.py:516
  69.1 17.1 %all-to-all-start = ((f32[32,40,128]{2,1,0:T(8,128)}), f32[32,40,128]{2,1,0:T(8,128)S(1)}, u32[]{:S(2)}, u32[]{:S(2)}) async-start(f32[32,40,128]{2,1,0:T(8,128)} %get-tuple-element.235), calls=%async_computation | async-start | bytes 1310720 | tf_op jit(solution)/shard_map/while/body/eval_jaxpr/all_to_all | solution.py:519
  73.3 3.7 %collective-permute-start = (f32[64,128]{1,0:T(8,128)}, f32[64,128]{1,0:T(8,128)S(1)}, u32[]{:S(2)}, u32[]{:S(2)}) collective-permute-start(f32[64,128]{1,0:T(8,128)} %get-tuple-element.234), channel_id=1, source_target_pairs={{0,1},{1,2},{2,3},{3,4},{4,5},{5,6},{6,7},{7,0},{8,9},{9,10},{10,1... | collective-permute-start | bytes 98312 | tf_op jit(solution)/shard_map/while/body/eval_jaxpr/ppermute | solution.py:516
  74.6 4.5 %collective-permute-start.1 = (f32[64,128]{1,0:T(8,128)}, f32[64,128]{1,0:T(8,128)S(1)}, u32[]{:S(2)}, u32[]{:S(2)}) collective-permute-start(f32[64,128]{1,0:T(8,128)} %get-tuple-element.234), channel_id=1, source_target_pairs={{0,7},{1,0},{2,1},{3,2},{4,3},{5,4},{6,5},{7,6},{8,15},{9,8},{10,9... | collective-permute-start | bytes 98312 | tf_op jit(solution)/shard_map/while/body/eval_jaxpr/ppermute | solution.py:516
  89.7 17.1 %all-to-all-start = ((f32[32,40,128]{2,1,0:T(8,128)}), f32[32,40,128]{2,1,0:T(8,128)S(1)}, u32[]{:S(2)}, u32[]{:S(2)}) async-start(f32[32,40,128]{2,1,0:T(8,128)} %get-tuple-element.235), calls=%async_computation | async-start | bytes 1310720 | tf_op jit(solution)/shard_map/while/body/eval_jaxpr/all_to_all | solution.py:519
  94.0 3.7 %collective-permute-start = (f32[64,128]{1,0:T(8,128)}, f32[64,128]{1,0:T(8,128)S(1)}, u32[]{:S(2)}, u32[]{:S(2)}) collective-permute-start(f32[64,128]{1,0:T(8,128)} %get-tuple-element.234), channel_id=1, source_target_pairs={{0,1},{1,2},{2,3},{3,4},{4,5},{5,6},{6,7},{7,0},{8,9},{9,10},{10,1... | collective-permute-start | bytes 98312 | tf_op jit(solution)/shard_map/while/body/eval_jaxpr/ppermute | solution.py:516
  95.2 4.5 %collective-permute-start.1 = (f32[64,128]{1,0:T(8,128)}, f32[64,128]{1,0:T(8,128)S(1)}, u32[]{:S(2)}, u32[]{:S(2)}) collective-permute-start(f32[64,128]{1,0:T(8,128)} %get-tuple-element.234), channel_id=1, source_target_pairs={{0,7},{1,0},{2,1},{3,2},{4,3},{5,4},{6,5},{7,6},{8,15},{9,8},{10,9... | collective-permute-start | bytes 98312 | tf_op jit(solution)/shard_map/while/body/eval_jaxpr/ppermute | solution.py:516
  110.4 17.1 %all-to-all-start = ((f32[32,40,128]{2,1,0:T(8,128)}), f32[32,40,128]{2,1,0:T(8,128)S(1)}, u32[]{:S(2)}, u32[]{:S(2)}) async-start(f32[32,40,128]{2,1,0:T(8,128)} %get-tuple-element.235), calls=%async_computation | async-start | bytes 1310720 | tf_op jit(solution)/shard_map/while/body/eval_jaxpr/all_to_all | solution.py:519
  114.6 3.7 %collective-permute-start = (f32[64,128]{1,0:T(8,128)}, f32[64,128]{1,0:T(8,128)S(1)}, u32[]{:S(2)}, u32[]{:S(2)}) collective-permute-start(f32[64,128]{1,0:T(8,128)} %get-tuple-element.234), channel_id=1, source_target_pairs={{0,1},{1,2},{2,3},{3,4},{4,5},{5,6},{6,7},{7,0},{8,9},{9,10},{10,1... | collective-permute-start | bytes 98312 | tf_op jit(solution)/shard_map/while/body/eval_jaxpr/ppermute | solution.py:516
  115.9 4.5 %collective-permute-start.1 = (f32[64,128]{1,0:T(8,128)}, f32[64,128]{1,0:T(8,128)S(1)}, u32[]{:S(2)}, u32[]{:S(2)}) collective-permute-start(f32[64,128]{1,0:T(8,128)} %get-tuple-element.234), channel_id=1, source_target_pairs={{0,7},{1,0},{2,1},{3,2},{4,3},{5,4},{6,5},{7,6},{8,15},{9,8},{10,9... | collective-permute-start | bytes 98312 | tf_op jit(solution)/shard_map/while/body/eval_jaxpr/ppermute | solution.py:516
  131.1 17.1 %all-to-all-start = ((f32[32,40,128]{2,1,0:T(8,128)}), f32[32,40,128]{2,1,0:T(8,128)S(1)}, u32[]{:S(2)}, u32[]{:S(2)}) async-start(f32[32,40,128]{2,1,0:T(8,128)} %get-tuple-element.235), calls=%async_computation | async-start | bytes 1310720 | tf_op jit(solution)/shard_map/while/body/eval_jaxpr/all_to_all | solution.py:519
  135.3 3.7 %collective-permute-start = (f32[64,128]{1,0:T(8,128)}, f32[64,128]{1,0:T(8,128)S(1)}, u32[]{:S(2)}, u32[]{:S(2)}) collective-permute-start(f32[64,128]{1,0:T(8,128)} %get-tuple-element.234), channel_id=1, source_target_pairs={{0,1},{1,2},{2,3},{3,4},{4,5},{5,6},{6,7},{7,0},{8,9},{9,10},{10,1... | collective-permute-start | bytes 98312 | tf_op jit(solution)/shard_map/while/body/eval_jaxpr/ppermute | solution.py:516
  136.5 4.5 %collective-permute-start.1 = (f32[64,128]{1,0:T(8,128)}, f32[64,128]{1,0:T(8,128)S(1)}, u32[]{:S(2)}, u32[]{:S(2)}) collective-permute-start(f32[64,128]{1,0:T(8,128)} %get-tuple-element.234), channel_id=1, source_target_pairs={{0,7},{1,0},{2,1},{3,2},{4,3},{5,4},{6,5},{7,6},{8,15},{9,8},{10,9... | collective-permute-start | bytes 98312 | tf_op jit(solution)/shard_map/while/body/eval_jaxpr/ppermute | solution.py:516
  151.7 17.1 %all-to-all-start = ((f32[32,40,128]{2,1,0:T(8,128)}), f32[32,40,128]{2,1,0:T(8,128)S(1)}, u32[]{:S(2)}, u32[]{:S(2)}) async-start(f32[32,40,128]{2,1,0:T(8,128)} %get-tuple-element.235), calls=%async_computation | async-start | bytes 1310720 | tf_op jit(solution)/shard_map/while/body/eval_jaxpr/all_to_all | solution.py:519
  156.0 3.7 %collective-permute-start = (f32[64,128]{1,0:T(8,128)}, f32[64,128]{1,0:T(8,128)S(1)}, u32[]{:S(2)}, u32[]{:S(2)}) collective-permute-start(f32[64,128]{1,0:T(8,128)} %get-tuple-element.234), channel_id=1, source_target_pairs={{0,1},{1,2},{2,3},{3,4},{4,5},{5,6},{6,7},{7,0},{8,9},{9,10},{10,1... | collective-permute-start | bytes 98312 | tf_op jit(solution)/shard_map/while/body/eval_jaxpr/ppermute | solution.py:516
  157.2 4.5 %collective-permute-start.1 = (f32[64,128]{1,0:T(8,128)}, f32[64,128]{1,0:T(8,128)S(1)}, u32[]{:S(2)}, u32[]{:S(2)}) collective-permute-start(f32[64,128]{1,0:T(8,128)} %get-tuple-element.234), channel_id=1, source_target_pairs={{0,7},{1,0},{2,1},{3,2},{4,3},{5,4},{6,5},{7,6},{8,15},{9,8},{10,9... | collective-permute-start | bytes 98312 | tf_op jit(solution)/shard_map/while/body/eval_jaxpr/ppermute | solution.py:516
  172.4 17.1 %all-to-all-start = ((f32[32,40,128]{2,1,0:T(8,128)}), f32[32,40,128]{2,1,0:T(8,128)S(1)}, u32[]{:S(2)}, u32[]{:S(2)}) async-start(f32[32,40,128]{2,1,0:T(8,128)} %get-tuple-element.235), calls=%async_computation | async-start | bytes 1310720 | tf_op jit(solution)/shard_map/while/body/eval_jaxpr/all_to_all | solution.py:519
  176.6 3.7 %collective-permute-start = (f32[64,128]{1,0:T(8,128)}, f32[64,128]{1,0:T(8,128)S(1)}, u32[]{:S(2)}, u32[]{:S(2)}) collective-permute-start(f32[64,128]{1,0:T(8,128)} %get-tuple-element.234), channel_id=1, source_target_pairs={{0,1},{1,2},{2,3},{3,4},{4,5},{5,6},{6,7},{7,0},{8,9},{9,10},{10,1... | collective-permute-start | bytes 98312 | tf_op jit(solution)/shard_map/while/body/eval_jaxpr/ppermute | solution.py:516
  177.9 4.5 %collective-permute-start.1 = (f32[64,128]{1,0:T(8,128)}, f32[64,128]{1,0:T(8,128)S(1)}, u32[]{:S(2)}, u32[]{:S(2)}) collective-permute-start(f32[64,128]{1,0:T(8,128)} %get-tuple-element.234), channel_id=1, source_target_pairs={{0,7},{1,0},{2,1},{3,2},{4,3},{5,4},{6,5},{7,6},{8,15},{9,8},{10,9... | collective-permute-start | bytes 98312 | tf_op jit(solution)/shard_map/while/body/eval_jaxpr/ppermute | solution.py:516
  193.1 10.0 %copy-start.6 = (f32[32,64,128]{2,1,0:T(8,128)}, f32[32,64,128]{2,1,0:T(8,128)S(1)}, u32[]{:S(2)}) copy-start(f32[32,64,128]{2,1,0:T(8,128)S(1)} %get-tuple-element.270) | copy-start | bytes 3145732
  193.1 17.1 %all-to-all-start.2 = ((f32[32,40,128]{2,1,0:T(8,128)}), f32[32,40,128]{2,1,0:T(8,128)S(1)}, u32[]{:S(2)}, u32[]{:S(2)}) async-start(f32[32,40,128]{2,1,0:T(8,128)} %get-tuple-element.102), calls=%async_computation.2 | async-start | bytes 1310720 | tf_op jit(solution)/shard_map/all_to_all | solution.py:519
  197.3 3.7 %collective-permute-start.2 = (f32[64,128]{1,0:T(8,128)}, f32[64,128]{1,0:T(8,128)S(1)}, u32[]{:S(2)}, u32[]{:S(2)}) collective-permute-start(f32[64,128]{1,0:T(8,128)} %get-tuple-element.104), channel_id=1, source_target_pairs={{0,1},{1,2},{2,3},{3,4},{4,5},{5,6},{6,7},{7,0},{8,9},{9,10},{10,1... | collective-permute-start | bytes 98312 | tf_op jit(solution)/shard_map/ppermute | solution.py:516
  198.5 4.5 %collective-permute-start.3 = (f32[64,128]{1,0:T(8,128)}, f32[64,128]{1,0:T(8,128)S(1)}, u32[]{:S(2)}, u32[]{:S(2)}) collective-permute-start(f32[64,128]{1,0:T(8,128)} %get-tuple-element.104), channel_id=1, source_target_pairs={{0,7},{1,0},{2,1},{3,2},{4,3},{5,4},{6,5},{7,6},{8,15},{9,8},{10,9... | collective-permute-start | bytes 98312 | tf_op jit(solution)/shard_map/ppermute | solution.py:516
  201.0 9.2 %copy-start.11 = (s32[5,32,128]{2,1,0:T(8,128)S(1)}, s32[5,32,128]{2,1,0:T(8,128)}, u32[]{:S(2)}) copy-start(s32[5,32,128]{2,1,0:T(8,128)} %get-tuple-element.280) | copy-start | bytes 245764
  213.9 7.1 %copy-start.8 = (f32[3,512,128]{2,1,0:T(8,128)S(1)}, f32[3,512,128]{2,1,0:T(8,128)}, u32[]{:S(2)}) copy-start(f32[3,512,128]{2,1,0:T(8,128)} %get-tuple-element.271) | copy-start | bytes 2359300
  213.9 20.1 %all-to-all-start.3 = ((f32[32,56,128]{2,1,0:T(8,128)}), f32[32,56,128]{2,1,0:T(8,128)S(1)}, u32[]{:S(2)}, u32[]{:S(2)}) async-start(f32[32,56,128]{2,1,0:T(8,128)} %get-tuple-element.107), calls=%async_computation.3 | async-start | bytes 1835008 | tf_op jit(solution)/shard_map/all_to_all | solution.py:519
  218.2 4.7 %copy-start.7 = (f32[32,64,128]{2,1,0:T(8,128)S(1)}, f32[32,64,128]{2,1,0:T(8,128)}, u32[]{:S(2)}) copy-start(f32[32,64,128]{2,1,0:T(8,128)} %copy-done.6) | copy-start | bytes 3145732
  218.3 4.7 %collective-permute-start.5 = (f32[64,128]{1,0:T(8,128)S(1)}, f32[64,128]{1,0:T(8,128)S(1)}, u32[]{:S(2)}, u32[]{:S(2)}) collective-permute-start(f32[64,128]{1,0:T(8,128)S(1)} %get-tuple-element.109), channel_id=1, source_target_pairs={{0,7},{1,0},{2,1},{3,2},{4,3},{5,4},{6,5},{7,6},{8,15},{9,8},{10,9... | collective-permute-start | bytes 98312 | tf_op jit(solution)/shard_map/ppermute | solution.py:516
  218.3 4.6 %collective-permute-start.4 = (f32[64,128]{1,0:T(8,128)S(1)}, f32[64,128]{1,0:T(8,128)S(1)}, u32[]{:S(2)}, u32[]{:S(2)}) collective-permute-start(f32[64,128]{1,0:T(8,128)S(1)} %get-tuple-element.109), channel_id=1, source_target_pairs={{0,1},{1,2},{2,3},{3,4},{4,5},{5,6},{6,7},{7,0},{8,9},{9,10},{10,1... | collective-permute-start | bytes 98312 | tf_op jit(solution)/shard_map/ppermute | solution.py:516
  222.9 11.1 %copy-start.3 = (f32[16,2048]{1,0:T(8,128)S(1)}, f32[16,2048]{1,0:T(8,128)}, u32[]{:S(2)}) copy-start(f32[16,2048]{1,0:T(8,128)} %cond_hbm.3) | copy-start | bytes 393220
  222.9 11.1 %copy-start.9 = (f32[12,2,32,128]{3,2,1,0:T(8,128)S(1)}, f32[12,2,32,128]{3,2,1,0:T(8,128)}, u32[]{:S(2)}) copy-start(f32[12,2,32,128]{3,2,1,0:T(8,128)} %get-tuple-element.276) | copy-start | bytes 1179652
  222.9 11.1 %copy-start.10 = (bf16[2,512,128]{2,1,0:T(8,128)(2,1)S(1)}, bf16[2,512,128]{2,1,0:T(8,128)(2,1)}, u32[]{:S(2)}) copy-start(bf16[2,512,128]{2,1,0:T(8,128)(2,1)} %get-tuple-element.278) | copy-start | bytes 786436

commit v3 on v2

--- a/solution.py
+++ b/solution.py
@@ -17,6 +17,7 @@
 SLOTS = 16
 TILE = 8
 VMEM_LIMIT = 16 << 20
+WHOLE_VMEM = 60 << 20
 
 
 def iota(dims, dim):
@@ -64,7 +65,7 @@
         return copy
 
 
-def call(kernel, ins, outs, scratch, copies, held=(), held_out=(), flops=0, nbytes=0, aliases=None):
+def call(kernel, ins, outs, scratch, copies, held=(), held_out=(), flops=0, nbytes=0, aliases=None, limit=VMEM_LIMIT):
     return pl.pallas_call(
         kernel,
         out_shape=outs,
@@ -78,7 +79,7 @@
         ],
         scratch_shapes=[pltpu.VMEM(s.shape, s.dtype) for s in scratch]
         + [pltpu.SemaphoreType.DMA((copies,))],
-        compiler_params=pltpu.CompilerParams(vmem_limit_bytes=VMEM_LIMIT),
+        compiler_params=pltpu.CompilerParams(vmem_limit_bytes=limit),
         cost_estimate=pl.CostEstimate(flops=flops, bytes_accessed=nbytes, transcendentals=0),
         input_output_aliases=aliases or {},
     )(*ins)
@@ -143,11 +144,10 @@
     back.wait()
 
 
-def outer_kernel(solid_hbm, heat_hbm, solid, heat, cols_hbm, cols, sems):
+def outer_kernel(solid_hbm, solid, cols, sems):
     copies = Copies(sems)
-    nz, nx, ny = heat.shape
+    nz, nx, ny = solid_hbm.shape
     inner = pl.ds(8, nx)
-    warm = copies.start(heat_hbm, heat)
     copies.start(solid_hbm, solid.at[pl.ds(1, nz), inner, :]).wait()
     lane = iota((nx, ny), 1)
     ends = jnp.where(lane < nz, 0, ny - 1)
@@ -164,14 +164,11 @@
         return found
 
     cols[...] = lax.fori_loop(0, nz // unroll, some, jnp.zeros((nx, ny), F32))
-    back = copies.start(cols, cols_hbm)
-    warm.wait()
-    back.wait()
 
 
 def owner_kernel(
     got_hbm, solid, const_hbm,
-    hit, hit_t, reply, weight, swell, index, scan, msg_hbm,
+    hit, hit_t, reply, weight, swell, scan, msg_hbm,
     got, const, msg, edges, sems,
 ):
     copies = Copies(sems)
@@ -194,7 +191,7 @@
         seg = jnp.where(mine, pick(part, SLOTS + lane8 % SLOTS), 0.0)
         seg = jnp.sum(seg, axis=0, keepdims=True).astype(I32)
         seg8 = jnp.broadcast_to(seg, (TILE, LANES))
-        index[4, g * TILE : (g + 1) * TILE, :] = seg8
+        scan[14, 0, g * TILE : (g + 1) * TILE, :] = seg8.astype(F32)
         cap = pick(cap8, seg8 // 16)[0:1]
         hits.append((rows == row.astype(I32)).astype(F32))
         caps.append(jnp.transpose(jnp.broadcast_to(cap, (LANES, LANES))))
@@ -227,12 +224,13 @@
     swell[0] = own_rate * jnp.exp(ahead + cond - middle)
     swell[1] = jnp.exp(middle - ahead)
     swell[2] = own_caprate
+    scan[14, 1] = jnp.zeros((n_flow, LANES), F32)
     lane_f, sub_f = iota((n_flow, LANES), 1), iota((n_flow, LANES), 0)
     inlet = jnp.broadcast_to(const[1:2, :], (n_flow, LANES))
     for half in range(2):
         slot = got[:, SLOTS + 1 + half, :].astype(I32)
-        index[half] = (sub_f % TILE) * SLOTS + slot % SLOTS
-        index[2 + half] = slot // SLOTS
+        scan[12, half] = ((sub_f % TILE) * SLOTS + slot % SLOTS).astype(F32)
+        scan[13, half] = (slot // SLOTS).astype(F32)
         gain = jnp.exp(-got[:, SLOTS + 3 + half, :])
         inner = lane_f % 16
         for step in range(4):
@@ -275,59 +273,53 @@
     ]
 
 
-def take_message(copies, got_hbm, got, edges):
-    n_flow, me = got.shape[0], lax.axis_index("flow")
-    rows = pl.ds(TILE, edges.shape[1])
-    return [
-        copies.start(got_hbm.at[:, pl.ds(0, TILE), :], got),
-        copies.start(got_hbm.at[lax.rem(me + n_flow - 1, n_flow), rows, :], edges.at[0]),
-        copies.start(got_hbm.at[lax.rem(me + 1, n_flow), rows, :], edges.at[1]),
-    ]
-
-
-def add_outer_rows(solid, edges):
+def add_outer_rows(solid, got):
     n_flow, me = lax.axis_size("flow"), lax.axis_index("flow")
-    nz, nx = edges.shape[1], solid.shape[1] - 16
-    north = jnp.where(me > 0, KAPPA * edges[0], 0.0)
-    south = jnp.where(me < n_flow - 1, KAPPA * edges[1], 0.0)
+    nz, nx = solid.shape[0] - 2, solid.shape[1] - 16
+    rows = pl.ds(TILE, nz)
+    north = got[lax.rem(me + n_flow - 1, n_flow), rows, :]
+    south = got[lax.rem(me + 1, n_flow), rows, :]
+    north = jnp.where(me > 0, KAPPA * north, 0.0)
+    south = jnp.where(me < n_flow - 1, KAPPA * south, 0.0)
     layers = pl.ds(1, nz)
     solid[layers, 8, :] = solid[layers, 8, :] + north
     solid[layers, 7 + nx, :] = solid[layers, 7 + nx, :] + south
     return north, south
 
 
-def march_kernel(solid, hit, hit_t, swell, sink, flux, sems):
-    del sems
-    slots = hit_t.shape[0]
-    piece = slots // 4
+def march_kernel(part, solid, hit, hit_t, swell, *rest):
+    *earlier_sink, sink, flux, _ = rest
+    slots = flux.shape[1]
+    piece = slots // 2
     nx, ny = sink.shape
     bottom = solid[1, pl.ds(8, nx), :]
     padded = jnp.concatenate([bottom, jnp.zeros((LANES - nx, ny), F32)], axis=0)
     wide = jnp.concatenate(parts(padded, 3), axis=1)
     earlier = (iota((LANES, LANES), 0) < iota((LANES, LANES), 1)).astype(F32).astype(BF16)
-    for i in range(4):
-        rows = pl.ds(i * piece, piece)
+    for i in range(2):
+        rows = pl.ds(part * slots + i * piece, piece)
+        to = pl.ds(i * piece, piece)
         triple = mul(hit_t[rows, :], wide)
         temp = (triple[:, 0:ny] + triple[:, ny : 2 * ny]) + triple[:, 2 * ny :]
         high, low = parts(swell[0, rows, :] * temp, 2)
         before = swell[1, rows, :] * (mul(high, earlier) + mul(low, earlier))
         high, low = parts(swell[2, rows, :] * (temp - before), 2)
-        flux[0, rows, :] = high
-        flux[1, rows, :] = low
-    sink[...] = mul(hit[...], flux[0]) + mul(hit[...], flux[1])
+        flux[0, to, :] = high
+        flux[1, to, :] = low
+    own = hit[:, part * slots : (part + 1) * slots]
+    total = mul(own, flux[0]) + mul(own, flux[1])
+    for other in earlier_sink:
+        total = total + other[...]
+    sink[...] = total
 
 
 def conduct_kernel(
-    old, heat, west_hbm, east_hbm, sink, solid, cols_hbm, west, east, cols, sems
+    old, heat, west, east, sink, solid, cols, sems
 ):
     del old
     nz, nx, ny = heat.shape
-    copies = Copies(sems)
+    del sems
     inner = pl.ds(8, nx)
-    for copy in [
-        copies.start(west_hbm, west), copies.start(east_hbm, east)
-    ]:
-        copy.wait()
     lot, n_span = lax.axis_index("span"), lax.axis_size("span")
     lane = iota((nx, ny), 1)
     border = (lane == 0) | (lane == ny - 1)
@@ -354,25 +346,31 @@
 
     zero = jnp.zeros((nx, ny), F32)
     cols[...], _ = lax.fori_loop(0, nz // unroll, some, (zero, zero))
-    back = copies.start(cols, cols_hbm)
     solid[1, inner, :] = solid[1, inner, :] - sink[...]
-    back.wait()
-
-
-def entering(got, index, scan):
+
+
+def take_scan(copies, scan_hbm, scan):
+    places, gains = pl.ds(12, 3), pl.ds(0, 12)
+    return [
+        copies.start(scan_hbm.at[rows], scan.at[rows]) for rows in (places, gains)
+    ]
+
+
+def entering(got, scan, gains):
     n_flow = got.shape[0]
     ends = [[], []]
     for g in range(n_flow // TILE):
         rows = slice(g * TILE, (g + 1) * TILE)
-        lanes = [index[half, rows, :] for half in range(2)]
-        origin = [index[2 + half, rows, :] for half in range(2)]
+        lanes = [scan[12, half, rows, :].astype(I32) for half in range(2)]
+        origin = [scan[13, half, rows, :] for half in range(2)]
         acc = [jnp.zeros((TILE, LANES), F32) for _ in range(2)]
         for o in range(n_flow):
             line = jnp.broadcast_to(got[o, g : g + 1, :], (TILE, LANES))
             for half in range(2):
-                acc[half] = jnp.where(origin[half] == o, pick(line, lanes[half]), acc[half])
+                acc[half] = jnp.where(origin[half] == float(o), pick(line, lanes[half]), acc[half])
         for half in range(2):
             ends[half].append(acc[half])
+    gains.wait()
     result = []
     sub, lane = iota((n_flow, LANES), 0), iota((n_flow, LANES), 1)
     for half in range(2):
@@ -390,12 +388,12 @@
     return result
 
 
-def hosted(enter, index):
+def hosted(enter, scan):
     lane8, sub8 = iota((TILE, LANES), 1), iota((TILE, LANES), 0)
     found = []
     for g in range(enter[0].shape[0] // TILE):
         rows = slice(g * TILE, (g + 1) * TILE)
-        seg = index[4, rows, :]
+        seg = scan[14, 0, rows, :].astype(I32)
         low, high = (pick(enter[half][rows], seg % LANES) for half in range(2))
         value = jnp.where(lane8 // SLOTS == sub8, jnp.where(seg < LANES, low, high), 0.0)
         found.append(jnp.sum(value, axis=0, keepdims=True))
@@ -410,24 +408,24 @@
 
 def after_kernel(
     last,
-    got_hbm, old, plain_hbm, index, scan, hit, reply, weight, hit_t,
-    solid, msg_hbm, cols_hbm,
-    got, edges, plain, msg, cols, sems,
+    got, old, plain, scan_hbm, hit, reply_hbm, weight_hbm, hit_t,
+    solid, msg_hbm, cols,
+    scan, edges, msg, reply, weight, sems,
 ):
     del old
     copies = Copies(sems)
-    first, *then = take_message(copies, got_hbm, got, edges)
-    then.append(copies.start(plain_hbm, plain))
-    first.wait()
-    carry = hosted(entering(got, index, scan), index)
+    places, gains = take_scan(copies, scan_hbm, scan)
+    come = [copies.start(reply_hbm, reply), copies.start(weight_hbm, weight)]
+    north, south = add_outer_rows(solid, got)
+    places.wait()
+    carry = hosted(entering(got, scan, gains), scan)
     own_hit = hit[...]
     nx = own_hit.shape[0]
     inner = pl.ds(8, nx)
-    for copy in then:
-        copy.wait()
-    north, south = add_outer_rows(solid, edges)
+    come[0].wait()
     new = new_bottom(carry, solid[1, inner, :], own_hit, reply)
     solid[1, inner, :] = new
+    come[1].wait()
     write_shifts(new, weight, own_hit.astype(F32), msg)
     back = send_message(copies, solid, msg, edges, msg_hbm)
     nx, ny = new.shape
@@ -450,33 +448,34 @@
     value = plain[...] + jnp.where(sub == 0, ends_of(north), 0.0)
     value = value + jnp.where(sub == nx - 1, ends_of(south), 0.0)
     cols[...] = jnp.where(lane % nz == 0, pick(new, jnp.where(lane < nz, 0, ny - 1)), value)
-    back.append(copies.start(cols, cols_hbm))
     for copy in back:
         copy.wait()
 
 
 def final_kernel(
-    got_hbm, solid_hbm, place_hbm, cond_hbm, index, scan, hit, reply, out_hbm, coolant_hbm,
-    got, edges, temps, place, cond, solid, coolant, sems,
+    got, old, place_hbm, cond_hbm, scan_hbm, hit, reply_hbm, solid, out_hbm, coolant_hbm,
+    scan, place, cond, reply, coolant, sems,
 ):
     copies = Copies(sems)
     nz, nx = out_hbm.shape[0], out_hbm.shape[1]
     inner = pl.ds(8, nx)
-    first, *then = take_message(copies, got_hbm, got, edges)
-    whole = copies.start(solid_hbm, solid)
-    rows = pl.ds(TILE + nz, SLOTS)
-    then += [copies.start(got_hbm.at[:, rows, :], temps), copies.start(place_hbm, place)]
-    then += load_segments(copies, cond_hbm, cond)
-    first.wait()
-    enter = entering(got, index, scan)
-    carry = hosted(enter, index)
-    for copy in [whole, *then]:
+    del old
+    places, gains = take_scan(copies, scan_hbm, scan)
+    come = copies.start(reply_hbm, reply)
+    then = [copies.start(place_hbm, place), *load_segments(copies, cond_hbm, cond)]
+    add_outer_rows(solid, got)
+    upper = pl.ds(2, nz - 1)
+    back = [copies.start(solid.at[upper, inner, :], out_hbm.at[pl.ds(1, nz - 1)])]
+    places.wait()
+    enter = entering(got, scan, gains)
+    carry = hosted(enter, scan)
+    come.wait()
+    solid[1, inner, :] = new_bottom(carry, solid[1, inner, :], hit[...], reply)
+    back.append(copies.start(solid.at[1, inner, :], out_hbm.at[0]))
+    for copy in then:
         copy.wait()
-    add_outer_rows(solid, edges)
-    solid[1, inner, :] = new_bottom(carry, solid[1, inner, :], hit[...], reply)
-    back = [copies.start(solid.at[pl.ds(1, nz), inner, :], out_hbm)]
     n_flow = got.shape[0]
-    stacked = temps[...].reshape(n_flow * SLOTS, LANES)
+    stacked = got[:, TILE + nz :, :].reshape(n_flow * SLOTS, LANES)
     temp = sum(mul(place[...], part) for part in parts(stacked, 3))
     segs = temp.shape[0]
     lane = iota((segs, LANES), 1)
@@ -510,11 +509,6 @@
         jnp.stack([heat_capacity, inlet_temp]), ((0, TILE - 2), (0, LANES - channels))
     )
 
-    def beside_span(cols):
-        up = [(i, (i + 1) % n_span) for i in range(n_span)]
-        down = [(i, (i - 1) % n_span) for i in range(n_span)]
-        return lax.ppermute(cols, "span", up), lax.ppermute(cols, "span", down)
-
     def exchange(message):
         return lax.all_to_all(message, "flow", 0, 0, tiled=True)
 
@@ -529,54 +523,65 @@
         (pay_spec, place_spec),
         (lines, lines, split, pay_spec, place_spec),
         20,
+        limit=WHOLE_VMEM,
     )
     got = exchange(pay)
     room = spec((nz + 2, nx + 16, ny))
-    solid, heat, cols = call(
-        outer_kernel, (solid_start, heat_gen), (room, block, layer), (layer,), 3, held_out=(0, 1)
+    solid, cols = call(
+        outer_kernel, (solid_start,), (room, layer), (), 1, held_out=(0, 1), limit=WHOLE_VMEM
     )
     hit_spec, hit_t_spec = spec((nx, slots), BF16), spec((slots, LANES), BF16)
     reply_spec, weight_spec = spec((2, slots, LANES), BF16), spec((2, LANES, slots), BF16)
     swell_spec = spec((3, slots, LANES))
-    index_spec, scan_spec = spec((5, n_flow, LANES), I32), spec((12, 2, n_flow, LANES))
+    scan_spec = spec((15, 2, n_flow, LANES))
     msg_spec = spec((n_flow, TILE + nz, LANES))
     long_spec = spec((n_flow, TILE + nz + SLOTS, LANES))
-    short_spec, temps_spec = spec((n_flow, TILE, LANES)), spec((n_flow, SLOTS, LANES))
+    short_spec = spec((n_flow, TILE, LANES))
     constants = (
-        hit_spec, hit_t_spec, reply_spec, weight_spec, swell_spec, index_spec, scan_spec, msg_spec,
-    )
-    hit, hit_t, reply, weight, swell, index, scan, message = call(
+        hit_spec, hit_t_spec, reply_spec, weight_spec, swell_spec, scan_spec, msg_spec,
+    )
+    hit, hit_t, reply, weight, swell, scan, message = call(
         owner_kernel,
         (got, solid, const),
         constants,
         (pay_spec, spec((TILE, LANES)), short_spec, edges_spec),
         5,
         held=(1,),
-        held_out=range(7),
-    )
+        held_out=range(6),
+    )
+
+    def march(part, *operands):
+        (sink,) = call(
+            functools.partial(march_kernel, part),
+            operands,
+            (layer,),
+            (spec((2, slots // 2, LANES), BF16),),
+            1,
+            held=range(len(operands)),
+            held_out=(0,),
+            flops=1_000_000,
+            nbytes=1_500_000,
+        )
+        return sink
 
     def beside(solid, cols, message):
         got = exchange(message)
-        west, east = beside_span(cols)
-        (sink,) = call(
-            march_kernel,
-            (solid, hit, hit_t, swell),
-            (layer,),
-            (reply_spec,),
-            1,
-            held=range(4),
-            held_out=(0,),
-            flops=2_000_000,
-            nbytes=3_000_000,
-        )
+        up = [(i, (i + 1) % n_span) for i in range(n_span)]
+        down = [(i, (i - 1) % n_span) for i in range(n_span)]
+        west = lax.ppermute(cols, "span", up)
+        sink = march(0, solid, hit, hit_t, swell)
+        cols, sink = lax.optimization_barrier((cols, sink))
+        east = lax.ppermute(cols, "span", down)
+        west, sink = lax.optimization_barrier((west, sink))
+        sink = march(1, solid, hit, hit_t, swell, sink)
         solid, cols = call(
             conduct_kernel,
-            (solid, heat, west, east, sink),
+            (solid, heat_gen, west, east, sink),
             (room, layer),
-            (layer, layer, layer),
-            3,
-            held=(0, 1, 4),
-            held_out=(0,),
+            (),
+            1,
+            held=range(5),
+            held_out=(0, 1),
             flops=4_000_000,
             nbytes=6_000_000,
             aliases={0: 0},
@@ -587,15 +592,16 @@
         got, solid, cols = beside(*state)
         solid, message, cols = call(
             functools.partial(after_kernel, last),
-            (got, solid, cols, index, scan, hit, reply, weight, hit_t),
+            (got, solid, cols, scan, hit, reply, weight, hit_t),
             (room, long_spec if last else msg_spec, layer),
             (
-                short_spec, edges_spec, layer,
-                spec((n_flow, TILE + SLOTS, LANES)) if last else short_spec, layer,
+                scan_spec,
+                edges_spec, spec((n_flow, TILE + SLOTS, LANES)) if last else short_spec,
+                reply_spec, weight_spec,
             ),
-            9,
-            held=(1, *range(3, 9)),
-            held_out=(0,),
+            8,
+            held=(0, 1, 2, 4, 7),
+            held_out=(0, 2),
             flops=4_000_000,
             nbytes=4_000_000,
             aliases={1: 0},
@@ -604,14 +610,17 @@
 
     state = lax.fori_loop(0, STEPS - 2, lambda turn, now: step(now), (solid, cols, message))
     got, solid, _ = beside(*step(state, last=True))
-    return call(
+    _, solid, coolant = call(
         final_kernel,
-        (got, solid, place, conductance, index, scan, hit, reply),
-        (block, spec((channels, stations))),
-        (short_spec, edges_spec, temps_spec, place_spec, split, room, split),
-        7 + 2 * split.shape[1],
-        held=(4, 5, 6, 7),
-    )
+        (got, solid, place, conductance, scan, hit, reply),
+        (room, block, spec((channels, stations))),
+        (scan_spec, place_spec, split, reply_spec, split),
+        6 + 2 * split.shape[1],
+        held=(0, 1, 5),
+        held_out=(0,),
+        aliases={1: 0},
+    )
+    return solid, coolant
 
 
 def solution(mesh):

time: 241 us -> 234 us (0.971)
  Pallas kernels: 92.7 us -> 79.1 us
  waiting for transfers between devices: 70.3 us -> 82.1 us
  local copies, waits for them, and re-layouts: 4.75 us -> 0.08 us
    pallas_call x33 -> x43, Pallas kernels: 92.7 us -> 79.1 us  [call(): pl.pallas_call(kernel, out_shape=outs, in_specs=[pl.BlockSpec(memory_spac...]
    ppermute x20, waiting for transfers between devices: 18.1 us -> 29.4 us  [the longest x10 23.2 us: beside(): east = lax.ppermute(cols, 'span', down)]
    unnamed x28 -> x18, local copies, waits for them, and re-layouts: 4.75 us -> 0.04 us
  transfers between devices with their start and end apart: 31 -> 31, of which waited for: 20 -> 31; matrix products, arithmetic and copies ran while one was open for 0% -> 0% of each run, Pallas kernels for 21% -> 18%
where the time goes in v3:
time: 234 us; the launch traced here: 232 us
  waiting for transfers between devices  82.1 us (35%)
  Pallas kernels  79.1 us (34%)
  starting transfers between devices  69.2 us (30%)
    pallas_call x43, Pallas kernels, call(): pl.pallas_call(kernel, out_shape=outs, in_specs=[pl.BlockSpec(memory_spac...  79.1 us
    all_to_all x11, waiting for transfers between devices, exchange(): return lax.all_to_all(message, 'flow', 0, 0, tiled=True)  52.7 us
    all_to_all x11, starting transfers between devices, exchange(): return lax.all_to_all(message, 'flow', 0, 0, tiled=True)  51.6 us
    ppermute x10, waiting for transfers between devices, beside(): east = lax.ppermute(cols, 'span', down)  23.2 us
    ppermute x10, starting transfers between devices, beside(): west = lax.ppermute(cols, 'span', up)  10.3 us
    ppermute x10, starting transfers between devices, beside(): east = lax.ppermute(cols, 'span', down)  7.32 us
    ppermute x10, waiting for transfers between devices, beside(): west = lax.ppermute(cols, 'span', up)  6.23 us
  transfers between devices with their start and end apart: 31, of which 31 were waited for; matrix products, arithmetic and copies ran while one was open for 0% of the time, Pallas kernels for 18%

profile of v3, /device:TPU:97, one launch (start us, length us, event | category | flops | bytes accessed | tf_op | source)
XLA Modules:
  0.0 231.8 jit_solution(18279842575230393171)
XLA Ops:
  0.7 2.5 %shard_map.87 = (f32[32,24,128]{2,1,0:T(8,128)}, bf16[256,512]{1,0:T(8,128)(2,1)}) custom-call(s32[2,128]{1,0:T(2,128)} %bitcast.4, s32[2,128]{1,0:T(2,128)} %bitcast.5, f32[16,2048]{1,0:T(8,128)} %cond_hbm.3), custom_call_target="tpu_custom_call" | custom-call | tf_op jit(solution)/shard_map/pallas_call | solution.py:69
  3.2 7.8 %all-to-all-start.1 = ((f32[32,24,128]{2,1,0:T(8,128)}), f32[32,24,128]{2,1,0:T(8,128)S(1)}, u32[]{:S(2)}, u32[]{:S(2)}) async-start(f32[32,24,128]{2,1,0:T(8,128)} %get-tuple-element.99), calls=%async_computation.1 | async-start | bytes 786432 | tf_op jit(solution)/shard_map/all_to_all | solution.py:513
  13.1 8.1 %all-to-all-done.1.got_hbm = f32[32,24,128]{2,1,0:T(8,128)S(1)} async-done(((f32[32,24,128]{2,1,0:T(8,128)}), f32[32,24,128]{2,1,0:T(8,128)S(1)}, u32[]{:S(2)}, u32[]{:S(2)}) %all-to-all-start.1) | async-done | bytes 393248 | tf_op jit(solution)/shard_map/all_to_all | solution.py:513
  21.1 3.1 %shard_map.88 = (bf16[64,512]{1,0:T(8,128)(2,1)S(1)}, bf16[512,128]{1,0:T(8,128)(2,1)S(1)}, bf16[2,512,128]{2,1,0:T(8,128)(2,1)S(1)}, bf16[2,128,512]{2,1,0:T(8,...) custom-call(f32[32,24,128]{2,1,0:T(8,128)S(1)} %all-to-all-done.1.got_hbm, ...), custom_call_target="tpu_custom_call" | custom-call | tf_op jit(solution)/shard_map/pallas_call | solution.py:69
  24.2 163.6 %while.14 = (s32[]{:T(128)}, f32[34,80,128]{2,1,0:T(8,128)S(1)}, f32[64,128]{1,0:T(8,128)S(1)}, f32[32,40,128]{2,1,0:T(8,128)}, bf16[64,512]{1,0:T(8,128)(2,1)S(...) while((s32[]{:T(128)}, f32[34,80,128]{2,1,0:T(8,128)S(1)}, ...), condition=%wide.region_1.2_spmd, body=%wide.region_0.1_spmd.sunk | while | flops 10000002 | bytes 19422784 | solution.py:611
  24.2 3.9 %all-to-all-start = ((f32[32,40,128]{2,1,0:T(8,128)}), f32[32,40,128]{2,1,0:T(8,128)S(1)}, u32[]{:S(2)}, u32[]{:S(2)}) async-start(f32[32,40,128]{2,1,0:T(8,128)} %get-tuple-element.249), calls=%async_computation | async-start | bytes 1310720 | tf_op jit(solution)/shard_map/while/body/eval_jaxpr/all_to_all | solution.py:513
  28.2 2.9 %collective-permute-start = (f32[64,128]{1,0:T(8,128)S(1)}, f32[64,128]{1,0:T(8,128)S(1)}, u32[]{:S(2)}, u32[]{:S(2)}) collective-permute-start(f32[64,128]{1,0:T(8,128)S(1)} %get-tuple-element.227), channel_id=1, source_target_pairs={{0,1},{1,2},{2,3},{3,4},{4,5},{5,6},{6,7},{7,0},{8,9},{9,10},{10,1... | collective-permute-start | bytes 98312 | tf_op jit(solution)/shard_map/while/body/eval_jaxpr/ppermute | solution.py:571
  32.8 3.3 %collective-permute-done.1.east = f32[64,128]{1,0:T(8,128)S(1)} collective-permute-done((f32[64,128]{1,0:T(8,128)S(1)}, f32[64,128]{1,0:T(8,128)S(1)}, u32[]{:S(2)}, u32[]{:S(2)}) %collective-permute-start.1) | collective-permute-done | bytes 32800 | tf_op jit(solution)/shard_map/while/body/eval_jaxpr/ppermute | solution.py:574
  36.1 2.6 %eval_jaxpr.6 = (f32[34,80,128]{2,1,0:T(8,128)S(1)}, f32[64,128]{1,0:T(8,128)S(1)}) custom-call(f32[34,80,128]{2,1,0:T(8,128)S(1)} %get-tuple-element.247.solid.old, f32[32,64,128]{2,1,0:T(8,128)S(1)} %copy-done.2, f32[64,128]{1,0:T(8,128)S(1)} %collective-permute-done.west, ...), custom_call_target="tpu_custom_call", output_to_operand_aliasing={{0}: (0, {})} | custom-call | flops 4000000 | bytes 6000000 | tf_op jit(solution)/shard_map/while/body/eval_jaxpr/pallas_call | solution.py:69
  38.8 2.4 %all-to-all-done.got = f32[32,40,128]{2,1,0:T(8,128)S(1)} async-done(((f32[32,40,128]{2,1,0:T(8,128)}), f32[32,40,128]{2,1,0:T(8,128)S(1)}, u32[]{:S(2)}, u32[]{:S(2)}) %all-to-all-start) | async-done | bytes 655392 | tf_op jit(solution)/shard_map/while/body/eval_jaxpr/all_to_all | solution.py:513
  41.2 3.1 %eval_jaxpr.7 = (f32[34,80,128]{2,1,0:T(8,128)S(1)}, f32[32,40,128]{2,1,0:T(8,128)}, f32[64,128]{1,0:T(8,128)S(1)}) custom-call(f32[32,40,128]{2,1,0:T(8,128)S(1)} %all-to-all-done.got, f32[34,80,128]{2,1,0:T(8,128)S(1)} %get-tuple-element.229.old, f32[64,128]{1,0:T(8,128)S(1)} %get-tuple-element.230.plain, ...), custom_call_target="tpu_custom_call", output_to_operand_aliasing={{0}: (1, {})} | custom-call | flops 4000000 | bytes 4000000 | tf_op jit(solution)/shard_map/while/body/eval_jaxpr/pallas_call | solution.py:69
  44.3 6.2 %all-to-all-start = ((f32[32,40,128]{2,1,0:T(8,128)}), f32[32,40,128]{2,1,0:T(8,128)S(1)}, u32[]{:S(2)}, u32[]{:S(2)}) async-start(f32[32,40,128]{2,1,0:T(8,128)} %get-tuple-element.249), calls=%async_computation | async-start | bytes 1310720 | tf_op jit(solution)/shard_map/while/body/eval_jaxpr/all_to_all | solution.py:513
  56.3 2.6 %eval_jaxpr.6 = (f32[34,80,128]{2,1,0:T(8,128)S(1)}, f32[64,128]{1,0:T(8,128)S(1)}) custom-call(f32[34,80,128]{2,1,0:T(8,128)S(1)} %get-tuple-element.247.solid.old, f32[32,64,128]{2,1,0:T(8,128)S(1)} %copy-done.2, f32[64,128]{1,0:T(8,128)S(1)} %collective-permute-done.west, ...), custom_call_target="tpu_custom_call", output_to_operand_aliasing={{0}: (0, {})} | custom-call | flops 4000000 | bytes 6000000 | tf_op jit(solution)/shard_map/while/body/eval_jaxpr/pallas_call | solution.py:69
  59.0 4.4 %all-to-all-done.got = f32[32,40,128]{2,1,0:T(8,128)S(1)} async-done(((f32[32,40,128]{2,1,0:T(8,128)}), f32[32,40,128]{2,1,0:T(8,128)S(1)}, u32[]{:S(2)}, u32[]{:S(2)}) %all-to-all-start) | async-done | bytes 655392 | tf_op jit(solution)/shard_map/while/body/eval_jaxpr/all_to_all | solution.py:513
  63.4 3.1 %eval_jaxpr.7 = (f32[34,80,128]{2,1,0:T(8,128)S(1)}, f32[32,40,128]{2,1,0:T(8,128)}, f32[64,128]{1,0:T(8,128)S(1)}) custom-call(f32[32,40,128]{2,1,0:T(8,128)S(1)} %all-to-all-done.got, f32[34,80,128]{2,1,0:T(8,128)S(1)} %get-tuple-element.229.old, f32[64,128]{1,0:T(8,128)S(1)} %get-tuple-element.230.plain, ...), custom_call_target="tpu_custom_call", output_to_operand_aliasing={{0}: (1, {})} | custom-call | flops 4000000 | bytes 4000000 | tf_op jit(solution)/shard_map/while/body/eval_jaxpr/pallas_call | solution.py:69
  66.5 4.2 %all-to-all-start = ((f32[32,40,128]{2,1,0:T(8,128)}), f32[32,40,128]{2,1,0:T(8,128)S(1)}, u32[]{:S(2)}, u32[]{:S(2)}) async-start(f32[32,40,128]{2,1,0:T(8,128)} %get-tuple-element.249), calls=%async_computation | async-start | bytes 1310720 | tf_op jit(solution)/shard_map/while/body/eval_jaxpr/all_to_all | solution.py:513
  76.6 2.6 %eval_jaxpr.6 = (f32[34,80,128]{2,1,0:T(8,128)S(1)}, f32[64,128]{1,0:T(8,128)S(1)}) custom-call(f32[34,80,128]{2,1,0:T(8,128)S(1)} %get-tuple-element.247.solid.old, f32[32,64,128]{2,1,0:T(8,128)S(1)} %copy-done.2, f32[64,128]{1,0:T(8,128)S(1)} %collective-permute-done.west, ...), custom_call_target="tpu_custom_call", output_to_operand_aliasing={{0}: (0, {})} | custom-call | flops 4000000 | bytes 6000000 | tf_op jit(solution)/shard_map/while/body/eval_jaxpr/pallas_call | solution.py:69
  79.2 4.4 %all-to-all-done.got = f32[32,40,128]{2,1,0:T(8,128)S(1)} async-done(((f32[32,40,128]{2,1,0:T(8,128)}), f32[32,40,128]{2,1,0:T(8,128)S(1)}, u32[]{:S(2)}, u32[]{:S(2)}) %all-to-all-start) | async-done | bytes 655392 | tf_op jit(solution)/shard_map/while/body/eval_jaxpr/all_to_all | solution.py:513
  83.6 3.1 %eval_jaxpr.7 = (f32[34,80,128]{2,1,0:T(8,128)S(1)}, f32[32,40,128]{2,1,0:T(8,128)}, f32[64,128]{1,0:T(8,128)S(1)}) custom-call(f32[32,40,128]{2,1,0:T(8,128)S(1)} %all-to-all-done.got, f32[34,80,128]{2,1,0:T(8,128)S(1)} %get-tuple-element.229.old, f32[64,128]{1,0:T(8,128)S(1)} %get-tuple-element.230.plain, ...), custom_call_target="tpu_custom_call", output_to_operand_aliasing={{0}: (1, {})} | custom-call | flops 4000000 | bytes 4000000 | tf_op jit(solution)/shard_map/while/body/eval_jaxpr/pallas_call | solution.py:69
  86.7 4.2 %all-to-all-start = ((f32[32,40,128]{2,1,0:T(8,128)}), f32[32,40,128]{2,1,0:T(8,128)S(1)}, u32[]{:S(2)}, u32[]{:S(2)}) async-start(f32[32,40,128]{2,1,0:T(8,128)} %get-tuple-element.249), calls=%async_computation | async-start | bytes 1310720 | tf_op jit(solution)/shard_map/while/body/eval_jaxpr/all_to_all | solution.py:513
  96.8 2.6 %eval_jaxpr.6 = (f32[34,80,128]{2,1,0:T(8,128)S(1)}, f32[64,128]{1,0:T(8,128)S(1)}) custom-call(f32[34,80,128]{2,1,0:T(8,128)S(1)} %get-tuple-element.247.solid.old, f32[32,64,128]{2,1,0:T(8,128)S(1)} %copy-done.2, f32[64,128]{1,0:T(8,128)S(1)} %collective-permute-done.west, ...), custom_call_target="tpu_custom_call", output_to_operand_aliasing={{0}: (0, {})} | custom-call | flops 4000000 | bytes 6000000 | tf_op jit(solution)/shard_map/while/body/eval_jaxpr/pallas_call | solution.py:69
  99.4 4.4 %all-to-all-done.got = f32[32,40,128]{2,1,0:T(8,128)S(1)} async-done(((f32[32,40,128]{2,1,0:T(8,128)}), f32[32,40,128]{2,1,0:T(8,128)S(1)}, u32[]{:S(2)}, u32[]{:S(2)}) %all-to-all-start) | async-done | bytes 655392 | tf_op jit(solution)/shard_map/while/body/eval_jaxpr/all_to_all | solution.py:513
  103.9 3.1 %eval_jaxpr.7 = (f32[34,80,128]{2,1,0:T(8,128)S(1)}, f32[32,40,128]{2,1,0:T(8,128)}, f32[64,128]{1,0:T(8,128)S(1)}) custom-call(f32[32,40,128]{2,1,0:T(8,128)S(1)} %all-to-all-done.got, f32[34,80,128]{2,1,0:T(8,128)S(1)} %get-tuple-element.229.old, f32[64,128]{1,0:T(8,128)S(1)} %get-tuple-element.230.plain, ...), custom_call_target="tpu_custom_call", output_to_operand_aliasing={{0}: (1, {})} | custom-call | flops 4000000 | bytes 4000000 | tf_op jit(solution)/shard_map/while/body/eval_jaxpr/pallas_call | solution.py:69
  106.9 4.2 %all-to-all-start = ((f32[32,40,128]{2,1,0:T(8,128)}), f32[32,40,128]{2,1,0:T(8,128)S(1)}, u32[]{:S(2)}, u32[]{:S(2)}) async-start(f32[32,40,128]{2,1,0:T(8,128)} %get-tuple-element.249), calls=%async_computation | async-start | bytes 1310720 | tf_op jit(solution)/shard_map/while/body/eval_jaxpr/all_to_all | solution.py:513
  117.0 2.6 %eval_jaxpr.6 = (f32[34,80,128]{2,1,0:T(8,128)S(1)}, f32[64,128]{1,0:T(8,128)S(1)}) custom-call(f32[34,80,128]{2,1,0:T(8,128)S(1)} %get-tuple-element.247.solid.old, f32[32,64,128]{2,1,0:T(8,128)S(1)} %copy-done.2, f32[64,128]{1,0:T(8,128)S(1)} %collective-permute-done.west, ...), custom_call_target="tpu_custom_call", output_to_operand_aliasing={{0}: (0, {})} | custom-call | flops 4000000 | bytes 6000000 | tf_op jit(solution)/shard_map/while/body/eval_jaxpr/pallas_call | solution.py:69
  119.6 4.4 %all-to-all-done.got = f32[32,40,128]{2,1,0:T(8,128)S(1)} async-done(((f32[32,40,128]{2,1,0:T(8,128)}), f32[32,40,128]{2,1,0:T(8,128)S(1)}, u32[]{:S(2)}, u32[]{:S(2)}) %all-to-all-start) | async-done | bytes 655392 | tf_op jit(solution)/shard_map/while/body/eval_jaxpr/all_to_all | solution.py:513
  124.1 3.1 %eval_jaxpr.7 = (f32[34,80,128]{2,1,0:T(8,128)S(1)}, f32[32,40,128]{2,1,0:T(8,128)}, f32[64,128]{1,0:T(8,128)S(1)}) custom-call(f32[32,40,128]{2,1,0:T(8,128)S(1)} %all-to-all-done.got, f32[34,80,128]{2,1,0:T(8,128)S(1)} %get-tuple-element.229.old, f32[64,128]{1,0:T(8,128)S(1)} %get-tuple-element.230.plain, ...), custom_call_target="tpu_custom_call", output_to_operand_aliasing={{0}: (1, {})} | custom-call | flops 4000000 | bytes 4000000 | tf_op jit(solution)/shard_map/while/body/eval_jaxpr/pallas_call | solution.py:69
  127.2 4.2 %all-to-all-start = ((f32[32,40,128]{2,1,0:T(8,128)}), f32[32,40,128]{2,1,0:T(8,128)S(1)}, u32[]{:S(2)}, u32[]{:S(2)}) async-start(f32[32,40,128]{2,1,0:T(8,128)} %get-tuple-element.249), calls=%async_computation | async-start | bytes 1310720 | tf_op jit(solution)/shard_map/while/body/eval_jaxpr/all_to_all | solution.py:513
  137.2 2.6 %eval_jaxpr.6 = (f32[34,80,128]{2,1,0:T(8,128)S(1)}, f32[64,128]{1,0:T(8,128)S(1)}) custom-call(f32[34,80,128]{2,1,0:T(8,128)S(1)} %get-tuple-element.247.solid.old, f32[32,64,128]{2,1,0:T(8,128)S(1)} %copy-done.2, f32[64,128]{1,0:T(8,128)S(1)} %collective-permute-done.west, ...), custom_call_target="tpu_custom_call", output_to_operand_aliasing={{0}: (0, {})} | custom-call | flops 4000000 | bytes 6000000 | tf_op jit(solution)/shard_map/while/body/eval_jaxpr/pallas_call | solution.py:69
  139.8 4.4 %all-to-all-done.got = f32[32,40,128]{2,1,0:T(8,128)S(1)} async-done(((f32[32,40,128]{2,1,0:T(8,128)}), f32[32,40,128]{2,1,0:T(8,128)S(1)}, u32[]{:S(2)}, u32[]{:S(2)}) %all-to-all-start) | async-done | bytes 655392 | tf_op jit(solution)/shard_map/while/body/eval_jaxpr/all_to_all | solution.py:513
  144.3 3.1 %eval_jaxpr.7 = (f32[34,80,128]{2,1,0:T(8,128)S(1)}, f32[32,40,128]{2,1,0:T(8,128)}, f32[64,128]{1,0:T(8,128)S(1)}) custom-call(f32[32,40,128]{2,1,0:T(8,128)S(1)} %all-to-all-done.got, f32[34,80,128]{2,1,0:T(8,128)S(1)} %get-tuple-element.229.old, f32[64,128]{1,0:T(8,128)S(1)} %get-tuple-element.230.plain, ...), custom_call_target="tpu_custom_call", output_to_operand_aliasing={{0}: (1, {})} | custom-call | flops 4000000 | bytes 4000000 | tf_op jit(solution)/shard_map/while/body/eval_jaxpr/pallas_call | solution.py:69
  147.4 4.2 %all-to-all-start = ((f32[32,40,128]{2,1,0:T(8,128)}), f32[32,40,128]{2,1,0:T(8,128)S(1)}, u32[]{:S(2)}, u32[]{:S(2)}) async-start(f32[32,40,128]{2,1,0:T(8,128)} %get-tuple-element.249), calls=%async_computation | async-start | bytes 1310720 | tf_op jit(solution)/shard_map/while/body/eval_jaxpr/all_to_all | solution.py:513
  157.4 2.6 %eval_jaxpr.6 = (f32[34,80,128]{2,1,0:T(8,128)S(1)}, f32[64,128]{1,0:T(8,128)S(1)}) custom-call(f32[34,80,128]{2,1,0:T(8,128)S(1)} %get-tuple-element.247.solid.old, f32[32,64,128]{2,1,0:T(8,128)S(1)} %copy-done.2, f32[64,128]{1,0:T(8,128)S(1)} %collective-permute-done.west, ...), custom_call_target="tpu_custom_call", output_to_operand_aliasing={{0}: (0, {})} | custom-call | flops 4000000 | bytes 6000000 | tf_op jit(solution)/shard_map/while/body/eval_jaxpr/pallas_call | solution.py:69
  160.1 4.4 %all-to-all-done.got = f32[32,40,128]{2,1,0:T(8,128)S(1)} async-done(((f32[32,40,128]{2,1,0:T(8,128)}), f32[32,40,128]{2,1,0:T(8,128)S(1)}, u32[]{:S(2)}, u32[]{:S(2)}) %all-to-all-start) | async-done | bytes 655392 | tf_op jit(solution)/shard_map/while/body/eval_jaxpr/all_to_all | solution.py:513
  164.5 3.1 %eval_jaxpr.7 = (f32[34,80,128]{2,1,0:T(8,128)S(1)}, f32[32,40,128]{2,1,0:T(8,128)}, f32[64,128]{1,0:T(8,128)S(1)}) custom-call(f32[32,40,128]{2,1,0:T(8,128)S(1)} %all-to-all-done.got, f32[34,80,128]{2,1,0:T(8,128)S(1)} %get-tuple-element.229.old, f32[64,128]{1,0:T(8,128)S(1)} %get-tuple-element.230.plain, ...), custom_call_target="tpu_custom_call", output_to_operand_aliasing={{0}: (1, {})} | custom-call | flops 4000000 | bytes 4000000 | tf_op jit(solution)/shard_map/while/body/eval_jaxpr/pallas_call | solution.py:69
  167.6 4.2 %all-to-all-start = ((f32[32,40,128]{2,1,0:T(8,128)}), f32[32,40,128]{2,1,0:T(8,128)S(1)}, u32[]{:S(2)}, u32[]{:S(2)}) async-start(f32[32,40,128]{2,1,0:T(8,128)} %get-tuple-element.249), calls=%async_computation | async-start | bytes 1310720 | tf_op jit(solution)/shard_map/while/body/eval_jaxpr/all_to_all | solution.py:513
  177.6 2.6 %eval_jaxpr.6 = (f32[34,80,128]{2,1,0:T(8,128)S(1)}, f32[64,128]{1,0:T(8,128)S(1)}) custom-call(f32[34,80,128]{2,1,0:T(8,128)S(1)} %get-tuple-element.247.solid.old, f32[32,64,128]{2,1,0:T(8,128)S(1)} %copy-done.2, f32[64,128]{1,0:T(8,128)S(1)} %collective-permute-done.west, ...), custom_call_target="tpu_custom_call", output_to_operand_aliasing={{0}: (0, {})} | custom-call | flops 4000000 | bytes 6000000 | tf_op jit(solution)/shard_map/while/body/eval_jaxpr/pallas_call | solution.py:69
  180.3 4.4 %all-to-all-done.got = f32[32,40,128]{2,1,0:T(8,128)S(1)} async-done(((f32[32,40,128]{2,1,0:T(8,128)}), f32[32,40,128]{2,1,0:T(8,128)S(1)}, u32[]{:S(2)}, u32[]{:S(2)}) %all-to-all-start) | async-done | bytes 655392 | tf_op jit(solution)/shard_map/while/body/eval_jaxpr/all_to_all | solution.py:513
  184.7 3.1 %eval_jaxpr.7 = (f32[34,80,128]{2,1,0:T(8,128)S(1)}, f32[32,40,128]{2,1,0:T(8,128)}, f32[64,128]{1,0:T(8,128)S(1)}) custom-call(f32[32,40,128]{2,1,0:T(8,128)S(1)} %all-to-all-done.got, f32[34,80,128]{2,1,0:T(8,128)S(1)} %get-tuple-element.229.old, f32[64,128]{1,0:T(8,128)S(1)} %get-tuple-element.230.plain, ...), custom_call_target="tpu_custom_call", output_to_operand_aliasing={{0}: (1, {})} | custom-call | flops 4000000 | bytes 4000000 | tf_op jit(solution)/shard_map/while/body/eval_jaxpr/pallas_call | solution.py:69
  187.8 4.2 %all-to-all-start.2 = ((f32[32,40,128]{2,1,0:T(8,128)}), f32[32,40,128]{2,1,0:T(8,128)S(1)}, u32[]{:S(2)}, u32[]{:S(2)}) async-start(f32[32,40,128]{2,1,0:T(8,128)} %get-tuple-element.107), calls=%async_computation.2 | async-start | bytes 1310720 | tf_op jit(solution)/shard_map/all_to_all | solution.py:513
  195.6 2.2 collective-permute-done.3.east
  197.9 2.6 %shard_map.91 = (f32[34,80,128]{2,1,0:T(8,128)S(1)}, f32[64,128]{1,0:T(8,128)S(1)}) custom-call(f32[34,80,128]{2,1,0:T(8,128)S(1)} %get-tuple-element.108.solid.old, f32[32,64,128]{2,1,0:T(8,128)S(1)} %copy-done.3, f32[64,128]{1,0:T(8,128)S(1)} %collective-permute-done.2.west, ...), custom_call_target="tpu_custom_call", output_to_operand_aliasing={{0}: (0, {})} | custom-call | flops 4000000 | bytes 6000000 | tf_op jit(solution)/shard_map/pallas_call | solution.py:69
  200.5 4.4 %all-to-all-done.2.got = f32[32,40,128]{2,1,0:T(8,128)S(1)} async-done(((f32[32,40,128]{2,1,0:T(8,128)}), f32[32,40,128]{2,1,0:T(8,128)S(1)}, u32[]{:S(2)}, u32[]{:S(2)}) %all-to-all-start.2) | async-done | bytes 655392 | tf_op jit(solution)/shard_map/all_to_all | solution.py:513
  204.9 3.2 %shard_map.92 = (f32[34,80,128]{2,1,0:T(8,128)S(1)}, f32[32,56,128]{2,1,0:T(8,128)}, f32[64,128]{1,0:T(8,128)S(1)}) custom-call(f32[32,40,128]{2,1,0:T(8,128)S(1)} %all-to-all-done.2.got, f32[34,80,128]{2,1,0:T(8,128)S(1)} %get-tuple-element.114.old, f32[64,128]{1,0:T(8,128)S(1)} %get-tuple-element.115.plain, ...), custom_call_target="tpu_custom_call", output_to_operand_aliasing={{0}: (1, {})} | custom-call | flops 4000000 | bytes 4000000 | tf_op jit(solution)/shard_map/pallas_call | solution.py:69
  208.2 4.2 %all-to-all-start.3 = ((f32[32,56,128]{2,1,0:T(8,128)}), f32[32,56,128]{2,1,0:T(8,128)S(1)}, u32[]{:S(2)}, u32[]{:S(2)}) async-start(f32[32,56,128]{2,1,0:T(8,128)} %get-tuple-element.116), calls=%async_computation.3 | async-start | bytes 1835008 | tf_op jit(solution)/shard_map/all_to_all | solution.py:513
  218.2 3.3 %shard_map.95 = (f32[34,80,128]{2,1,0:T(8,128)S(1)}, f32[64,128]{1,0:T(8,128)}) custom-call(f32[34,80,128]{2,1,0:T(8,128)S(1)} %get-tuple-element.117.solid.old, f32[32,64,128]{2,1,0:T(8,128)S(1)} %copy-done.4, f32[64,128]{1,0:T(8,128)S(1)} %collective-permute-done.4.west, ...), custom_call_target="tpu_custom_call", output_to_operand_aliasing={{0}: (0, {})} | custom-call | flops 4000000 | bytes 6000000 | tf_op jit(solution)/shard_map/pallas_call | solution.py:69
  221.5 6.7 %all-to-all-done.3.got = f32[32,56,128]{2,1,0:T(8,128)S(1)} async-done(((f32[32,56,128]{2,1,0:T(8,128)}), f32[32,56,128]{2,1,0:T(8,128)S(1)}, u32[]{:S(2)}, u32[]{:S(2)}) %all-to-all-start.3) | async-done | bytes 917536 | tf_op jit(solution)/shard_map/all_to_all | solution.py:513
  228.2 3.7 %shard_map.96 = (f32[34,80,128]{2,1,0:T(8,128)S(1)}, f32[32,64,128]{2,1,0:T(8,128)}, f32[16,2048]{1,0:T(8,128)}) custom-call(f32[32,56,128]{2,1,0:T(8,128)S(1)} %all-to-all-done.3.got, f32[34,80,128]{2,1,0:T(8,128)S(1)} %get-tuple-element.123.old, bf16[256,512]{1,0:T(8,128)(2,1)S(1)} %copy-done.1, ...), custom_call_target="tpu_custom_call", output_to_operand_aliasing={{0}: (1, {})} | custom-call | tf_op jit(solution)/shard_map/pallas_call | solution.py:69
  (93 shorter events, 53.8 us)
Async XLA Ops:
  0.6 12.4 %copy-start.8 = (f32[16]{0:T(128)S(1)}, f32[16]{0:T(128)}, u32[]{:S(2)}) copy-start(f32[16]{0:T(128)} %param.13) | copy-start | bytes 196
  0.6 12.4 %copy-start.9 = (f32[16]{0:T(128)S(1)}, f32[16]{0:T(128)}, u32[]{:S(2)}) copy-start(f32[16]{0:T(128)} %param.12) | copy-start | bytes 196
  3.2 17.9 %all-to-all-start.1 = ((f32[32,24,128]{2,1,0:T(8,128)}), f32[32,24,128]{2,1,0:T(8,128)S(1)}, u32[]{:S(2)}, u32[]{:S(2)}) async-start(f32[32,24,128]{2,1,0:T(8,128)} %get-tuple-element.99), calls=%async_computation.1 | async-start | bytes 786432 | tf_op jit(solution)/shard_map/all_to_all | solution.py:513
  24.2 17.0 %all-to-all-start = ((f32[32,40,128]{2,1,0:T(8,128)}), f32[32,40,128]{2,1,0:T(8,128)S(1)}, u32[]{:S(2)}, u32[]{:S(2)}) async-start(f32[32,40,128]{2,1,0:T(8,128)} %get-tuple-element.249), calls=%async_computation | async-start | bytes 1310720 | tf_op jit(solution)/shard_map/while/body/eval_jaxpr/all_to_all | solution.py:513
  28.2 4.0 %collective-permute-start = (f32[64,128]{1,0:T(8,128)S(1)}, f32[64,128]{1,0:T(8,128)S(1)}, u32[]{:S(2)}, u32[]{:S(2)}) collective-permute-start(f32[64,128]{1,0:T(8,128)S(1)} %get-tuple-element.227), channel_id=1, source_target_pairs={{0,1},{1,2},{2,3},{3,4},{4,5},{5,6},{6,7},{7,0},{8,9},{9,10},{10,1... | collective-permute-start | bytes 98312 | tf_op jit(solution)/shard_map/while/body/eval_jaxpr/ppermute | solution.py:571
  31.8 4.3 %collective-permute-start.1 = (f32[64,128]{1,0:T(8,128)S(1)}, f32[64,128]{1,0:T(8,128)S(1)}, u32[]{:S(2)}, u32[]{:S(2)}) collective-permute-start(f32[64,128]{1,0:T(8,128)S(1)} %get-tuple-element.227), channel_id=1, source_target_pairs={{0,7},{1,0},{2,1},{3,2},{4,3},{5,4},{6,5},{7,6},{8,15},{9,8},{10,9... | collective-permute-start | bytes 98312 | tf_op jit(solution)/shard_map/while/body/eval_jaxpr/ppermute | solution.py:574
  31.9 4.3 %copy-start.2 = (f32[32,64,128]{2,1,0:T(8,128)S(1)}, f32[32,64,128]{2,1,0:T(8,128)}, u32[]{:S(2)}) copy-start(f32[32,64,128]{2,1,0:T(8,128)} %get-tuple-element.265.heat) | copy-start | bytes 3145732 | tf_op jit(solution)/shard_map/while
  44.3 19.1 %all-to-all-start = ((f32[32,40,128]{2,1,0:T(8,128)}), f32[32,40,128]{2,1,0:T(8,128)S(1)}, u32[]{:S(2)}, u32[]{:S(2)}) async-start(f32[32,40,128]{2,1,0:T(8,128)} %get-tuple-element.249), calls=%async_computation | async-start | bytes 1310720 | tf_op jit(solution)/shard_map/while/body/eval_jaxpr/all_to_all | solution.py:513
  50.5 2.9 %collective-permute-start = (f32[64,128]{1,0:T(8,128)S(1)}, f32[64,128]{1,0:T(8,128)S(1)}, u32[]{:S(2)}, u32[]{:S(2)}) collective-permute-start(f32[64,128]{1,0:T(8,128)S(1)} %get-tuple-element.227), channel_id=1, source_target_pairs={{0,1},{1,2},{2,3},{3,4},{4,5},{5,6},{6,7},{7,0},{8,9},{9,10},{10,1... | collective-permute-start | bytes 98312 | tf_op jit(solution)/shard_map/while/body/eval_jaxpr/ppermute | solution.py:571
  52.0 4.3 %collective-permute-start.1 = (f32[64,128]{1,0:T(8,128)S(1)}, f32[64,128]{1,0:T(8,128)S(1)}, u32[]{:S(2)}, u32[]{:S(2)}) collective-permute-start(f32[64,128]{1,0:T(8,128)S(1)} %get-tuple-element.227), channel_id=1, source_target_pairs={{0,7},{1,0},{2,1},{3,2},{4,3},{5,4},{6,5},{7,6},{8,15},{9,8},{10,9... | collective-permute-start | bytes 98312 | tf_op jit(solution)/shard_map/while/body/eval_jaxpr/ppermute | solution.py:574
  52.8 3.5 %copy-start.2 = (f32[32,64,128]{2,1,0:T(8,128)S(1)}, f32[32,64,128]{2,1,0:T(8,128)}, u32[]{:S(2)}) copy-start(f32[32,64,128]{2,1,0:T(8,128)} %get-tuple-element.265.heat) | copy-start | bytes 3145732 | tf_op jit(solution)/shard_map/while
  66.5 17.1 %all-to-all-start = ((f32[32,40,128]{2,1,0:T(8,128)}), f32[32,40,128]{2,1,0:T(8,128)S(1)}, u32[]{:S(2)}, u32[]{:S(2)}) async-start(f32[32,40,128]{2,1,0:T(8,128)} %get-tuple-element.249), calls=%async_computation | async-start | bytes 1310720 | tf_op jit(solution)/shard_map/while/body/eval_jaxpr/all_to_all | solution.py:513
  70.7 2.9 %collective-permute-start = (f32[64,128]{1,0:T(8,128)S(1)}, f32[64,128]{1,0:T(8,128)S(1)}, u32[]{:S(2)}, u32[]{:S(2)}) collective-permute-start(f32[64,128]{1,0:T(8,128)S(1)} %get-tuple-element.227), channel_id=1, source_target_pairs={{0,1},{1,2},{2,3},{3,4},{4,5},{5,6},{6,7},{7,0},{8,9},{9,10},{10,1... | collective-permute-start | bytes 98312 | tf_op jit(solution)/shard_map/while/body/eval_jaxpr/ppermute | solution.py:571
  72.2 4.3 %collective-permute-start.1 = (f32[64,128]{1,0:T(8,128)S(1)}, f32[64,128]{1,0:T(8,128)S(1)}, u32[]{:S(2)}, u32[]{:S(2)}) collective-permute-start(f32[64,128]{1,0:T(8,128)S(1)} %get-tuple-element.227), channel_id=1, source_target_pairs={{0,7},{1,0},{2,1},{3,2},{4,3},{5,4},{6,5},{7,6},{8,15},{9,8},{10,9... | collective-permute-start | bytes 98312 | tf_op jit(solution)/shard_map/while/body/eval_jaxpr/ppermute | solution.py:574
  73.0 3.5 %copy-start.2 = (f32[32,64,128]{2,1,0:T(8,128)S(1)}, f32[32,64,128]{2,1,0:T(8,128)}, u32[]{:S(2)}) copy-start(f32[32,64,128]{2,1,0:T(8,128)} %get-tuple-element.265.heat) | copy-start | bytes 3145732 | tf_op jit(solution)/shard_map/while
  86.7 17.1 %all-to-all-start = ((f32[32,40,128]{2,1,0:T(8,128)}), f32[32,40,128]{2,1,0:T(8,128)S(1)}, u32[]{:S(2)}, u32[]{:S(2)}) async-start(f32[32,40,128]{2,1,0:T(8,128)} %get-tuple-element.249), calls=%async_computation | async-start | bytes 1310720 | tf_op jit(solution)/shard_map/while/body/eval_jaxpr/all_to_all | solution.py:513
  90.9 2.9 %collective-permute-start = (f32[64,128]{1,0:T(8,128)S(1)}, f32[64,128]{1,0:T(8,128)S(1)}, u32[]{:S(2)}, u32[]{:S(2)}) collective-permute-start(f32[64,128]{1,0:T(8,128)S(1)} %get-tuple-element.227), channel_id=1, source_target_pairs={{0,1},{1,2},{2,3},{3,4},{4,5},{5,6},{6,7},{7,0},{8,9},{9,10},{10,1... | collective-permute-start | bytes 98312 | tf_op jit(solution)/shard_map/while/body/eval_jaxpr/ppermute | solution.py:571
  92.4 4.3 %collective-permute-start.1 = (f32[64,128]{1,0:T(8,128)S(1)}, f32[64,128]{1,0:T(8,128)S(1)}, u32[]{:S(2)}, u32[]{:S(2)}) collective-permute-start(f32[64,128]{1,0:T(8,128)S(1)} %get-tuple-element.227), channel_id=1, source_target_pairs={{0,7},{1,0},{2,1},{3,2},{4,3},{5,4},{6,5},{7,6},{8,15},{9,8},{10,9... | collective-permute-start | bytes 98312 | tf_op jit(solution)/shard_map/while/body/eval_jaxpr/ppermute | solution.py:574
  93.2 3.5 %copy-start.2 = (f32[32,64,128]{2,1,0:T(8,128)S(1)}, f32[32,64,128]{2,1,0:T(8,128)}, u32[]{:S(2)}) copy-start(f32[32,64,128]{2,1,0:T(8,128)} %get-tuple-element.265.heat) | copy-start | bytes 3145732 | tf_op jit(solution)/shard_map/while
  106.9 17.1 %all-to-all-start = ((f32[32,40,128]{2,1,0:T(8,128)}), f32[32,40,128]{2,1,0:T(8,128)S(1)}, u32[]{:S(2)}, u32[]{:S(2)}) async-start(f32[32,40,128]{2,1,0:T(8,128)} %get-tuple-element.249), calls=%async_computation | async-start | bytes 1310720 | tf_op jit(solution)/shard_map/while/body/eval_jaxpr/all_to_all | solution.py:513
  111.2 2.9 %collective-permute-start = (f32[64,128]{1,0:T(8,128)S(1)}, f32[64,128]{1,0:T(8,128)S(1)}, u32[]{:S(2)}, u32[]{:S(2)}) collective-permute-start(f32[64,128]{1,0:T(8,128)S(1)} %get-tuple-element.227), channel_id=1, source_target_pairs={{0,1},{1,2},{2,3},{3,4},{4,5},{5,6},{6,7},{7,0},{8,9},{9,10},{10,1... | collective-permute-start | bytes 98312 | tf_op jit(solution)/shard_map/while/body/eval_jaxpr/ppermute | solution.py:571
  112.6 4.3 %collective-permute-start.1 = (f32[64,128]{1,0:T(8,128)S(1)}, f32[64,128]{1,0:T(8,128)S(1)}, u32[]{:S(2)}, u32[]{:S(2)}) collective-permute-start(f32[64,128]{1,0:T(8,128)S(1)} %get-tuple-element.227), channel_id=1, source_target_pairs={{0,7},{1,0},{2,1},{3,2},{4,3},{5,4},{6,5},{7,6},{8,15},{9,8},{10,9... | collective-permute-start | bytes 98312 | tf_op jit(solution)/shard_map/while/body/eval_jaxpr/ppermute | solution.py:574
  113.4 3.5 %copy-start.2 = (f32[32,64,128]{2,1,0:T(8,128)S(1)}, f32[32,64,128]{2,1,0:T(8,128)}, u32[]{:S(2)}) copy-start(f32[32,64,128]{2,1,0:T(8,128)} %get-tuple-element.265.heat) | copy-start | bytes 3145732 | tf_op jit(solution)/shard_map/while
  127.2 17.1 %all-to-all-start = ((f32[32,40,128]{2,1,0:T(8,128)}), f32[32,40,128]{2,1,0:T(8,128)S(1)}, u32[]{:S(2)}, u32[]{:S(2)}) async-start(f32[32,40,128]{2,1,0:T(8,128)} %get-tuple-element.249), calls=%async_computation | async-start | bytes 1310720 | tf_op jit(solution)/shard_map/while/body/eval_jaxpr/all_to_all | solution.py:513
  131.4 2.9 %collective-permute-start = (f32[64,128]{1,0:T(8,128)S(1)}, f32[64,128]{1,0:T(8,128)S(1)}, u32[]{:S(2)}, u32[]{:S(2)}) collective-permute-start(f32[64,128]{1,0:T(8,128)S(1)} %get-tuple-element.227), channel_id=1, source_target_pairs={{0,1},{1,2},{2,3},{3,4},{4,5},{5,6},{6,7},{7,0},{8,9},{9,10},{10,1... | collective-permute-start | bytes 98312 | tf_op jit(solution)/shard_map/while/body/eval_jaxpr/ppermute | solution.py:571
  132.9 4.3 %collective-permute-start.1 = (f32[64,128]{1,0:T(8,128)S(1)}, f32[64,128]{1,0:T(8,128)S(1)}, u32[]{:S(2)}, u32[]{:S(2)}) collective-permute-start(f32[64,128]{1,0:T(8,128)S(1)} %get-tuple-element.227), channel_id=1, source_target_pairs={{0,7},{1,0},{2,1},{3,2},{4,3},{5,4},{6,5},{7,6},{8,15},{9,8},{10,9... | collective-permute-start | bytes 98312 | tf_op jit(solution)/shard_map/while/body/eval_jaxpr/ppermute | solution.py:574
  133.7 3.5 %copy-start.2 = (f32[32,64,128]{2,1,0:T(8,128)S(1)}, f32[32,64,128]{2,1,0:T(8,128)}, u32[]{:S(2)}) copy-start(f32[32,64,128]{2,1,0:T(8,128)} %get-tuple-element.265.heat) | copy-start | bytes 3145732 | tf_op jit(solution)/shard_map/while
  147.4 17.1 %all-to-all-start = ((f32[32,40,128]{2,1,0:T(8,128)}), f32[32,40,128]{2,1,0:T(8,128)S(1)}, u32[]{:S(2)}, u32[]{:S(2)}) async-start(f32[32,40,128]{2,1,0:T(8,128)} %get-tuple-element.249), calls=%async_computation | async-start | bytes 1310720 | tf_op jit(solution)/shard_map/while/body/eval_jaxpr/all_to_all | solution.py:513
  151.6 2.9 %collective-permute-start = (f32[64,128]{1,0:T(8,128)S(1)}, f32[64,128]{1,0:T(8,128)S(1)}, u32[]{:S(2)}, u32[]{:S(2)}) collective-permute-start(f32[64,128]{1,0:T(8,128)S(1)} %get-tuple-element.227), channel_id=1, source_target_pairs={{0,1},{1,2},{2,3},{3,4},{4,5},{5,6},{6,7},{7,0},{8,9},{9,10},{10,1... | collective-permute-start | bytes 98312 | tf_op jit(solution)/shard_map/while/body/eval_jaxpr/ppermute | solution.py:571
  153.1 4.3 %collective-permute-start.1 = (f32[64,128]{1,0:T(8,128)S(1)}, f32[64,128]{1,0:T(8,128)S(1)}, u32[]{:S(2)}, u32[]{:S(2)}) collective-permute-start(f32[64,128]{1,0:T(8,128)S(1)} %get-tuple-element.227), channel_id=1, source_target_pairs={{0,7},{1,0},{2,1},{3,2},{4,3},{5,4},{6,5},{7,6},{8,15},{9,8},{10,9... | collective-permute-start | bytes 98312 | tf_op jit(solution)/shard_map/while/body/eval_jaxpr/ppermute | solution.py:574
  153.9 3.5 %copy-start.2 = (f32[32,64,128]{2,1,0:T(8,128)S(1)}, f32[32,64,128]{2,1,0:T(8,128)}, u32[]{:S(2)}) copy-start(f32[32,64,128]{2,1,0:T(8,128)} %get-tuple-element.265.heat) | copy-start | bytes 3145732 | tf_op jit(solution)/shard_map/while
  167.6 17.1 %all-to-all-start = ((f32[32,40,128]{2,1,0:T(8,128)}), f32[32,40,128]{2,1,0:T(8,128)S(1)}, u32[]{:S(2)}, u32[]{:S(2)}) async-start(f32[32,40,128]{2,1,0:T(8,128)} %get-tuple-element.249), calls=%async_computation | async-start | bytes 1310720 | tf_op jit(solution)/shard_map/while/body/eval_jaxpr/all_to_all | solution.py:513
  171.8 2.9 %collective-permute-start = (f32[64,128]{1,0:T(8,128)S(1)}, f32[64,128]{1,0:T(8,128)S(1)}, u32[]{:S(2)}, u32[]{:S(2)}) collective-permute-start(f32[64,128]{1,0:T(8,128)S(1)} %get-tuple-element.227), channel_id=1, source_target_pairs={{0,1},{1,2},{2,3},{3,4},{4,5},{5,6},{6,7},{7,0},{8,9},{9,10},{10,1... | collective-permute-start | bytes 98312 | tf_op jit(solution)/shard_map/while/body/eval_jaxpr/ppermute | solution.py:571
  173.3 4.3 %collective-permute-start.1 = (f32[64,128]{1,0:T(8,128)S(1)}, f32[64,128]{1,0:T(8,128)S(1)}, u32[]{:S(2)}, u32[]{:S(2)}) collective-permute-start(f32[64,128]{1,0:T(8,128)S(1)} %get-tuple-element.227), channel_id=1, source_target_pairs={{0,7},{1,0},{2,1},{3,2},{4,3},{5,4},{6,5},{7,6},{8,15},{9,8},{10,9... | collective-permute-start | bytes 98312 | tf_op jit(solution)/shard_map/while/body/eval_jaxpr/ppermute | solution.py:574
  174.1 3.5 %copy-start.2 = (f32[32,64,128]{2,1,0:T(8,128)S(1)}, f32[32,64,128]{2,1,0:T(8,128)}, u32[]{:S(2)}) copy-start(f32[32,64,128]{2,1,0:T(8,128)} %get-tuple-element.265.heat) | copy-start | bytes 3145732 | tf_op jit(solution)/shard_map/while
  187.8 5.7 %copy-start.6 = (bf16[2,512,128]{2,1,0:T(8,128)(2,1)}, bf16[2,512,128]{2,1,0:T(8,128)(2,1)S(1)}, u32[]{:S(2)}) copy-start(bf16[2,512,128]{2,1,0:T(8,128)(2,1)S(1)} %get-tuple-element.287) | copy-start | bytes 786436
  187.8 17.1 %all-to-all-start.2 = ((f32[32,40,128]{2,1,0:T(8,128)}), f32[32,40,128]{2,1,0:T(8,128)S(1)}, u32[]{:S(2)}, u32[]{:S(2)}) async-start(f32[32,40,128]{2,1,0:T(8,128)} %get-tuple-element.107), calls=%async_computation.2 | async-start | bytes 1310720 | tf_op jit(solution)/shard_map/all_to_all | solution.py:513
  192.0 2.9 %collective-permute-start.2 = (f32[64,128]{1,0:T(8,128)S(1)}, f32[64,128]{1,0:T(8,128)S(1)}, u32[]{:S(2)}, u32[]{:S(2)}) collective-permute-start(f32[64,128]{1,0:T(8,128)S(1)} %get-tuple-element.112), channel_id=1, source_target_pairs={{0,1},{1,2},{2,3},{3,4},{4,5},{5,6},{6,7},{7,0},{8,9},{9,10},{10,1... | collective-permute-start | bytes 98312 | tf_op jit(solution)/shard_map/ppermute | solution.py:571
  193.5 4.4 %copy-start.3 = (f32[32,64,128]{2,1,0:T(8,128)S(1)}, f32[32,64,128]{2,1,0:T(8,128)}, u32[]{:S(2)}) copy-start(f32[32,64,128]{2,1,0:T(8,128)} %get-tuple-element.284) | copy-start | bytes 3145732
  193.5 4.3 %collective-permute-start.3 = (f32[64,128]{1,0:T(8,128)S(1)}, f32[64,128]{1,0:T(8,128)S(1)}, u32[]{:S(2)}, u32[]{:S(2)}) collective-permute-start(f32[64,128]{1,0:T(8,128)S(1)} %get-tuple-element.112), channel_id=1, source_target_pairs={{0,7},{1,0},{2,1},{3,2},{4,3},{5,4},{6,5},{7,6},{8,15},{9,8},{10,9... | collective-permute-start | bytes 98312 | tf_op jit(solution)/shard_map/ppermute | solution.py:574
  208.2 20.0 %all-to-all-start.3 = ((f32[32,56,128]{2,1,0:T(8,128)}), f32[32,56,128]{2,1,0:T(8,128)S(1)}, u32[]{:S(2)}, u32[]{:S(2)}) async-start(f32[32,56,128]{2,1,0:T(8,128)} %get-tuple-element.116), calls=%async_computation.3 | async-start | bytes 1835008 | tf_op jit(solution)/shard_map/all_to_all | solution.py:513
  212.4 3.0 %collective-permute-start.4 = (f32[64,128]{1,0:T(8,128)S(1)}, f32[64,128]{1,0:T(8,128)S(1)}, u32[]{:S(2)}, u32[]{:S(2)}) collective-permute-start(f32[64,128]{1,0:T(8,128)S(1)} %get-tuple-element.121), channel_id=1, source_target_pairs={{0,1},{1,2},{2,3},{3,4},{4,5},{5,6},{6,7},{7,0},{8,9},{9,10},{10,1... | collective-permute-start | bytes 98312 | tf_op jit(solution)/shard_map/ppermute | solution.py:571
  213.9 4.4 %copy-start.4 = (f32[32,64,128]{2,1,0:T(8,128)S(1)}, f32[32,64,128]{2,1,0:T(8,128)}, u32[]{:S(2)}) copy-start(f32[32,64,128]{2,1,0:T(8,128)} %get-tuple-element.284) | copy-start | bytes 3145732
  213.9 4.3 %collective-permute-start.5 = (f32[64,128]{1,0:T(8,128)S(1)}, f32[64,128]{1,0:T(8,128)S(1)}, u32[]{:S(2)}, u32[]{:S(2)}) collective-permute-start(f32[64,128]{1,0:T(8,128)S(1)} %get-tuple-element.121), channel_id=1, source_target_pairs={{0,7},{1,0},{2,1},{3,2},{4,3},{5,4},{6,5},{7,6},{8,15},{9,8},{10,9... | collective-permute-start | bytes 98312 | tf_op jit(solution)/shard_map/ppermute | solution.py:574
  216.1 12.1 %copy-start = (f32[16,2048]{1,0:T(8,128)S(1)}, f32[16,2048]{1,0:T(8,128)}, u32[]{:S(2)}) copy-start(f32[16,2048]{1,0:T(8,128)} %cond_hbm.3) | copy-start | bytes 393220
  216.1 12.1 %copy-start.1 = (bf16[256,512]{1,0:T(8,128)(2,1)S(1)}, bf16[256,512]{1,0:T(8,128)(2,1)}, u32[]{:S(2)}) copy-start(bf16[256,512]{1,0:T(8,128)(2,1)} %get-tuple-element.124.place_hbm) | copy-start | bytes 786436
  216.1 12.1 %copy-start.5 = (f32[15,2,32,128]{3,2,1,0:T(8,128)S(1)}, f32[15,2,32,128]{3,2,1,0:T(8,128)}, u32[]{:S(2)}) copy-start(f32[15,2,32,128]{3,2,1,0:T(8,128)} %get-tuple-element.286) | copy-start | bytes 1474564
  218.2 9.9 %copy-start.7 = (bf16[2,512,128]{2,1,0:T(8,128)(2,1)S(1)}, bf16[2,512,128]{2,1,0:T(8,128)(2,1)}, u32[]{:S(2)}) copy-start(bf16[2,512,128]{2,1,0:T(8,128)(2,1)} %copy-done.6) | copy-start | bytes 786436

commit v4 on v3

--- a/solution.py
+++ b/solution.py
@@ -147,14 +147,12 @@
 def outer_kernel(solid_hbm, solid, cols, sems):
     copies = Copies(sems)
     nz, nx, ny = solid_hbm.shape
-    inner = pl.ds(8, nx)
+    inner = pl.ds(0, nx)
     copies.start(solid_hbm, solid.at[pl.ds(1, nz), inner, :]).wait()
     lane = iota((nx, ny), 1)
     ends = jnp.where(lane < nz, 0, ny - 1)
     solid[0, inner, :] = jnp.zeros((nx, ny), F32)
     solid[nz + 1, inner, :] = jnp.zeros((nx, ny), F32)
-    solid[pl.ds(1, nz), 7, :] = jnp.zeros((nz, ny), F32)
-    solid[pl.ds(1, nz), 8 + nx, :] = jnp.zeros((nz, ny), F32)
     unroll = 4
 
     def some(i, found):
@@ -174,7 +172,7 @@
     copies = Copies(sems)
     for copy in [copies.start(got_hbm, got), copies.start(const_hbm, const)]:
         copy.wait()
-    bottom = solid[1, pl.ds(8, hit.shape[0]), :]
+    bottom = solid[1]
     n_flow = got.shape[0]
     slots = n_flow * SLOTS
     block_rows = bottom.shape[0]
@@ -262,9 +260,9 @@
 
 def send_message(copies, solid, msg, edges, msg_hbm):
     n_flow, me = msg.shape[0], lax.axis_index("flow")
-    nz, nx = edges.shape[1], solid.shape[1] - 16
-    edges[0] = solid[pl.ds(1, nz), 8, :]
-    edges[1] = solid[pl.ds(1, nz), 7 + nx, :]
+    nz, nx = edges.shape[1], solid.shape[1]
+    edges[0] = solid[pl.ds(1, nz), 0, :]
+    edges[1] = solid[pl.ds(1, nz), nx - 1, :]
     rows = pl.ds(TILE, nz)
     return [
         copies.start(edges.at[0], msg_hbm.at[lax.rem(me + n_flow - 1, n_flow), rows, :]),
@@ -275,15 +273,15 @@
 
 def add_outer_rows(solid, got):
     n_flow, me = lax.axis_size("flow"), lax.axis_index("flow")
-    nz, nx = solid.shape[0] - 2, solid.shape[1] - 16
+    nz, nx = solid.shape[0] - 2, solid.shape[1]
     rows = pl.ds(TILE, nz)
     north = got[lax.rem(me + n_flow - 1, n_flow), rows, :]
     south = got[lax.rem(me + 1, n_flow), rows, :]
     north = jnp.where(me > 0, KAPPA * north, 0.0)
     south = jnp.where(me < n_flow - 1, KAPPA * south, 0.0)
     layers = pl.ds(1, nz)
-    solid[layers, 8, :] = solid[layers, 8, :] + north
-    solid[layers, 7 + nx, :] = solid[layers, 7 + nx, :] + south
+    solid[layers, 0, :] = solid[layers, 0, :] + north
+    solid[layers, nx - 1, :] = solid[layers, nx - 1, :] + south
     return north, south
 
 
@@ -292,7 +290,7 @@
     slots = flux.shape[1]
     piece = slots // 2
     nx, ny = sink.shape
-    bottom = solid[1, pl.ds(8, nx), :]
+    bottom = solid[1]
     padded = jnp.concatenate([bottom, jnp.zeros((LANES - nx, ny), F32)], axis=0)
     wide = jnp.concatenate(parts(padded, 3), axis=1)
     earlier = (iota((LANES, LANES), 0) < iota((LANES, LANES), 1)).astype(F32).astype(BF16)
@@ -319,9 +317,10 @@
     del old
     nz, nx, ny = heat.shape
     del sems
-    inner = pl.ds(8, nx)
+    inner = pl.ds(0, nx)
     lot, n_span = lax.axis_index("span"), lax.axis_size("span")
     lane = iota((nx, ny), 1)
+    sub = iota((nx, ny), 0)
     border = (lane == 0) | (lane == ny - 1)
     ends = jnp.where(lane < nz, 0, ny - 1)
     halo = jnp.where((lane < nz) & (lot < n_span - 1), east[...], 0.0)
@@ -336,7 +335,9 @@
             side = pick(halo, jnp.where(lane == 0, nz, 0) + z)
             right, left = pltpu.roll(mid, 1, 1), pltpu.roll(mid, ny - 1, 1)
             across = jnp.where(border, side + jnp.where(lane == 0, left, right), left + right)
-            total = across + (solid[z + 1, pl.ds(7, nx), :] + solid[z + 1, pl.ds(9, nx), :])
+            above = jnp.where(sub == 0, 0.0, pltpu.roll(mid, 1, 0))
+            below = jnp.where(sub == nx - 1, 0.0, pltpu.roll(mid, nx - 1, 0))
+            total = across + (above + below)
             total = total + (low + solid[z + 2, inner, :])
             new = mid + KAPPA * (total - 6.0 * mid) + heat[z]
             solid[z + 1, inner, :] = new
@@ -349,14 +350,7 @@
     solid[1, inner, :] = solid[1, inner, :] - sink[...]
 
 
-def take_scan(copies, scan_hbm, scan):
-    places, gains = pl.ds(12, 3), pl.ds(0, 12)
-    return [
-        copies.start(scan_hbm.at[rows], scan.at[rows]) for rows in (places, gains)
-    ]
-
-
-def entering(got, scan, gains):
+def entering(got, scan):
     n_flow = got.shape[0]
     ends = [[], []]
     for g in range(n_flow // TILE):
@@ -370,7 +364,6 @@
                 acc[half] = jnp.where(origin[half] == float(o), pick(line, lanes[half]), acc[half])
         for half in range(2):
             ends[half].append(acc[half])
-    gains.wait()
     result = []
     sub, lane = iota((n_flow, LANES), 0), iota((n_flow, LANES), 1)
     for half in range(2):
@@ -408,20 +401,18 @@
 
 def after_kernel(
     last,
-    got, old, plain, scan_hbm, hit, reply_hbm, weight_hbm, hit_t,
+    got, old, plain, scan, hit, reply_hbm, weight_hbm, hit_t,
     solid, msg_hbm, cols,
-    scan, edges, msg, reply, weight, sems,
+    edges, msg, reply, weight, sems,
 ):
     del old
     copies = Copies(sems)
-    places, gains = take_scan(copies, scan_hbm, scan)
     come = [copies.start(reply_hbm, reply), copies.start(weight_hbm, weight)]
-    north, south = add_outer_rows(solid, got)
-    places.wait()
-    carry = hosted(entering(got, scan, gains), scan)
+    carry = hosted(entering(got, scan), scan)
     own_hit = hit[...]
     nx = own_hit.shape[0]
-    inner = pl.ds(8, nx)
+    inner = pl.ds(0, nx)
+    north, south = add_outer_rows(solid, got)
     come[0].wait()
     new = new_bottom(carry, solid[1, inner, :], own_hit, reply)
     solid[1, inner, :] = new
@@ -453,21 +444,19 @@
 
 
 def final_kernel(
-    got, old, place_hbm, cond_hbm, scan_hbm, hit, reply_hbm, solid, out_hbm, coolant_hbm,
-    scan, place, cond, reply, coolant, sems,
+    got, old, place_hbm, cond_hbm, scan, hit, reply_hbm, solid, out_hbm, coolant_hbm,
+    place, cond, reply, coolant, sems,
 ):
     copies = Copies(sems)
     nz, nx = out_hbm.shape[0], out_hbm.shape[1]
-    inner = pl.ds(8, nx)
+    inner = pl.ds(0, nx)
     del old
-    places, gains = take_scan(copies, scan_hbm, scan)
     come = copies.start(reply_hbm, reply)
     then = [copies.start(place_hbm, place), *load_segments(copies, cond_hbm, cond)]
     add_outer_rows(solid, got)
     upper = pl.ds(2, nz - 1)
     back = [copies.start(solid.at[upper, inner, :], out_hbm.at[pl.ds(1, nz - 1)])]
-    places.wait()
-    enter = entering(got, scan, gains)
+    enter = entering(got, scan)
     carry = hosted(enter, scan)
     come.wait()
     solid[1, inner, :] = new_bottom(carry, solid[1, inner, :], hit[...], reply)
@@ -526,7 +515,7 @@
         limit=WHOLE_VMEM,
     )
     got = exchange(pay)
-    room = spec((nz + 2, nx + 16, ny))
+    room = spec((nz + 2, nx, ny))
     solid, cols = call(
         outer_kernel, (solid_start,), (room, layer), (), 1, held_out=(0, 1), limit=WHOLE_VMEM
     )
@@ -595,12 +584,11 @@
             (got, solid, cols, scan, hit, reply, weight, hit_t),
             (room, long_spec if last else msg_spec, layer),
             (
-                scan_spec,
                 edges_spec, spec((n_flow, TILE + SLOTS, LANES)) if last else short_spec,
                 reply_spec, weight_spec,
             ),
-            8,
-            held=(0, 1, 2, 4, 7),
+            6,
+            held=(0, 1, 2, 3, 4, 7),
             held_out=(0, 2),
             flops=4_000_000,
             nbytes=4_000_000,
@@ -614,9 +602,9 @@
         final_kernel,
         (got, solid, place, conductance, scan, hit, reply),
         (room, block, spec((channels, stations))),
-        (scan_spec, place_spec, split, reply_spec, split),
-        6 + 2 * split.shape[1],
-        held=(0, 1, 5),
+        (place_spec, split, reply_spec, split),
+        4 + 2 * split.shape[1],
+        held=(0, 1, 4, 5),
         held_out=(0,),
         aliases={1: 0},
     )

time: 234 us -> 233 us (level)
  no operation moved by 1% of the time
where the time goes in v4:
time: 233 us; the launch traced here: 231 us
  waiting for transfers between devices  82.1 us (35%)
  Pallas kernels  78.1 us (34%)
  starting transfers between devices  69.2 us (30%)
    pallas_call x43, Pallas kernels, call(): pl.pallas_call(kernel, out_shape=outs, in_specs=[pl.BlockSpec(memory_spac...  78.1 us
    all_to_all x11, waiting for transfers between devices, exchange(): return lax.all_to_all(message, 'flow', 0, 0, tiled=True)  52.7 us
    all_to_all x11, starting transfers between devices, exchange(): return lax.all_to_all(message, 'flow', 0, 0, tiled=True)  51.6 us
    ppermute x10, waiting for transfers between devices, beside(): east = lax.ppermute(cols, 'span', down)  23.2 us
    ppermute x10, starting transfers between devices, beside(): west = lax.ppermute(cols, 'span', up)  10.2 us
    ppermute x10, starting transfers between devices, beside(): east = lax.ppermute(cols, 'span', down)  7.34 us
    ppermute x10, waiting for transfers between devices, beside(): west = lax.ppermute(cols, 'span', up)  6.24 us
  transfers between devices with their start and end apart: 31, of which 31 were waited for; matrix products, arithmetic and copies ran while one was open for 0% of the time, Pallas kernels for 18%

profile of v4, /device:TPU:97, one launch (start us, length us, event | category | flops | bytes accessed | tf_op | source)
XLA Modules:
  0.0 230.8 jit_solution(14418720023661268742)
XLA Ops:
  0.7 2.5 %shard_map.87 = (f32[32,24,128]{2,1,0:T(8,128)}, bf16[256,512]{1,0:T(8,128)(2,1)}) custom-call(s32[2,128]{1,0:T(2,128)} %bitcast.4, s32[2,128]{1,0:T(2,128)} %bitcast.5, f32[16,2048]{1,0:T(8,128)} %cond_hbm.3), custom_call_target="tpu_custom_call" | custom-call | tf_op jit(solution)/shard_map/pallas_call | solution.py:69
  3.2 7.8 %all-to-all-start.1 = ((f32[32,24,128]{2,1,0:T(8,128)}), f32[32,24,128]{2,1,0:T(8,128)S(1)}, u32[]{:S(2)}, u32[]{:S(2)}) async-start(f32[32,24,128]{2,1,0:T(8,128)} %get-tuple-element.99), calls=%async_computation.1 | async-start | bytes 786432 | tf_op jit(solution)/shard_map/all_to_all | solution.py:502
  13.0 8.1 %all-to-all-done.1.got_hbm = f32[32,24,128]{2,1,0:T(8,128)S(1)} async-done(((f32[32,24,128]{2,1,0:T(8,128)}), f32[32,24,128]{2,1,0:T(8,128)S(1)}, u32[]{:S(2)}, u32[]{:S(2)}) %all-to-all-start.1) | async-done | bytes 393248 | tf_op jit(solution)/shard_map/all_to_all | solution.py:502
  21.1 3.0 %shard_map.88 = (bf16[64,512]{1,0:T(8,128)(2,1)S(1)}, bf16[512,128]{1,0:T(8,128)(2,1)S(1)}, bf16[2,512,128]{2,1,0:T(8,128)(2,1)}, bf16[2,128,512]{2,1,0:T(8,128)...) custom-call(f32[32,24,128]{2,1,0:T(8,128)S(1)} %all-to-all-done.1.got_hbm, ...), custom_call_target="tpu_custom_call" | custom-call | tf_op jit(solution)/shard_map/pallas_call | solution.py:69
  24.1 163.0 %while.14 = (s32[]{:T(128)}, f32[34,64,128]{2,1,0:T(8,128)S(1)}, f32[64,128]{1,0:T(8,128)S(1)}, f32[32,40,128]{2,1,0:T(8,128)}, bf16[64,512]{1,0:T(8,128)(2,1)S(...) while((s32[]{:T(128)}, f32[34,64,128]{2,1,0:T(8,128)S(1)}, ...), condition=%wide.region_1.2_spmd, body=%wide.region_0.1_spmd.sunk | while | flops 10000002 | bytes 19422784 | solution.py:599
  24.1 3.9 %all-to-all-start = ((f32[32,40,128]{2,1,0:T(8,128)}), f32[32,40,128]{2,1,0:T(8,128)S(1)}, u32[]{:S(2)}, u32[]{:S(2)}) async-start(f32[32,40,128]{2,1,0:T(8,128)} %get-tuple-element.249), calls=%async_computation | async-start | bytes 1310720 | tf_op jit(solution)/shard_map/while/body/eval_jaxpr/all_to_all | solution.py:502
  28.1 2.9 %collective-permute-start = (f32[64,128]{1,0:T(8,128)S(1)}, f32[64,128]{1,0:T(8,128)S(1)}, u32[]{:S(2)}, u32[]{:S(2)}) collective-permute-start(f32[64,128]{1,0:T(8,128)S(1)} %get-tuple-element.227), channel_id=1, source_target_pairs={{0,1},{1,2},{2,3},{3,4},{4,5},{5,6},{6,7},{7,0},{8,9},{9,10},{10,1... | collective-permute-start | bytes 98312 | tf_op jit(solution)/shard_map/while/body/eval_jaxpr/ppermute | solution.py:560
  32.7 3.3 %collective-permute-done.1.east = f32[64,128]{1,0:T(8,128)S(1)} collective-permute-done((f32[64,128]{1,0:T(8,128)S(1)}, f32[64,128]{1,0:T(8,128)S(1)}, u32[]{:S(2)}, u32[]{:S(2)}) %collective-permute-start.1) | collective-permute-done | bytes 32800 | tf_op jit(solution)/shard_map/while/body/eval_jaxpr/ppermute | solution.py:563
  36.0 2.6 %eval_jaxpr.6 = (f32[34,64,128]{2,1,0:T(8,128)S(1)}, f32[64,128]{1,0:T(8,128)S(1)}) custom-call(f32[34,64,128]{2,1,0:T(8,128)S(1)} %get-tuple-element.247.solid.old, f32[32,64,128]{2,1,0:T(8,128)S(1)} %copy-done.2, f32[64,128]{1,0:T(8,128)S(1)} %collective-permute-done.west, ...), custom_call_target="tpu_custom_call", output_to_operand_aliasing={{0}: (0, {})} | custom-call | flops 4000000 | bytes 6000000 | tf_op jit(solution)/shard_map/while/body/eval_jaxpr/pallas_call | solution.py:69
  38.7 2.4 %all-to-all-done.got = f32[32,40,128]{2,1,0:T(8,128)S(1)} async-done(((f32[32,40,128]{2,1,0:T(8,128)}), f32[32,40,128]{2,1,0:T(8,128)S(1)}, u32[]{:S(2)}, u32[]{:S(2)}) %all-to-all-start) | async-done | bytes 655392 | tf_op jit(solution)/shard_map/while/body/eval_jaxpr/all_to_all | solution.py:502
  41.1 3.0 %eval_jaxpr.7 = (f32[34,64,128]{2,1,0:T(8,128)S(1)}, f32[32,40,128]{2,1,0:T(8,128)}, f32[64,128]{1,0:T(8,128)S(1)}) custom-call(f32[32,40,128]{2,1,0:T(8,128)S(1)} %all-to-all-done.got, f32[34,64,128]{2,1,0:T(8,128)S(1)} %get-tuple-element.229.old, f32[64,128]{1,0:T(8,128)S(1)} %get-tuple-element.230.plain, ...), custom_call_target="tpu_custom_call", output_to_operand_aliasing={{0}: (1, {})} | custom-call | flops 4000000 | bytes 4000000 | tf_op jit(solution)/shard_map/while/body/eval_jaxpr/pallas_call | solution.py:69
  44.1 6.2 %all-to-all-start = ((f32[32,40,128]{2,1,0:T(8,128)}), f32[32,40,128]{2,1,0:T(8,128)S(1)}, u32[]{:S(2)}, u32[]{:S(2)}) async-start(f32[32,40,128]{2,1,0:T(8,128)} %get-tuple-element.249), calls=%async_computation | async-start | bytes 1310720 | tf_op jit(solution)/shard_map/while/body/eval_jaxpr/all_to_all | solution.py:502
  56.2 2.6 %eval_jaxpr.6 = (f32[34,64,128]{2,1,0:T(8,128)S(1)}, f32[64,128]{1,0:T(8,128)S(1)}) custom-call(f32[34,64,128]{2,1,0:T(8,128)S(1)} %get-tuple-element.247.solid.old, f32[32,64,128]{2,1,0:T(8,128)S(1)} %copy-done.2, f32[64,128]{1,0:T(8,128)S(1)} %collective-permute-done.west, ...), custom_call_target="tpu_custom_call", output_to_operand_aliasing={{0}: (0, {})} | custom-call | flops 4000000 | bytes 6000000 | tf_op jit(solution)/shard_map/while/body/eval_jaxpr/pallas_call | solution.py:69
  58.8 4.4 %all-to-all-done.got = f32[32,40,128]{2,1,0:T(8,128)S(1)} async-done(((f32[32,40,128]{2,1,0:T(8,128)}), f32[32,40,128]{2,1,0:T(8,128)S(1)}, u32[]{:S(2)}, u32[]{:S(2)}) %all-to-all-start) | async-done | bytes 655392 | tf_op jit(solution)/shard_map/while/body/eval_jaxpr/all_to_all | solution.py:502
  63.3 3.0 %eval_jaxpr.7 = (f32[34,64,128]{2,1,0:T(8,128)S(1)}, f32[32,40,128]{2,1,0:T(8,128)}, f32[64,128]{1,0:T(8,128)S(1)}) custom-call(f32[32,40,128]{2,1,0:T(8,128)S(1)} %all-to-all-done.got, f32[34,64,128]{2,1,0:T(8,128)S(1)} %get-tuple-element.229.old, f32[64,128]{1,0:T(8,128)S(1)} %get-tuple-element.230.plain, ...), custom_call_target="tpu_custom_call", output_to_operand_aliasing={{0}: (1, {})} | custom-call | flops 4000000 | bytes 4000000 | tf_op jit(solution)/shard_map/while/body/eval_jaxpr/pallas_call | solution.py:69
  66.3 4.2 %all-to-all-start = ((f32[32,40,128]{2,1,0:T(8,128)}), f32[32,40,128]{2,1,0:T(8,128)S(1)}, u32[]{:S(2)}, u32[]{:S(2)}) async-start(f32[32,40,128]{2,1,0:T(8,128)} %get-tuple-element.249), calls=%async_computation | async-start | bytes 1310720 | tf_op jit(solution)/shard_map/while/body/eval_jaxpr/all_to_all | solution.py:502
  76.3 2.6 %eval_jaxpr.6 = (f32[34,64,128]{2,1,0:T(8,128)S(1)}, f32[64,128]{1,0:T(8,128)S(1)}) custom-call(f32[34,64,128]{2,1,0:T(8,128)S(1)} %get-tuple-element.247.solid.old, f32[32,64,128]{2,1,0:T(8,128)S(1)} %copy-done.2, f32[64,128]{1,0:T(8,128)S(1)} %collective-permute-done.west, ...), custom_call_target="tpu_custom_call", output_to_operand_aliasing={{0}: (0, {})} | custom-call | flops 4000000 | bytes 6000000 | tf_op jit(solution)/shard_map/while/body/eval_jaxpr/pallas_call | solution.py:69
  79.0 4.4 %all-to-all-done.got = f32[32,40,128]{2,1,0:T(8,128)S(1)} async-done(((f32[32,40,128]{2,1,0:T(8,128)}), f32[32,40,128]{2,1,0:T(8,128)S(1)}, u32[]{:S(2)}, u32[]{:S(2)}) %all-to-all-start) | async-done | bytes 655392 | tf_op jit(solution)/shard_map/while/body/eval_jaxpr/all_to_all | solution.py:502
  83.4 3.0 %eval_jaxpr.7 = (f32[34,64,128]{2,1,0:T(8,128)S(1)}, f32[32,40,128]{2,1,0:T(8,128)}, f32[64,128]{1,0:T(8,128)S(1)}) custom-call(f32[32,40,128]{2,1,0:T(8,128)S(1)} %all-to-all-done.got, f32[34,64,128]{2,1,0:T(8,128)S(1)} %get-tuple-element.229.old, f32[64,128]{1,0:T(8,128)S(1)} %get-tuple-element.230.plain, ...), custom_call_target="tpu_custom_call", output_to_operand_aliasing={{0}: (1, {})} | custom-call | flops 4000000 | bytes 4000000 | tf_op jit(solution)/shard_map/while/body/eval_jaxpr/pallas_call | solution.py:69
  86.4 4.2 %all-to-all-start = ((f32[32,40,128]{2,1,0:T(8,128)}), f32[32,40,128]{2,1,0:T(8,128)S(1)}, u32[]{:S(2)}, u32[]{:S(2)}) async-start(f32[32,40,128]{2,1,0:T(8,128)} %get-tuple-element.249), calls=%async_computation | async-start | bytes 1310720 | tf_op jit(solution)/shard_map/while/body/eval_jaxpr/all_to_all | solution.py:502
  96.5 2.6 %eval_jaxpr.6 = (f32[34,64,128]{2,1,0:T(8,128)S(1)}, f32[64,128]{1,0:T(8,128)S(1)}) custom-call(f32[34,64,128]{2,1,0:T(8,128)S(1)} %get-tuple-element.247.solid.old, f32[32,64,128]{2,1,0:T(8,128)S(1)} %copy-done.2, f32[64,128]{1,0:T(8,128)S(1)} %collective-permute-done.west, ...), custom_call_target="tpu_custom_call", output_to_operand_aliasing={{0}: (0, {})} | custom-call | flops 4000000 | bytes 6000000 | tf_op jit(solution)/shard_map/while/body/eval_jaxpr/pallas_call | solution.py:69
  99.1 4.4 %all-to-all-done.got = f32[32,40,128]{2,1,0:T(8,128)S(1)} async-done(((f32[32,40,128]{2,1,0:T(8,128)}), f32[32,40,128]{2,1,0:T(8,128)S(1)}, u32[]{:S(2)}, u32[]{:S(2)}) %all-to-all-start) | async-done | bytes 655392 | tf_op jit(solution)/shard_map/while/body/eval_jaxpr/all_to_all | solution.py:502
  103.6 3.0 %eval_jaxpr.7 = (f32[34,64,128]{2,1,0:T(8,128)S(1)}, f32[32,40,128]{2,1,0:T(8,128)}, f32[64,128]{1,0:T(8,128)S(1)}) custom-call(f32[32,40,128]{2,1,0:T(8,128)S(1)} %all-to-all-done.got, f32[34,64,128]{2,1,0:T(8,128)S(1)} %get-tuple-element.229.old, f32[64,128]{1,0:T(8,128)S(1)} %get-tuple-element.230.plain, ...), custom_call_target="tpu_custom_call", output_to_operand_aliasing={{0}: (1, {})} | custom-call | flops 4000000 | bytes 4000000 | tf_op jit(solution)/shard_map/while/body/eval_jaxpr/pallas_call | solution.py:69
  106.6 4.2 %all-to-all-start = ((f32[32,40,128]{2,1,0:T(8,128)}), f32[32,40,128]{2,1,0:T(8,128)S(1)}, u32[]{:S(2)}, u32[]{:S(2)}) async-start(f32[32,40,128]{2,1,0:T(8,128)} %get-tuple-element.249), calls=%async_computation | async-start | bytes 1310720 | tf_op jit(solution)/shard_map/while/body/eval_jaxpr/all_to_all | solution.py:502
  116.6 2.6 %eval_jaxpr.6 = (f32[34,64,128]{2,1,0:T(8,128)S(1)}, f32[64,128]{1,0:T(8,128)S(1)}) custom-call(f32[34,64,128]{2,1,0:T(8,128)S(1)} %get-tuple-element.247.solid.old, f32[32,64,128]{2,1,0:T(8,128)S(1)} %copy-done.2, f32[64,128]{1,0:T(8,128)S(1)} %collective-permute-done.west, ...), custom_call_target="tpu_custom_call", output_to_operand_aliasing={{0}: (0, {})} | custom-call | flops 4000000 | bytes 6000000 | tf_op jit(solution)/shard_map/while/body/eval_jaxpr/pallas_call | solution.py:69
  119.3 4.4 %all-to-all-done.got = f32[32,40,128]{2,1,0:T(8,128)S(1)} async-done(((f32[32,40,128]{2,1,0:T(8,128)}), f32[32,40,128]{2,1,0:T(8,128)S(1)}, u32[]{:S(2)}, u32[]{:S(2)}) %all-to-all-start) | async-done | bytes 655392 | tf_op jit(solution)/shard_map/while/body/eval_jaxpr/all_to_all | solution.py:502
  123.7 3.0 %eval_jaxpr.7 = (f32[34,64,128]{2,1,0:T(8,128)S(1)}, f32[32,40,128]{2,1,0:T(8,128)}, f32[64,128]{1,0:T(8,128)S(1)}) custom-call(f32[32,40,128]{2,1,0:T(8,128)S(1)} %all-to-all-done.got, f32[34,64,128]{2,1,0:T(8,128)S(1)} %get-tuple-element.229.old, f32[64,128]{1,0:T(8,128)S(1)} %get-tuple-element.230.plain, ...), custom_call_target="tpu_custom_call", output_to_operand_aliasing={{0}: (1, {})} | custom-call | flops 4000000 | bytes 4000000 | tf_op jit(solution)/shard_map/while/body/eval_jaxpr/pallas_call | solution.py:69
  126.7 4.2 %all-to-all-start = ((f32[32,40,128]{2,1,0:T(8,128)}), f32[32,40,128]{2,1,0:T(8,128)S(1)}, u32[]{:S(2)}, u32[]{:S(2)}) async-start(f32[32,40,128]{2,1,0:T(8,128)} %get-tuple-element.249), calls=%async_computation | async-start | bytes 1310720 | tf_op jit(solution)/shard_map/while/body/eval_jaxpr/all_to_all | solution.py:502
  136.8 2.6 %eval_jaxpr.6 = (f32[34,64,128]{2,1,0:T(8,128)S(1)}, f32[64,128]{1,0:T(8,128)S(1)}) custom-call(f32[34,64,128]{2,1,0:T(8,128)S(1)} %get-tuple-element.247.solid.old, f32[32,64,128]{2,1,0:T(8,128)S(1)} %copy-done.2, f32[64,128]{1,0:T(8,128)S(1)} %collective-permute-done.west, ...), custom_call_target="tpu_custom_call", output_to_operand_aliasing={{0}: (0, {})} | custom-call | flops 4000000 | bytes 6000000 | tf_op jit(solution)/shard_map/while/body/eval_jaxpr/pallas_call | solution.py:69
  139.4 4.4 %all-to-all-done.got = f32[32,40,128]{2,1,0:T(8,128)S(1)} async-done(((f32[32,40,128]{2,1,0:T(8,128)}), f32[32,40,128]{2,1,0:T(8,128)S(1)}, u32[]{:S(2)}, u32[]{:S(2)}) %all-to-all-start) | async-done | bytes 655392 | tf_op jit(solution)/shard_map/while/body/eval_jaxpr/all_to_all | solution.py:502
  143.9 3.0 %eval_jaxpr.7 = (f32[34,64,128]{2,1,0:T(8,128)S(1)}, f32[32,40,128]{2,1,0:T(8,128)}, f32[64,128]{1,0:T(8,128)S(1)}) custom-call(f32[32,40,128]{2,1,0:T(8,128)S(1)} %all-to-all-done.got, f32[34,64,128]{2,1,0:T(8,128)S(1)} %get-tuple-element.229.old, f32[64,128]{1,0:T(8,128)S(1)} %get-tuple-element.230.plain, ...), custom_call_target="tpu_custom_call", output_to_operand_aliasing={{0}: (1, {})} | custom-call | flops 4000000 | bytes 4000000 | tf_op jit(solution)/shard_map/while/body/eval_jaxpr/pallas_call | solution.py:69
  146.9 4.2 %all-to-all-start = ((f32[32,40,128]{2,1,0:T(8,128)}), f32[32,40,128]{2,1,0:T(8,128)S(1)}, u32[]{:S(2)}, u32[]{:S(2)}) async-start(f32[32,40,128]{2,1,0:T(8,128)} %get-tuple-element.249), calls=%async_computation | async-start | bytes 1310720 | tf_op jit(solution)/shard_map/while/body/eval_jaxpr/all_to_all | solution.py:502
  156.9 2.6 %eval_jaxpr.6 = (f32[34,64,128]{2,1,0:T(8,128)S(1)}, f32[64,128]{1,0:T(8,128)S(1)}) custom-call(f32[34,64,128]{2,1,0:T(8,128)S(1)} %get-tuple-element.247.solid.old, f32[32,64,128]{2,1,0:T(8,128)S(1)} %copy-done.2, f32[64,128]{1,0:T(8,128)S(1)} %collective-permute-done.west, ...), custom_call_target="tpu_custom_call", output_to_operand_aliasing={{0}: (0, {})} | custom-call | flops 4000000 | bytes 6000000 | tf_op jit(solution)/shard_map/while/body/eval_jaxpr/pallas_call | solution.py:69
  159.6 4.4 %all-to-all-done.got = f32[32,40,128]{2,1,0:T(8,128)S(1)} async-done(((f32[32,40,128]{2,1,0:T(8,128)}), f32[32,40,128]{2,1,0:T(8,128)S(1)}, u32[]{:S(2)}, u32[]{:S(2)}) %all-to-all-start) | async-done | bytes 655392 | tf_op jit(solution)/shard_map/while/body/eval_jaxpr/all_to_all | solution.py:502
  164.0 3.0 %eval_jaxpr.7 = (f32[34,64,128]{2,1,0:T(8,128)S(1)}, f32[32,40,128]{2,1,0:T(8,128)}, f32[64,128]{1,0:T(8,128)S(1)}) custom-call(f32[32,40,128]{2,1,0:T(8,128)S(1)} %all-to-all-done.got, f32[34,64,128]{2,1,0:T(8,128)S(1)} %get-tuple-element.229.old, f32[64,128]{1,0:T(8,128)S(1)} %get-tuple-element.230.plain, ...), custom_call_target="tpu_custom_call", output_to_operand_aliasing={{0}: (1, {})} | custom-call | flops 4000000 | bytes 4000000 | tf_op jit(solution)/shard_map/while/body/eval_jaxpr/pallas_call | solution.py:69
  167.0 4.2 %all-to-all-start = ((f32[32,40,128]{2,1,0:T(8,128)}), f32[32,40,128]{2,1,0:T(8,128)S(1)}, u32[]{:S(2)}, u32[]{:S(2)}) async-start(f32[32,40,128]{2,1,0:T(8,128)} %get-tuple-element.249), calls=%async_computation | async-start | bytes 1310720 | tf_op jit(solution)/shard_map/while/body/eval_jaxpr/all_to_all | solution.py:502
  177.1 2.6 %eval_jaxpr.6 = (f32[34,64,128]{2,1,0:T(8,128)S(1)}, f32[64,128]{1,0:T(8,128)S(1)}) custom-call(f32[34,64,128]{2,1,0:T(8,128)S(1)} %get-tuple-element.247.solid.old, f32[32,64,128]{2,1,0:T(8,128)S(1)} %copy-done.2, f32[64,128]{1,0:T(8,128)S(1)} %collective-permute-done.west, ...), custom_call_target="tpu_custom_call", output_to_operand_aliasing={{0}: (0, {})} | custom-call | flops 4000000 | bytes 6000000 | tf_op jit(solution)/shard_map/while/body/eval_jaxpr/pallas_call | solution.py:69
  179.7 4.4 %all-to-all-done.got = f32[32,40,128]{2,1,0:T(8,128)S(1)} async-done(((f32[32,40,128]{2,1,0:T(8,128)}), f32[32,40,128]{2,1,0:T(8,128)S(1)}, u32[]{:S(2)}, u32[]{:S(2)}) %all-to-all-start) | async-done | bytes 655392 | tf_op jit(solution)/shard_map/while/body/eval_jaxpr/all_to_all | solution.py:502
  184.2 3.0 %eval_jaxpr.7 = (f32[34,64,128]{2,1,0:T(8,128)S(1)}, f32[32,40,128]{2,1,0:T(8,128)}, f32[64,128]{1,0:T(8,128)S(1)}) custom-call(f32[32,40,128]{2,1,0:T(8,128)S(1)} %all-to-all-done.got, f32[34,64,128]{2,1,0:T(8,128)S(1)} %get-tuple-element.229.old, f32[64,128]{1,0:T(8,128)S(1)} %get-tuple-element.230.plain, ...), custom_call_target="tpu_custom_call", output_to_operand_aliasing={{0}: (1, {})} | custom-call | flops 4000000 | bytes 4000000 | tf_op jit(solution)/shard_map/while/body/eval_jaxpr/pallas_call | solution.py:69
  187.2 4.2 %all-to-all-start.2 = ((f32[32,40,128]{2,1,0:T(8,128)}), f32[32,40,128]{2,1,0:T(8,128)S(1)}, u32[]{:S(2)}, u32[]{:S(2)}) async-start(f32[32,40,128]{2,1,0:T(8,128)} %get-tuple-element.107), calls=%async_computation.2 | async-start | bytes 1310720 | tf_op jit(solution)/shard_map/all_to_all | solution.py:502
  195.0 2.2 collective-permute-done.3.east
  197.2 2.6 %shard_map.91 = (f32[34,64,128]{2,1,0:T(8,128)S(1)}, f32[64,128]{1,0:T(8,128)S(1)}) custom-call(f32[34,64,128]{2,1,0:T(8,128)S(1)} %get-tuple-element.108.solid.old, f32[32,64,128]{2,1,0:T(8,128)S(1)} %copy-done.3, f32[64,128]{1,0:T(8,128)S(1)} %collective-permute-done.2.west, ...), custom_call_target="tpu_custom_call", output_to_operand_aliasing={{0}: (0, {})} | custom-call | flops 4000000 | bytes 6000000 | tf_op jit(solution)/shard_map/pallas_call | solution.py:69
  199.9 4.4 %all-to-all-done.2.got = f32[32,40,128]{2,1,0:T(8,128)S(1)} async-done(((f32[32,40,128]{2,1,0:T(8,128)}), f32[32,40,128]{2,1,0:T(8,128)S(1)}, u32[]{:S(2)}, u32[]{:S(2)}) %all-to-all-start.2) | async-done | bytes 655392 | tf_op jit(solution)/shard_map/all_to_all | solution.py:502
  204.3 3.1 %shard_map.92 = (f32[34,64,128]{2,1,0:T(8,128)S(1)}, f32[32,56,128]{2,1,0:T(8,128)}, f32[64,128]{1,0:T(8,128)S(1)}) custom-call(f32[32,40,128]{2,1,0:T(8,128)S(1)} %all-to-all-done.2.got, f32[34,64,128]{2,1,0:T(8,128)S(1)} %get-tuple-element.114.old, f32[64,128]{1,0:T(8,128)S(1)} %get-tuple-element.115.plain, ...), custom_call_target="tpu_custom_call", output_to_operand_aliasing={{0}: (1, {})} | custom-call | flops 4000000 | bytes 4000000 | tf_op jit(solution)/shard_map/pallas_call | solution.py:69
  207.5 4.2 %all-to-all-start.3 = ((f32[32,56,128]{2,1,0:T(8,128)}), f32[32,56,128]{2,1,0:T(8,128)S(1)}, u32[]{:S(2)}, u32[]{:S(2)}) async-start(f32[32,56,128]{2,1,0:T(8,128)} %get-tuple-element.116), calls=%async_computation.3 | async-start | bytes 1835008 | tf_op jit(solution)/shard_map/all_to_all | solution.py:502
  217.5 3.3 %shard_map.95 = (f32[34,64,128]{2,1,0:T(8,128)S(1)}, f32[64,128]{1,0:T(8,128)}) custom-call(f32[34,64,128]{2,1,0:T(8,128)S(1)} %get-tuple-element.117.solid.old, f32[32,64,128]{2,1,0:T(8,128)S(1)} %copy-done.4, f32[64,128]{1,0:T(8,128)S(1)} %collective-permute-done.4.west, ...), custom_call_target="tpu_custom_call", output_to_operand_aliasing={{0}: (0, {})} | custom-call | flops 4000000 | bytes 6000000 | tf_op jit(solution)/shard_map/pallas_call | solution.py:69
  220.8 6.7 %all-to-all-done.3.got = f32[32,56,128]{2,1,0:T(8,128)S(1)} async-done(((f32[32,56,128]{2,1,0:T(8,128)}), f32[32,56,128]{2,1,0:T(8,128)S(1)}, u32[]{:S(2)}, u32[]{:S(2)}) %all-to-all-start.3) | async-done | bytes 917536 | tf_op jit(solution)/shard_map/all_to_all | solution.py:502
  227.5 3.3 %shard_map.96 = (f32[34,64,128]{2,1,0:T(8,128)S(1)}, f32[32,64,128]{2,1,0:T(8,128)}, f32[16,2048]{1,0:T(8,128)}) custom-call(f32[32,56,128]{2,1,0:T(8,128)S(1)} %all-to-all-done.3.got, f32[34,64,128]{2,1,0:T(8,128)S(1)} %get-tuple-element.123.old, bf16[256,512]{1,0:T(8,128)(2,1)S(1)} %copy-done.1, ...), custom_call_target="tpu_custom_call", output_to_operand_aliasing={{0}: (1, {})} | custom-call | tf_op jit(solution)/shard_map/pallas_call | solution.py:69
  (89 shorter events, 53.8 us)
Async XLA Ops:
  0.6 12.4 %copy-start.6 = (f32[16]{0:T(128)S(1)}, f32[16]{0:T(128)}, u32[]{:S(2)}) copy-start(f32[16]{0:T(128)} %param.13) | copy-start | bytes 196
  0.6 12.4 %copy-start.7 = (f32[16]{0:T(128)S(1)}, f32[16]{0:T(128)}, u32[]{:S(2)}) copy-start(f32[16]{0:T(128)} %param.12) | copy-start | bytes 196
  3.2 17.9 %all-to-all-start.1 = ((f32[32,24,128]{2,1,0:T(8,128)}), f32[32,24,128]{2,1,0:T(8,128)S(1)}, u32[]{:S(2)}, u32[]{:S(2)}) async-start(f32[32,24,128]{2,1,0:T(8,128)} %get-tuple-element.99), calls=%async_computation.1 | async-start | bytes 786432 | tf_op jit(solution)/shard_map/all_to_all | solution.py:502
  24.1 17.0 %all-to-all-start = ((f32[32,40,128]{2,1,0:T(8,128)}), f32[32,40,128]{2,1,0:T(8,128)S(1)}, u32[]{:S(2)}, u32[]{:S(2)}) async-start(f32[32,40,128]{2,1,0:T(8,128)} %get-tuple-element.249), calls=%async_computation | async-start | bytes 1310720 | tf_op jit(solution)/shard_map/while/body/eval_jaxpr/all_to_all | solution.py:502
  28.1 4.0 %collective-permute-start = (f32[64,128]{1,0:T(8,128)S(1)}, f32[64,128]{1,0:T(8,128)S(1)}, u32[]{:S(2)}, u32[]{:S(2)}) collective-permute-start(f32[64,128]{1,0:T(8,128)S(1)} %get-tuple-element.227), channel_id=1, source_target_pairs={{0,1},{1,2},{2,3},{3,4},{4,5},{5,6},{6,7},{7,0},{8,9},{9,10},{10,1... | collective-permute-start | bytes 98312 | tf_op jit(solution)/shard_map/while/body/eval_jaxpr/ppermute | solution.py:560
  31.7 4.3 %collective-permute-start.1 = (f32[64,128]{1,0:T(8,128)S(1)}, f32[64,128]{1,0:T(8,128)S(1)}, u32[]{:S(2)}, u32[]{:S(2)}) collective-permute-start(f32[64,128]{1,0:T(8,128)S(1)} %get-tuple-element.227), channel_id=1, source_target_pairs={{0,7},{1,0},{2,1},{3,2},{4,3},{5,4},{6,5},{7,6},{8,15},{9,8},{10,9... | collective-permute-start | bytes 98312 | tf_op jit(solution)/shard_map/while/body/eval_jaxpr/ppermute | solution.py:563
  31.8 4.3 %copy-start.2 = (f32[32,64,128]{2,1,0:T(8,128)S(1)}, f32[32,64,128]{2,1,0:T(8,128)}, u32[]{:S(2)}) copy-start(f32[32,64,128]{2,1,0:T(8,128)} %get-tuple-element.265.heat) | copy-start | bytes 3145732 | tf_op jit(solution)/shard_map/while
  44.1 19.1 %all-to-all-start = ((f32[32,40,128]{2,1,0:T(8,128)}), f32[32,40,128]{2,1,0:T(8,128)S(1)}, u32[]{:S(2)}, u32[]{:S(2)}) async-start(f32[32,40,128]{2,1,0:T(8,128)} %get-tuple-element.249), calls=%async_computation | async-start | bytes 1310720 | tf_op jit(solution)/shard_map/while/body/eval_jaxpr/all_to_all | solution.py:502
  50.4 2.9 %collective-permute-start = (f32[64,128]{1,0:T(8,128)S(1)}, f32[64,128]{1,0:T(8,128)S(1)}, u32[]{:S(2)}, u32[]{:S(2)}) collective-permute-start(f32[64,128]{1,0:T(8,128)S(1)} %get-tuple-element.227), channel_id=1, source_target_pairs={{0,1},{1,2},{2,3},{3,4},{4,5},{5,6},{6,7},{7,0},{8,9},{9,10},{10,1... | collective-permute-start | bytes 98312 | tf_op jit(solution)/shard_map/while/body/eval_jaxpr/ppermute | solution.py:560
  51.8 4.3 %collective-permute-start.1 = (f32[64,128]{1,0:T(8,128)S(1)}, f32[64,128]{1,0:T(8,128)S(1)}, u32[]{:S(2)}, u32[]{:S(2)}) collective-permute-start(f32[64,128]{1,0:T(8,128)S(1)} %get-tuple-element.227), channel_id=1, source_target_pairs={{0,7},{1,0},{2,1},{3,2},{4,3},{5,4},{6,5},{7,6},{8,15},{9,8},{10,9... | collective-permute-start | bytes 98312 | tf_op jit(solution)/shard_map/while/body/eval_jaxpr/ppermute | solution.py:563
  52.6 3.5 %copy-start.2 = (f32[32,64,128]{2,1,0:T(8,128)S(1)}, f32[32,64,128]{2,1,0:T(8,128)}, u32[]{:S(2)}) copy-start(f32[32,64,128]{2,1,0:T(8,128)} %get-tuple-element.265.heat) | copy-start | bytes 3145732 | tf_op jit(solution)/shard_map/while
  66.3 17.1 %all-to-all-start = ((f32[32,40,128]{2,1,0:T(8,128)}), f32[32,40,128]{2,1,0:T(8,128)S(1)}, u32[]{:S(2)}, u32[]{:S(2)}) async-start(f32[32,40,128]{2,1,0:T(8,128)} %get-tuple-element.249), calls=%async_computation | async-start | bytes 1310720 | tf_op jit(solution)/shard_map/while/body/eval_jaxpr/all_to_all | solution.py:502
  70.5 2.9 %collective-permute-start = (f32[64,128]{1,0:T(8,128)S(1)}, f32[64,128]{1,0:T(8,128)S(1)}, u32[]{:S(2)}, u32[]{:S(2)}) collective-permute-start(f32[64,128]{1,0:T(8,128)S(1)} %get-tuple-element.227), channel_id=1, source_target_pairs={{0,1},{1,2},{2,3},{3,4},{4,5},{5,6},{6,7},{7,0},{8,9},{9,10},{10,1... | collective-permute-start | bytes 98312 | tf_op jit(solution)/shard_map/while/body/eval_jaxpr/ppermute | solution.py:560
  72.0 4.3 %collective-permute-start.1 = (f32[64,128]{1,0:T(8,128)S(1)}, f32[64,128]{1,0:T(8,128)S(1)}, u32[]{:S(2)}, u32[]{:S(2)}) collective-permute-start(f32[64,128]{1,0:T(8,128)S(1)} %get-tuple-element.227), channel_id=1, source_target_pairs={{0,7},{1,0},{2,1},{3,2},{4,3},{5,4},{6,5},{7,6},{8,15},{9,8},{10,9... | collective-permute-start | bytes 98312 | tf_op jit(solution)/shard_map/while/body/eval_jaxpr/ppermute | solution.py:563
  72.8 3.5 %copy-start.2 = (f32[32,64,128]{2,1,0:T(8,128)S(1)}, f32[32,64,128]{2,1,0:T(8,128)}, u32[]{:S(2)}) copy-start(f32[32,64,128]{2,1,0:T(8,128)} %get-tuple-element.265.heat) | copy-start | bytes 3145732 | tf_op jit(solution)/shard_map/while
  86.4 17.1 %all-to-all-start = ((f32[32,40,128]{2,1,0:T(8,128)}), f32[32,40,128]{2,1,0:T(8,128)S(1)}, u32[]{:S(2)}, u32[]{:S(2)}) async-start(f32[32,40,128]{2,1,0:T(8,128)} %get-tuple-element.249), calls=%async_computation | async-start | bytes 1310720 | tf_op jit(solution)/shard_map/while/body/eval_jaxpr/all_to_all | solution.py:502
  90.7 2.9 %collective-permute-start = (f32[64,128]{1,0:T(8,128)S(1)}, f32[64,128]{1,0:T(8,128)S(1)}, u32[]{:S(2)}, u32[]{:S(2)}) collective-permute-start(f32[64,128]{1,0:T(8,128)S(1)} %get-tuple-element.227), channel_id=1, source_target_pairs={{0,1},{1,2},{2,3},{3,4},{4,5},{5,6},{6,7},{7,0},{8,9},{9,10},{10,1... | collective-permute-start | bytes 98312 | tf_op jit(solution)/shard_map/while/body/eval_jaxpr/ppermute | solution.py:560
  92.1 4.3 %collective-permute-start.1 = (f32[64,128]{1,0:T(8,128)S(1)}, f32[64,128]{1,0:T(8,128)S(1)}, u32[]{:S(2)}, u32[]{:S(2)}) collective-permute-start(f32[64,128]{1,0:T(8,128)S(1)} %get-tuple-element.227), channel_id=1, source_target_pairs={{0,7},{1,0},{2,1},{3,2},{4,3},{5,4},{6,5},{7,6},{8,15},{9,8},{10,9... | collective-permute-start | bytes 98312 | tf_op jit(solution)/shard_map/while/body/eval_jaxpr/ppermute | solution.py:563
  92.9 3.5 %copy-start.2 = (f32[32,64,128]{2,1,0:T(8,128)S(1)}, f32[32,64,128]{2,1,0:T(8,128)}, u32[]{:S(2)}) copy-start(f32[32,64,128]{2,1,0:T(8,128)} %get-tuple-element.265.heat) | copy-start | bytes 3145732 | tf_op jit(solution)/shard_map/while
  106.6 17.1 %all-to-all-start = ((f32[32,40,128]{2,1,0:T(8,128)}), f32[32,40,128]{2,1,0:T(8,128)S(1)}, u32[]{:S(2)}, u32[]{:S(2)}) async-start(f32[32,40,128]{2,1,0:T(8,128)} %get-tuple-element.249), calls=%async_computation | async-start | bytes 1310720 | tf_op jit(solution)/shard_map/while/body/eval_jaxpr/all_to_all | solution.py:502
  110.8 2.9 %collective-permute-start = (f32[64,128]{1,0:T(8,128)S(1)}, f32[64,128]{1,0:T(8,128)S(1)}, u32[]{:S(2)}, u32[]{:S(2)}) collective-permute-start(f32[64,128]{1,0:T(8,128)S(1)} %get-tuple-element.227), channel_id=1, source_target_pairs={{0,1},{1,2},{2,3},{3,4},{4,5},{5,6},{6,7},{7,0},{8,9},{9,10},{10,1... | collective-permute-start | bytes 98312 | tf_op jit(solution)/shard_map/while/body/eval_jaxpr/ppermute | solution.py:560
  112.3 4.3 %collective-permute-start.1 = (f32[64,128]{1,0:T(8,128)S(1)}, f32[64,128]{1,0:T(8,128)S(1)}, u32[]{:S(2)}, u32[]{:S(2)}) collective-permute-start(f32[64,128]{1,0:T(8,128)S(1)} %get-tuple-element.227), channel_id=1, source_target_pairs={{0,7},{1,0},{2,1},{3,2},{4,3},{5,4},{6,5},{7,6},{8,15},{9,8},{10,9... | collective-permute-start | bytes 98312 | tf_op jit(solution)/shard_map/while/body/eval_jaxpr/ppermute | solution.py:563
  113.1 3.5 %copy-start.2 = (f32[32,64,128]{2,1,0:T(8,128)S(1)}, f32[32,64,128]{2,1,0:T(8,128)}, u32[]{:S(2)}) copy-start(f32[32,64,128]{2,1,0:T(8,128)} %get-tuple-element.265.heat) | copy-start | bytes 3145732 | tf_op jit(solution)/shard_map/while
  126.7 17.1 %all-to-all-start = ((f32[32,40,128]{2,1,0:T(8,128)}), f32[32,40,128]{2,1,0:T(8,128)S(1)}, u32[]{:S(2)}, u32[]{:S(2)}) async-start(f32[32,40,128]{2,1,0:T(8,128)} %get-tuple-element.249), calls=%async_computation | async-start | bytes 1310720 | tf_op jit(solution)/shard_map/while/body/eval_jaxpr/all_to_all | solution.py:502
  130.9 2.9 %collective-permute-start = (f32[64,128]{1,0:T(8,128)S(1)}, f32[64,128]{1,0:T(8,128)S(1)}, u32[]{:S(2)}, u32[]{:S(2)}) collective-permute-start(f32[64,128]{1,0:T(8,128)S(1)} %get-tuple-element.227), channel_id=1, source_target_pairs={{0,1},{1,2},{2,3},{3,4},{4,5},{5,6},{6,7},{7,0},{8,9},{9,10},{10,1... | collective-permute-start | bytes 98312 | tf_op jit(solution)/shard_map/while/body/eval_jaxpr/ppermute | solution.py:560
  132.4 4.3 %collective-permute-start.1 = (f32[64,128]{1,0:T(8,128)S(1)}, f32[64,128]{1,0:T(8,128)S(1)}, u32[]{:S(2)}, u32[]{:S(2)}) collective-permute-start(f32[64,128]{1,0:T(8,128)S(1)} %get-tuple-element.227), channel_id=1, source_target_pairs={{0,7},{1,0},{2,1},{3,2},{4,3},{5,4},{6,5},{7,6},{8,15},{9,8},{10,9... | collective-permute-start | bytes 98312 | tf_op jit(solution)/shard_map/while/body/eval_jaxpr/ppermute | solution.py:563
  133.2 3.5 %copy-start.2 = (f32[32,64,128]{2,1,0:T(8,128)S(1)}, f32[32,64,128]{2,1,0:T(8,128)}, u32[]{:S(2)}) copy-start(f32[32,64,128]{2,1,0:T(8,128)} %get-tuple-element.265.heat) | copy-start | bytes 3145732 | tf_op jit(solution)/shard_map/while
  146.9 17.1 %all-to-all-start = ((f32[32,40,128]{2,1,0:T(8,128)}), f32[32,40,128]{2,1,0:T(8,128)S(1)}, u32[]{:S(2)}, u32[]{:S(2)}) async-start(f32[32,40,128]{2,1,0:T(8,128)} %get-tuple-element.249), calls=%async_computation | async-start | bytes 1310720 | tf_op jit(solution)/shard_map/while/body/eval_jaxpr/all_to_all | solution.py:502
  151.1 2.9 %collective-permute-start = (f32[64,128]{1,0:T(8,128)S(1)}, f32[64,128]{1,0:T(8,128)S(1)}, u32[]{:S(2)}, u32[]{:S(2)}) collective-permute-start(f32[64,128]{1,0:T(8,128)S(1)} %get-tuple-element.227), channel_id=1, source_target_pairs={{0,1},{1,2},{2,3},{3,4},{4,5},{5,6},{6,7},{7,0},{8,9},{9,10},{10,1... | collective-permute-start | bytes 98312 | tf_op jit(solution)/shard_map/while/body/eval_jaxpr/ppermute | solution.py:560
  152.6 4.3 %collective-permute-start.1 = (f32[64,128]{1,0:T(8,128)S(1)}, f32[64,128]{1,0:T(8,128)S(1)}, u32[]{:S(2)}, u32[]{:S(2)}) collective-permute-start(f32[64,128]{1,0:T(8,128)S(1)} %get-tuple-element.227), channel_id=1, source_target_pairs={{0,7},{1,0},{2,1},{3,2},{4,3},{5,4},{6,5},{7,6},{8,15},{9,8},{10,9... | collective-permute-start | bytes 98312 | tf_op jit(solution)/shard_map/while/body/eval_jaxpr/ppermute | solution.py:563
  153.4 3.5 %copy-start.2 = (f32[32,64,128]{2,1,0:T(8,128)S(1)}, f32[32,64,128]{2,1,0:T(8,128)}, u32[]{:S(2)}) copy-start(f32[32,64,128]{2,1,0:T(8,128)} %get-tuple-element.265.heat) | copy-start | bytes 3145732 | tf_op jit(solution)/shard_map/while
  167.0 17.1 %all-to-all-start = ((f32[32,40,128]{2,1,0:T(8,128)}), f32[32,40,128]{2,1,0:T(8,128)S(1)}, u32[]{:S(2)}, u32[]{:S(2)}) async-start(f32[32,40,128]{2,1,0:T(8,128)} %get-tuple-element.249), calls=%async_computation | async-start | bytes 1310720 | tf_op jit(solution)/shard_map/while/body/eval_jaxpr/all_to_all | solution.py:502
  171.2 2.9 %collective-permute-start = (f32[64,128]{1,0:T(8,128)S(1)}, f32[64,128]{1,0:T(8,128)S(1)}, u32[]{:S(2)}, u32[]{:S(2)}) collective-permute-start(f32[64,128]{1,0:T(8,128)S(1)} %get-tuple-element.227), channel_id=1, source_target_pairs={{0,1},{1,2},{2,3},{3,4},{4,5},{5,6},{6,7},{7,0},{8,9},{9,10},{10,1... | collective-permute-start | bytes 98312 | tf_op jit(solution)/shard_map/while/body/eval_jaxpr/ppermute | solution.py:560
  172.7 4.3 %collective-permute-start.1 = (f32[64,128]{1,0:T(8,128)S(1)}, f32[64,128]{1,0:T(8,128)S(1)}, u32[]{:S(2)}, u32[]{:S(2)}) collective-permute-start(f32[64,128]{1,0:T(8,128)S(1)} %get-tuple-element.227), channel_id=1, source_target_pairs={{0,7},{1,0},{2,1},{3,2},{4,3},{5,4},{6,5},{7,6},{8,15},{9,8},{10,9... | collective-permute-start | bytes 98312 | tf_op jit(solution)/shard_map/while/body/eval_jaxpr/ppermute | solution.py:563
  173.5 3.5 %copy-start.2 = (f32[32,64,128]{2,1,0:T(8,128)S(1)}, f32[32,64,128]{2,1,0:T(8,128)}, u32[]{:S(2)}) copy-start(f32[32,64,128]{2,1,0:T(8,128)} %get-tuple-element.265.heat) | copy-start | bytes 3145732 | tf_op jit(solution)/shard_map/while
  187.2 17.1 %all-to-all-start.2 = ((f32[32,40,128]{2,1,0:T(8,128)}), f32[32,40,128]{2,1,0:T(8,128)S(1)}, u32[]{:S(2)}, u32[]{:S(2)}) async-start(f32[32,40,128]{2,1,0:T(8,128)} %get-tuple-element.107), calls=%async_computation.2 | async-start | bytes 1310720 | tf_op jit(solution)/shard_map/all_to_all | solution.py:502
  191.4 2.9 %collective-permute-start.2 = (f32[64,128]{1,0:T(8,128)S(1)}, f32[64,128]{1,0:T(8,128)S(1)}, u32[]{:S(2)}, u32[]{:S(2)}) collective-permute-start(f32[64,128]{1,0:T(8,128)S(1)} %get-tuple-element.112), channel_id=1, source_target_pairs={{0,1},{1,2},{2,3},{3,4},{4,5},{5,6},{6,7},{7,0},{8,9},{9,10},{10,1... | collective-permute-start | bytes 98312 | tf_op jit(solution)/shard_map/ppermute | solution.py:560
  192.9 4.4 %copy-start.3 = (f32[32,64,128]{2,1,0:T(8,128)S(1)}, f32[32,64,128]{2,1,0:T(8,128)}, u32[]{:S(2)}) copy-start(f32[32,64,128]{2,1,0:T(8,128)} %get-tuple-element.284) | copy-start | bytes 3145732
  192.9 4.3 %collective-permute-start.3 = (f32[64,128]{1,0:T(8,128)S(1)}, f32[64,128]{1,0:T(8,128)S(1)}, u32[]{:S(2)}, u32[]{:S(2)}) collective-permute-start(f32[64,128]{1,0:T(8,128)S(1)} %get-tuple-element.112), channel_id=1, source_target_pairs={{0,7},{1,0},{2,1},{3,2},{4,3},{5,4},{6,5},{7,6},{8,15},{9,8},{10,9... | collective-permute-start | bytes 98312 | tf_op jit(solution)/shard_map/ppermute | solution.py:563
  207.5 20.0 %all-to-all-start.3 = ((f32[32,56,128]{2,1,0:T(8,128)}), f32[32,56,128]{2,1,0:T(8,128)S(1)}, u32[]{:S(2)}, u32[]{:S(2)}) async-start(f32[32,56,128]{2,1,0:T(8,128)} %get-tuple-element.116), calls=%async_computation.3 | async-start | bytes 1835008 | tf_op jit(solution)/shard_map/all_to_all | solution.py:502
  211.7 3.0 %collective-permute-start.4 = (f32[64,128]{1,0:T(8,128)S(1)}, f32[64,128]{1,0:T(8,128)S(1)}, u32[]{:S(2)}, u32[]{:S(2)}) collective-permute-start(f32[64,128]{1,0:T(8,128)S(1)} %get-tuple-element.121), channel_id=1, source_target_pairs={{0,1},{1,2},{2,3},{3,4},{4,5},{5,6},{6,7},{7,0},{8,9},{9,10},{10,1... | collective-permute-start | bytes 98312 | tf_op jit(solution)/shard_map/ppermute | solution.py:560
  213.2 4.4 %copy-start.4 = (f32[32,64,128]{2,1,0:T(8,128)S(1)}, f32[32,64,128]{2,1,0:T(8,128)}, u32[]{:S(2)}) copy-start(f32[32,64,128]{2,1,0:T(8,128)} %get-tuple-element.284) | copy-start | bytes 3145732
  213.2 4.3 %collective-permute-start.5 = (f32[64,128]{1,0:T(8,128)S(1)}, f32[64,128]{1,0:T(8,128)S(1)}, u32[]{:S(2)}, u32[]{:S(2)}) collective-permute-start(f32[64,128]{1,0:T(8,128)S(1)} %get-tuple-element.121), channel_id=1, source_target_pairs={{0,7},{1,0},{2,1},{3,2},{4,3},{5,4},{6,5},{7,6},{8,15},{9,8},{10,9... | collective-permute-start | bytes 98312 | tf_op jit(solution)/shard_map/ppermute | solution.py:563
  215.4 12.1 %copy-start = (f32[16,2048]{1,0:T(8,128)S(1)}, f32[16,2048]{1,0:T(8,128)}, u32[]{:S(2)}) copy-start(f32[16,2048]{1,0:T(8,128)} %cond_hbm.3) | copy-start | bytes 393220
  215.4 12.1 %copy-start.1 = (bf16[256,512]{1,0:T(8,128)(2,1)S(1)}, bf16[256,512]{1,0:T(8,128)(2,1)}, u32[]{:S(2)}) copy-start(bf16[256,512]{1,0:T(8,128)(2,1)} %get-tuple-element.124.place_hbm) | copy-start | bytes 786436
  215.4 12.1 %copy-start.5 = (bf16[2,512,128]{2,1,0:T(8,128)(2,1)S(1)}, bf16[2,512,128]{2,1,0:T(8,128)(2,1)}, u32[]{:S(2)}) copy-start(bf16[2,512,128]{2,1,0:T(8,128)(2,1)} %get-tuple-element.291) | copy-start | bytes 786436
